TPU v7x, 128 devices: a whole 4x4x4 slice. The times are simulated.
128 devices in a mesh: seq: 32 (over z, x_lo, y), fsdp: 4 (over x_hi, core).
Axes of the slice: x: 4 (x_hi: 2, x_lo: 2; x = x_hi * 2 + x_lo), y: 4, z: 4, core: 2. Of those that a mesh axis runs over, the one named last changes fastest.
Arguments:
- inputs: bfloat16 [4, 16384, 640], P('fsdp', 'seq'), may hold values from -6 to 6
- doc_start: int32 [4, 16384], P('fsdp', 'seq'), may hold values from 0 to 15360, as said below
- w_query: bfloat16 [640, 1024], P('fsdp'), may hold values from -0.25 to 0.25
- w_key: bfloat16 [640, 256], P('fsdp'), may hold values from -0.25 to 0.25
- w_value: bfloat16 [640, 256], P('fsdp'), may hold values from -0.25 to 0.25
- w_output: bfloat16 [1024, 640], P('fsdp'), may hold values from -0.375 to 0.375
- w_gate: bfloat16 [640, 2048], P('fsdp'), may hold values from -0.25 to 0.25
- w_up: bfloat16 [640, 2048], P('fsdp'), may hold values from -0.25 to 0.25
- w_down: bfloat16 [2048, 640], P('fsdp'), may hold values from -0.125 to 0.125
- norm_attn_in: bfloat16 [640], P('fsdp'), may hold values from 0.099609375 to 1.8984375
- norm_attn_out: bfloat16 [640], P('fsdp'), may hold values from 0.099609375 to 1.8984375
- norm_ffn_in: bfloat16 [640], P('fsdp'), may hold values from 0.099609375 to 1.8984375
- norm_ffn_out: bfloat16 [640], P('fsdp'), may hold values from 0.099609375 to 1.8984375
- norm_query: bfloat16 [256], P('fsdp'), may hold values from 0.099609375 to 1.8984375
- norm_key: bfloat16 [256], P('fsdp'), may hold values from 0.099609375 to 1.8984375
- cotangent: bfloat16 [4, 16384, 640], P('fsdp', 'seq'), may hold values from -6 to 6
Outputs:
- layer_out: bfloat16 [4, 16384, 640], P('fsdp', 'seq')
- input_grad: float32 [4, 16384, 640], P('fsdp', 'seq')
- query_grad: float32 [640, 1024], P('fsdp')
- key_grad: float32 [640, 256], P('fsdp')
- value_grad: float32 [640, 256], P('fsdp')
- output_grad: float32 [1024, 640], P('fsdp')
- gate_grad: float32 [640, 2048], P('fsdp')
- up_grad: float32 [640, 2048], P('fsdp')
- down_grad: float32 [2048, 640], P('fsdp')
- attn_in_grad: float32 [640], P('fsdp')
- attn_out_grad: float32 [640], P('fsdp')
- ffn_in_grad: float32 [640], P('fsdp')
- ffn_out_grad: float32 [640], P('fsdp')
- query_norm_grad: float32 [256], P('fsdp')
- key_norm_grad: float32 [256], P('fsdp')
Inputs may be any that keep to these rules, and one draw needn't show every extreme that they name: Each row of 16384 tokens holds exactly two documents, each of 1024 tokens or more: doc_start is 0 up to the second document's first index and that index from there on; in some row the second document is exactly 1024 tokens long.
All inputs are finite; a program needn't handle non-finite values.
Results may differ from a plain program's by a relative error of at most 0.034.
Values may be sent and summed in bfloat16 or wider, within the bound.
A program may use at most 192 MiB of HBM per device.

v0:
```python
import jax
import jax.numpy as jnp
from jax import lax
from jax.sharding import PartitionSpec as P

WINDOW = 512


epsilon = 1e-06
rope_base = 10000.0
masked_value = -1e30


def side_by_side(arrays, axis, dim, along):
    ends, at = ([], 0)
    for a in arrays[:-1]:
        at += a.shape[along]
        ends.append(at)
    both = jnp.concatenate(arrays, axis=along)
    return tuple(jnp.split(lax.all_gather(both, axis, axis=dim, tiled=True), ends, axis=along))


def from_behind(shard, axis, by):
    count = lax.axis_size(axis)
    pairs = [(i, i + by) for i in range(count) if 0 <= i + by < count]
    return lax.ppermute(shard, axis, pairs)


def side_by_side_2(arrays, axis, dim, along):
    both = jnp.concatenate(arrays, axis=along)
    out, at, gathered = (lax.psum_scatter(both, axis, scatter_dimension=dim, tiled=True), 0, [])
    for a in arrays:
        gathered.append(lax.slice_in_dim(out, at, at + a.shape[along], axis=along))
        at += a.shape[along]
    return tuple(gathered)


def rms_scale(values, gains):
    return values * lax.rsqrt(jnp.mean(values * values, -1, keepdims=True) + epsilon) * gains


def rope_tables(positions, head_width):
    half_width = head_width // 2
    frequency = rope_base ** (-(jnp.arange(half_width, dtype=jnp.float32) * (2.0 / head_width)))
    angles = positions[:, None] * frequency[None, :]
    cosine = jnp.cos(angles)
    sine_part = jnp.sin(angles)
    return (jnp.concatenate([cosine, cosine], -1), jnp.concatenate([sine_part, sine_part], -1))


def rotate(values, cosine, sine_part):
    half_width = values.shape[-1] // 2
    turned = jnp.concatenate([-values[..., half_width:], values[..., :half_width]], -1)
    return values * cosine + turned * sine_part


def forward_dot(left, right):
    return jnp.dot(left, right, preferred_element_type=jnp.float32)


def contract_rows(left, right):
    return lax.dot_general(
        left, right, (((0,), (0,)), ((), ())), preferred_element_type=jnp.float32
    )


def contract_cols(left, right):
    return lax.dot_general(
        left, right, (((1,), (1,)), ((), ())), preferred_element_type=jnp.float32
    )


def gated_product(gate_value, up_value):
    return jax.nn.gelu(gate_value, approximate=True) * up_value


def body(
    inputs,
    doc_start,
    w_query,
    w_key,
    w_value,
    w_output,
    w_gate,
    w_up,
    w_down,
    norm_attn_in,
    norm_attn_out,
    norm_ffn_in,
    norm_ffn_out,
    norm_query,
    norm_key,
    cotangent,
):
    gathered = (
        *side_by_side((w_query, w_key, w_value), "fsdp", 0, 1),
        lax.all_gather(w_output, "fsdp", axis=0, tiled=True),
        *side_by_side((w_gate, w_up), "fsdp", 0, 1),
        lax.all_gather(w_down, "fsdp", axis=0, tiled=True),
        lax.all_gather(norm_attn_in, "fsdp", axis=0, tiled=True),
        lax.all_gather(norm_attn_out, "fsdp", axis=0, tiled=True),
        lax.all_gather(norm_ffn_in, "fsdp", axis=0, tiled=True),
        lax.all_gather(norm_ffn_out, "fsdp", axis=0, tiled=True),
        lax.all_gather(norm_query, "fsdp", axis=0, tiled=True),
        lax.all_gather(norm_key, "fsdp", axis=0, tiled=True),
    )
    full_query, full_key, full_value, full_output, full_gate, full_up, full_down = gathered[:7]
    gain_attn_in, gain_attn_out, gain_ffn_in, gain_ffn_out, gain_query, gain_key = [
        member.astype(jnp.float32) for member in gathered[7:]
    ]
    length = inputs.shape[1]
    head_width = full_key.shape[1]
    head_count = full_query.shape[1] // head_width
    span_count = -(-(WINDOW - 1) // length)
    block_index = lax.axis_index("seq")
    row_index = block_index * length + jnp.arange(length, dtype=jnp.int32)
    doc_local = doc_start[0]
    positions = (row_index - doc_local).astype(jnp.float32)
    cosine, sine_part = rope_tables(positions, head_width)
    source = inputs[0].astype(jnp.float32)
    normed, pull_attn_in = jax.vjp(rms_scale, source, gain_attn_in)
    normed_low = normed.astype(jnp.bfloat16)
    query_raw = forward_dot(normed_low, full_query)
    key_raw = forward_dot(normed_low, full_key)
    value_raw = forward_dot(normed_low, full_value)

    def shape_query(raw_rows, gains):
        return rotate(
            rms_scale(raw_rows.reshape(length, head_count, head_width), gains),
            cosine[:, None, :],
            sine_part[:, None, :],
        )

    def shape_key(raw_rows, gains):
        return rotate(rms_scale(raw_rows, gains), cosine, sine_part)

    query_rows, pull_query = jax.vjp(shape_query, query_raw, gain_query)
    key_rows, pull_key = jax.vjp(shape_key, key_raw, gain_key)
    query_low = query_rows.astype(jnp.bfloat16)
    key_low = key_rows.astype(jnp.bfloat16)
    value_low = value_raw.astype(jnp.bfloat16)
    distance = 1
    key_from, value_from = from_behind((key_low, value_low), "seq", distance)
    earlier_keys = [key_from]
    earlier_values = [value_from]
    all_keys = jnp.concatenate(earlier_keys + [key_low], 0)
    all_values = jnp.concatenate(earlier_values + [value_low], 0)
    key_index = (block_index - span_count) * length + jnp.arange(
        (span_count + 1) * length, dtype=jnp.int32
    )
    visible = (
        (key_index[None, :] >= doc_local[:, None])
        & (key_index[None, :] <= row_index[:, None])
        & (row_index[:, None] - key_index[None, :] < WINDOW)
    )
    score_scale = head_width ** (-0.5)

    def score_rows():
        raw_scores = (
            jnp.einsum("thd,kd->htk", query_low, all_keys, preferred_element_type=jnp.float32)
            * score_scale
        )
        return jnp.where(visible[None], raw_scores, masked_value)

    scores = score_rows()
    row_max = jnp.max(scores, -1, keepdims=True)
    shifted = jnp.exp(scores - row_max)
    row_total = jnp.sum(shifted, -1, keepdims=True)
    soft_weights = shifted / row_total
    log_total = row_max + jnp.log(row_total)
    weights_low = soft_weights.astype(jnp.bfloat16)
    attended = jnp.einsum(
        "htk,kd->thd", weights_low, all_values, preferred_element_type=jnp.float32
    )
    attended = attended.reshape(length, head_count * head_width).astype(jnp.bfloat16)
    projected = forward_dot(attended, full_output)
    branch_one, pull_attn_out = jax.vjp(rms_scale, projected, gain_attn_out)
    hidden_one = source + branch_one
    normed_two, pull_ffn_in = jax.vjp(rms_scale, hidden_one, gain_ffn_in)
    normed_two_low = normed_two.astype(jnp.bfloat16)
    gate_value = forward_dot(normed_two_low, full_gate)
    up_value = forward_dot(normed_two_low, full_up)
    product, pull_product = jax.vjp(gated_product, gate_value, up_value)
    product_low = product.astype(jnp.bfloat16)
    down_value = forward_dot(product_low, full_down)
    branch_two, pull_ffn_out = jax.vjp(rms_scale, down_value, gain_ffn_out)
    layer_out = (hidden_one + branch_two).astype(jnp.bfloat16)[None]
    again = (
        *side_by_side((w_query, w_key, w_value), "fsdp", 0, 1),
        lax.all_gather(w_output, "fsdp", axis=0, tiled=True),
        *side_by_side((w_gate, w_up), "fsdp", 0, 1),
        lax.all_gather(w_down, "fsdp", axis=0, tiled=True),
    )
    back_query, back_key, back_value, back_output, back_gate, back_up, back_down = again
    upstream = cotangent[0].astype(jnp.float32)
    d_down, grad_ffn_out = pull_ffn_out(upstream)
    d_down_low = d_down.astype(jnp.bfloat16)
    grad_down = contract_rows(product_low, d_down_low)
    d_product = contract_cols(d_down_low, back_down)
    d_gate, d_up = pull_product(d_product)
    d_gate_low = d_gate.astype(jnp.bfloat16)
    d_up_low = d_up.astype(jnp.bfloat16)
    grad_gate = contract_rows(normed_two_low, d_gate_low)
    grad_up = contract_rows(normed_two_low, d_up_low)
    d_normed_two = contract_cols(d_gate_low, back_gate) + contract_cols(d_up_low, back_up)
    d_hidden_part, grad_ffn_in = pull_ffn_in(d_normed_two)
    d_hidden = upstream + d_hidden_part
    d_projected, grad_attn_out = pull_attn_out(d_hidden)
    d_projected_low = d_projected.astype(jnp.bfloat16)
    grad_output = contract_rows(attended, d_projected_low)
    d_attended = (
        contract_cols(d_projected_low, back_output)
        .astype(jnp.bfloat16)
        .reshape(length, head_count, head_width)
    )
    soft_again = jnp.exp(score_rows() - log_total)
    d_soft = jnp.einsum("thd,kd->htk", d_attended, all_values, preferred_element_type=jnp.float32)
    inner_sum = jnp.sum(soft_again * d_soft, -1, keepdims=True)
    d_scores = (soft_again * (d_soft - inner_sum)).astype(jnp.bfloat16)
    d_queries = (
        jnp.einsum("htk,kd->thd", d_scores, all_keys, preferred_element_type=jnp.float32)
        * score_scale
    )
    d_keys = (
        jnp.einsum("htk,thd->kd", d_scores, query_low, preferred_element_type=jnp.float32)
        * score_scale
    )
    d_values = jnp.einsum(
        "htk,thd->kd",
        soft_again.astype(jnp.bfloat16),
        d_attended,
        preferred_element_type=jnp.float32,
    )
    d_key_own = d_keys[span_count * length :]
    d_value_own = d_values[span_count * length :]
    distance = 1
    first_row = (span_count - distance) * length
    key_back = from_behind(
        d_keys[first_row : first_row + length].astype(jnp.bfloat16), "seq", -distance
    ).astype(jnp.float32)
    value_back = from_behind(
        d_values[first_row : first_row + length].astype(jnp.bfloat16), "seq", -distance
    ).astype(jnp.float32)
    d_key_own = d_key_own + key_back
    d_value_own = d_value_own + value_back
    d_key_raw, grad_key_norm = pull_key(d_key_own)
    d_query_raw, grad_query_norm = pull_query(d_queries)
    d_query_low = d_query_raw.astype(jnp.bfloat16)
    d_key_low = d_key_raw.astype(jnp.bfloat16)
    d_value_low = d_value_own.astype(jnp.bfloat16)
    grad_query = contract_rows(normed_low, d_query_low)
    grad_key = contract_rows(normed_low, d_key_low)
    grad_value = contract_rows(normed_low, d_value_low)
    d_normed = (
        contract_cols(d_query_low, back_query)
        + contract_cols(d_key_low, back_key)
        + contract_cols(d_value_low, back_value)
    )
    d_source, grad_attn_in = pull_attn_in(d_normed)
    input_grad = (d_hidden + d_source)[None]
    shares = (
        *tuple(
            (
                part.astype(jnp.float32)
                for part in side_by_side_2(
                    (
                        grad_query.astype(jnp.bfloat16),
                        grad_key.astype(jnp.bfloat16),
                        grad_value.astype(jnp.bfloat16),
                    ),
                    "fsdp",
                    0,
                    1,
                )
            )
        ),
        lax.psum_scatter(
            grad_output.astype(jnp.bfloat16), "fsdp", scatter_dimension=0, tiled=True
        ).astype(jnp.float32),
        *tuple(
            (
                part.astype(jnp.float32)
                for part in side_by_side_2(
                    (grad_gate.astype(jnp.bfloat16), grad_up.astype(jnp.bfloat16)), "fsdp", 0, 1
                )
            )
        ),
        lax.psum_scatter(
            grad_down.astype(jnp.bfloat16), "fsdp", scatter_dimension=0, tiled=True
        ).astype(jnp.float32),
        lax.psum_scatter(
            grad_attn_in.astype(jnp.bfloat16), "fsdp", scatter_dimension=0, tiled=True
        ).astype(jnp.float32),
        lax.psum_scatter(
            grad_attn_out.astype(jnp.bfloat16), "fsdp", scatter_dimension=0, tiled=True
        ).astype(jnp.float32),
        lax.psum_scatter(
            grad_ffn_in.astype(jnp.bfloat16), "fsdp", scatter_dimension=0, tiled=True
        ).astype(jnp.float32),
        lax.psum_scatter(
            grad_ffn_out.astype(jnp.bfloat16), "fsdp", scatter_dimension=0, tiled=True
        ).astype(jnp.float32),
        lax.psum_scatter(
            grad_query_norm.astype(jnp.bfloat16), "fsdp", scatter_dimension=0, tiled=True
        ).astype(jnp.float32),
        lax.psum_scatter(
            grad_key_norm.astype(jnp.bfloat16), "fsdp", scatter_dimension=0, tiled=True
        ).astype(jnp.float32),
    )
    finals = (
        lax.psum(shares[0].astype(jnp.bfloat16), "seq").astype(jnp.float32),
        lax.psum(shares[1].astype(jnp.bfloat16), "seq").astype(jnp.float32),
        lax.psum(shares[2].astype(jnp.bfloat16), "seq").astype(jnp.float32),
        lax.psum(shares[3].astype(jnp.bfloat16), "seq").astype(jnp.float32),
        lax.psum(shares[4].astype(jnp.bfloat16), "seq").astype(jnp.float32),
        lax.psum(shares[5].astype(jnp.bfloat16), "seq").astype(jnp.float32),
        lax.psum(shares[6].astype(jnp.bfloat16), "seq").astype(jnp.float32),
        lax.psum(shares[7].astype(jnp.bfloat16), "seq").astype(jnp.float32),
        lax.psum(shares[8].astype(jnp.bfloat16), "seq").astype(jnp.float32),
        lax.psum(shares[9].astype(jnp.bfloat16), "seq").astype(jnp.float32),
        lax.psum(shares[10].astype(jnp.bfloat16), "seq").astype(jnp.float32),
        lax.psum(shares[11].astype(jnp.bfloat16), "seq").astype(jnp.float32),
        lax.psum(shares[12].astype(jnp.bfloat16), "seq").astype(jnp.float32),
    )
    return (
        layer_out,
        input_grad,
        finals[0],
        finals[1],
        finals[2],
        finals[3],
        finals[4],
        finals[5],
        finals[6],
        finals[7],
        finals[8],
        finals[9],
        finals[10],
        finals[11],
        finals[12],
    )


def solution(mesh):
    in_specs = (
        P("fsdp", "seq", None),
        P("fsdp", "seq"),
        P("fsdp", None),
        P("fsdp", None),
        P("fsdp", None),
        P("fsdp", None),
        P("fsdp", None),
        P("fsdp", None),
        P("fsdp", None),
        P("fsdp"),
        P("fsdp"),
        P("fsdp"),
        P("fsdp"),
        P("fsdp"),
        P("fsdp"),
        P("fsdp", "seq", None),
    )
    out_specs = (
        P("fsdp", "seq", None),
        P("fsdp", "seq", None),
        P("fsdp", None),
        P("fsdp", None),
        P("fsdp", None),
        P("fsdp", None),
        P("fsdp", None),
        P("fsdp", None),
        P("fsdp", None),
        P("fsdp"),
        P("fsdp"),
        P("fsdp"),
        P("fsdp"),
        P("fsdp"),
        P("fsdp"),
    )
    return jax.shard_map(body, mesh=mesh, in_specs=in_specs, out_specs=out_specs, check_vma=False)
```

profile of v0, /device:TPU:0, one launch (start us, length us, event | category | flops | bytes accessed | tf_op | source)
XLA Modules:
  0.0 709.8 jit_solution(8686373132811952509)
XLA Ops:
  7.2 2.0 pad_maximum_fusion.5
  10.2 1.1 pad_maximum_fusion.2
  15.6 10.3 %all-reduce.19 = (bf16[640]{0:T(1024)(128)(2,1)S(1)}, bf16[256]{0:T(256)(128)(2,1)S(1)}, bf16[256]{0:T(256)(128)(2,1)S(1)}, bf16[640]{0:T(1024)(128)(2,1)S(1)}, ...) all-reduce(bf16[640]{0:T(1024)(128)(2,1)S(1)} %dynamic-update-slice, ...), channel_id=1, replica_groups=mesh['seq'=32,'fsdp'=4] {'fsdp'}, use_global_device_ids=true, to_apply=%add.4 | all-reduce | flops 3072 | bytes 12288
  27.7 1.5 fusion.29
  30.2 8.4 %all-gather.5.cloned.1.call-done = bf16[640,1536]{1,0:T(8,128)(2,1)} async-done(((bf16[160,1536]{1,0:T(8,128)(2,1)}), bf16[640,1536]{1,0:T(8,128)(2,1)}) %all-gather.5.cloned.1.call-update) | async-done | bytes 1966096 | tf_op jit(solution)/shard_map/all_gather | solution.py:20
  38.7 2.1 convolution_convert_fusion.8
  40.8 4.1 collective-permute-start
  44.8 1.5 multiply_reduce_fusion.12
  47.6 3.5 collective-permute-start.1
  51.3 1.4 copy.43
  52.7 2.4 multiply_reduce_fusion.2
  58.1 2.6 fusion.106
  60.8 1.2 fusion.3
  61.9 2.1 copy-done
  64.1 2.6 fusion.39
  66.7 2.8 multiply_reduce_fusion.9
  71.1 1.0 multiply_convert_fusion.2
  72.1 41.5 %all-gather.9.cloned.1.call-done = bf16[640,4096]{1,0:T(8,128)(2,1)} async-done(((bf16[160,4096]{1,0:T(8,128)(2,1)}), bf16[640,4096]{1,0:T(8,128)(2,1)}) %all-gather.9.cloned.1.call-update) | async-done | bytes 5242896 | tf_op jit(solution)/shard_map/all_gather | solution.py:20
  113.6 3.9 fusion.22
  117.5 2.0 copy-done.67
  119.5 4.5 multiply_convert_fusion.1
  124.0 20.2 %all-gather.11.cloned.1.call-done = bf16[2048,640]{1,0:T(8,128)(2,1)} async-done(((bf16[512,640]{1,0:T(8,128)(2,1)}), bf16[2048,640]{1,0:T(8,128)(2,1)}) %all-gather.11.cloned.1.call-update) | async-done | bytes 2621456 | tf_op jit(solution)/shard_map/all_gather | solution.py:99
  144.2 4.4 multiply_reduce_fusion.7
  149.2 1.4 fusion.54
  150.6 4.7 fusion.11
  155.4 1.9 fusion.16
  157.4 2.1 multiply_reduce_fusion.3
  160.7 1.4 copy-done.59
  162.2 1.0 convolution_convert_fusion.5
  163.2 2.8 fusion
  166.1 2.9 fusion.2
  168.9 1.3 fusion.43
  170.3 1.4 collective-permute-start.2
  171.7 1.3 fusion.40
  173.0 1.4 collective-permute-start.3
  174.5 7.0 collective-permute-done.2
  181.6 2.2 bitcast_multiply_fusion.1
  187.2 1.1 convolution_convert_fusion.4
  189.6 1.5 pad_maximum_fusion.1
  191.1 3.3 convolution_convert_fusion.2
  194.4 1.6 convolution_convert_fusion.1
  196.0 2.7 pad_maximum_fusion
  199.8 3.3 convolution_convert_fusion.3
  203.1 5.2 convolution_convert_fusion
  208.4 22.5 %reduce-scatter.5.cloned.1.call-done = bf16[160,1536]{1,0:T(8,128)(2,1)} async-done(((bf16[640,1536]{1,0:T(8,128)(2,1)}), bf16[160,1536]{1,0:T(8,128)(2,1)}) %reduce-scatter.5.cloned.1.call-update) | async-done | bytes 491536 | tf_op jit(solution)/shard_map/reduce_scatter | solution.py:31
  230.9 1.7 slice.62
  232.7 1.6 fusion.104
  234.3 57.1 %reduce-scatter.9.cloned.1.call-done = bf16[160,4096]{1,0:T(8,128)(2,1)} async-done(((bf16[640,4096]{1,0:T(8,128)(2,1)}), bf16[160,4096]{1,0:T(8,128)(2,1)}) %reduce-scatter.9.cloned.1.call-update) | async-done | bytes 1310736 | tf_op jit(solution)/shard_map/reduce_scatter | solution.py:31
  291.4 2.5 fusion.102
  293.9 33.7 %reduce-scatter.7.cloned.1.call-done = bf16[256,640]{1,0:T(8,128)(2,1)} async-done(((bf16[1024,640]{1,0:T(8,128)(2,1)}), bf16[256,640]{1,0:T(8,128)(2,1)}) %reduce-scatter.7.cloned.1.call-update) | async-done | bytes 327696 | tf_op jit(solution)/shard_map/reduce_scatter | solution.py:277
  327.5 43.9 %reduce-scatter.11.cloned.1.call-done = bf16[512,640]{1,0:T(8,128)(2,1)} async-done(((bf16[2048,640]{1,0:T(8,128)(2,1)}), bf16[512,640]{1,0:T(8,128)(2,1)}) %reduce-scatter.11.cloned.1.call-update) | async-done | bytes 655376 | tf_op jit(solution)/shard_map/reduce_scatter | solution.py:288
  372.7 2.2 fusion.59
  376.2 2.7 fusion.49
  378.9 7.4 %all-reduce.18 = (bf16[640]{0:T(1024)(128)(2,1)S(1)}, bf16[640]{0:T(1024)(128)(2,1)S(1)}, bf16[640]{0:T(1024)(128)(2,1)S(1)}, bf16[640]{0:T(1024)(128)(2,1)S(1)}...) all-reduce(bf16[640]{0:T(1024)(128)(2,1)S(1)} %get-tuple-element.23, ...), channel_id=6, replica_groups=mesh['seq'=32,'fsdp'=4] {'fsdp'}, use_global_device_ids=true, to_apply=%region_27.28.clone | all-reduce | flops 3072 | bytes 12288
  386.8 83.3 %all-reduce.16 = (bf16[160]{0:T(256)(128)(2,1)S(1)}, bf16[160]{0:T(256)(128)(2,1)S(1)}, bf16[160]{0:T(256)(128)(2,1)S(1)}, bf16[160]{0:T(256)(128)(2,1)S(1)}, bf...) all-reduce(bf16[160]{0:T(256)(128)(2,1)S(1)} %dynamic-slice.7, ...), channel_id=1, replica_groups=mesh['seq'=32,'fsdp'=4] {'seq'}, use_global_device_ids=true, to_apply=%region_28.29 | all-reduce | flops 768 | bytes 3072 | tf_op jit(solution)/shard_map/psum | solution.py:318
  473.4 2.7 fusion.57
  476.2 216.3 %all-reduce.22.cloned.1.call-done = (bf16[160,1024]{1,0:T(8,128)(2,1)}, bf16[160,256]{1,0:T(8,128)(2,1)}, bf16[160,256]{1,0:T(8,128)(2,1)}, bf16[256,640]{1,0:T(...) async-done(((bf16[160,1024]{1,0:T(8,128)(2,1)}, bf16[160,256]{1,0:T(8,128)(2,1)}, bf16[160,256]{1,0:T(8,128)(2,1)}, ...) | async-done | bytes 2785296 | tf_op jit(solution)/shard_map/psum | solution.py:311
  692.5 1.6 convert_element_type.268
  694.1 1.6 convert_element_type.269
  695.8 1.9 convert_element_type.267
  697.6 1.9 convert_element_type.271
  699.5 1.2 convert_element_type.274
  700.7 1.2 convert_element_type.275
  701.9 1.1 convert_element_type.277
  (248 shorter events, 25.2 us)
Async XLA Ops:
  7.2 3.0 copy-start.23
  7.2 3.0 copy-start.24
  7.2 31.5 %all-gather.5.cloned.1.call-start = ((), (), s32[]{:S(2)}) async-start(), calls=%async_computation.4 | async-start | bytes 2457600 | tf_op jit(solution)/shard_map/all_gather | solution.py:20
  9.2 57.5 %all-gather.7.cloned.1.call-start = ((), (), s32[]{:S(2)}) async-start(), calls=%async_computation.5 | async-start | bytes 1638400 | tf_op jit(solution)/shard_map/all_gather | solution.py:97
  10.0 2.0 copy-start.56
  10.0 3.9 copy-start.5
  10.0 4.2 copy-start.53
  10.0 4.2 copy-start.60
  10.0 4.4 copy-start.61
  10.0 4.7 copy-start.62
  10.1 4.9 copy-start.63
  10.1 5.1 copy-start.64
  10.1 5.3 copy-start.65
  10.1 103.5 %all-gather.9.cloned.1.call-start = ((), (), s32[]{:S(2)}) async-start(), calls=%async_computation.6 | async-start | bytes 6553600 | tf_op jit(solution)/shard_map/all_gather | solution.py:20
  11.3 132.9 %all-gather.11.cloned.1.call-start = ((), (), s32[]{:S(2)}) async-start(), calls=%async_computation.7 | async-start | bytes 3276800 | tf_op jit(solution)/shard_map/all_gather | solution.py:99
  11.9 219.0 %reduce-scatter.5.cloned.1.call-start = ((), (), s32[]{:S(2)}) async-start(), calls=%async_computation.8 | async-start | bytes 2457600 | tf_op jit(solution)/shard_map/reduce_scatter | solution.py:31
  14.1 32.2 %copy-start.47 = (f32[512]{0:T(512)}, f32[512]{0:T(512)S(1)}, u32[]{:S(2)}) copy-start(f32[512]{0:T(512)S(1)} %fusion.50) | copy-start | bytes 6148
  14.1 38.6 %copy-start.45 = (f32[512]{0:T(512)}, f32[512]{0:T(512)S(1)}, u32[]{:S(2)}) copy-start(f32[512]{0:T(512)S(1)} %fusion.84) | copy-start | bytes 6148
  26.5 20.0 %copy-start.49 = (f32[256]{0:T(256)}, f32[256]{0:T(256)S(1)}, u32[]{:S(2)}) copy-start(f32[256]{0:T(256)S(1)} %convert_element_type.231) | copy-start | bytes 3076
  26.5 26.2 %copy-start.38 = (f32[640]{0:T(1024)}, f32[640]{0:T(1024)S(1)}, u32[]{:S(2)}) copy-start(f32[640]{0:T(1024)S(1)} %convert_element_type.228) | copy-start | bytes 7684
  30.2 16.4 %copy-start.11 = (f32[512,128]{0,1:T(8,128)}, f32[512,128]{0,1:T(8,128)S(1)}, u32[]{:S(2)}) copy-start(f32[512,128]{0,1:T(8,128)S(1)} %get-tuple-element.79) | copy-start | bytes 786436
  30.2 16.4 %copy-start.13 = (f32[512,128]{0,1:T(8,128)}, f32[512,128]{0,1:T(8,128)S(1)}, u32[]{:S(2)}) copy-start(f32[512,128]{0,1:T(8,128)S(1)} %get-tuple-element.80) | copy-start | bytes 786436
  40.8 21.2 %collective-permute-start = (bf16[512,256]{1,0:T(8,128)(2,1)}, bf16[512,256]{1,0:T(8,128)(2,1)}, u32[]{:S(2)}, u32[]{:S(2)}) collective-permute-start(bf16[512,256]{1,0:T(8,128)(2,1)} %convolution_convert_fusion.8), channel_id=1, source_target_pairs={{0,4},{4,8},{8,12},{12,16},{16,20},{20,24},{24,28},{28,32},{32,36}... | collective-permute-start | bytes 786440 | tf_op jit(solution)/shard_map/ppermute | solution.py:26
  46.5 4.6 copy-start.16
  47.6 10.3 %copy-start.18 = (bf16[512,256]{0,1:T(8,128)(2,1)}, bf16[512,256]{0,1:T(8,128)(2,1)S(1)}, u32[]{:S(2)}) copy-start(bf16[512,256]{0,1:T(8,128)(2,1)S(1)} %get-tuple-element.76) | copy-start | bytes 786436
  47.6 10.3 %collective-permute-start.1 = (bf16[512,256]{0,1:T(8,128)(2,1)S(1)}, bf16[512,256]{0,1:T(8,128)(2,1)}, u32[]{:S(2)}, u32[]{:S(2)}) collective-permute-start(bf16[512,256]{0,1:T(8,128)(2,1)S(1)} %get-tuple-element.76), channel_id=1, source_target_pairs={{0,4},{4,8},{8,12},{12,16},{16,20},{20,24},{24,28},{28,32},{32,36}... | collective-permute-start | bytes 786440 | tf_op jit(solution)/shard_map/ppermute | solution.py:26
  52.7 3.1 copy-start.51
  57.8 2.9 copy-start.21
  60.7 3.3 copy-start
  60.8 3.3 copy-start.43
  66.7 2.9 copy-start.66
  66.7 3.9 copy-start.6
  113.6 5.9 copy-start.27
  113.6 5.9 copy-start.57
  144.2 4.4 copy-start.10
  144.2 4.4 copy-start.37
  144.2 6.4 copy-start.68
  144.2 6.4 copy-start.72
  149.2 6.1 slice-start.2
  150.6 4.7 copy-start.25
  150.6 4.7 slice-start.3
  155.3 2.1 copy-start.71
  155.3 7.9 %slice-start = ((s8[8388608]{0:T(1024)(128)(4,1)}), s8[4194304]{0:T(1024)(128)(4,1)S(1)}, s32[]{:S(2)}) async-start(s8[8388608]{0:T(1024)(128)(4,1)} %bitcast.145), calls=%async_computation.13 | async-start | bytes 8388608
  157.4 2.1 copy-start.2
  157.4 5.8 slice-start.1
  160.4 2.8 copy-start.3
  166.0 2.9 copy-start.22
  170.3 11.2 %copy-start.14 = (f32[512,128]{0,1:T(8,128)S(1)}, f32[512,128]{0,1:T(8,128)}, u32[]{:S(2)}) copy-start(f32[512,128]{0,1:T(8,128)} %copy-done.13) | copy-start | bytes 786436
  170.3 11.2 %collective-permute-start.2 = (bf16[512,256]{0,1:T(8,128)(2,1)S(1)}, bf16[512,256]{0,1:T(8,128)(2,1)S(1)}, u32[]{:S(2)}, u32[]{:S(2)}) collective-permute-start(bf16[512,256]{0,1:T(8,128)(2,1)S(1)} %slice.82), channel_id=1, source_target_pairs={{4,0},{8,4},{12,8},{16,12},{20,16},{24,20},{28,24},{32,28},{36,32}... | collective-permute-start | bytes 786440 | tf_op jit(solution)/shard_map/ppermute | solution.py:26
  173.0 16.0 %copy-start.34 = (f32[1024,256]{1,0:T(8,128)}, f32[1024,256]{1,0:T(8,128)S(1)}, u32[]{:S(2)}) copy-start(f32[1024,256]{1,0:T(8,128)S(1)} %fusion.40) | copy-start | bytes 3145732
  173.0 8.6 %copy-start.19 = (bf16[512,256]{0,1:T(8,128)(2,1)S(1)}, bf16[512,256]{0,1:T(8,128)(2,1)}, u32[]{:S(2)}) copy-start(bf16[512,256]{0,1:T(8,128)(2,1)} %copy-done.18) | copy-start | bytes 786436
  173.0 16.0 %collective-permute-start.3 = (bf16[512,256]{1,0:T(8,128)(2,1)S(1)}, bf16[512,256]{1,0:T(8,128)(2,1)S(1)}, u32[]{:S(2)}, u32[]{:S(2)}) collective-permute-start(bf16[512,256]{1,0:T(8,128)(2,1)S(1)} %slice.81), channel_id=1, source_target_pairs={{4,0},{8,4},{12,8},{16,12},{20,16},{24,20},{28,24},{32,28},{36,32}... | collective-permute-start | bytes 786440 | tf_op jit(solution)/shard_map/ppermute | solution.py:26
  191.1 100.3 %reduce-scatter.9.cloned.1.call-start = ((), (), s32[]{:S(2)}) async-start(), calls=%async_computation.10 | async-start | bytes 6553600 | tf_op jit(solution)/shard_map/reduce_scatter | solution.py:31
  191.1 3.3 copy-start.70
  198.7 4.4 copy-start.26
  198.7 128.8 %reduce-scatter.7.cloned.1.call-start = ((), (), s32[]{:S(2)}) async-start(), calls=%async_computation.9 | async-start | bytes 1638400 | tf_op jit(solution)/shard_map/reduce_scatter | solution.py:277
  203.1 168.3 %reduce-scatter.11.cloned.1.call-start = ((), (), s32[]{:S(2)}) async-start(), calls=%async_computation.11 | async-start | bytes 3276800 | tf_op jit(solution)/shard_map/reduce_scatter | solution.py:288
  208.3 484.1 %all-reduce.22.cloned.1.call-start = ((), (), s32[]{:S(2)}) async-start(), calls=%async_computation.12 | async-start | bytes 5570560 | tf_op jit(solution)/shard_map/psum | solution.py:311
  234.3 138.4 %copy-start.17 = (bf16[640,1536]{1,0:T(8,128)(2,1)S(1)}, bf16[640,1536]{1,0:T(8,128)(2,1)}, u32[]{:S(2)}) copy-start(bf16[640,1536]{1,0:T(8,128)(2,1)} %all-gather.5.cloned.1.call-done) | copy-start | bytes 5898244
  376.2 97.2 %copy-start.48 = (f32[512]{0:T(512)S(1)}, f32[512]{0:T(512)}, u32[]{:S(2)}) copy-start(f32[512]{0:T(512)} %copy-done.47) | copy-start | bytes 6148
  376.2 97.2 %copy-start.4 = (f32[512,640]{1,0:T(8,128)S(1)}, f32[512,640]{1,0:T(8,128)}, u32[]{:S(2)}) copy-start(f32[512,640]{1,0:T(8,128)} %copy-done.3) | copy-start | bytes 3932164
  692.5 7.0 copy-start.33
  694.1 6.6 copy-start.32
  699.5 2.4 copy-start.31
  (26 other events, 32.8 us)
Sparse Core Ops, SparseCore 0:
  10.3 28.3 all-gather.4
  40.3 21.7 all-gather.6
  64.4 49.1 all-gather.8
  115.1 29.0 all-gather.10
  191.2 39.7 reduce-scatter.4
  233.6 57.7 reduce-scatter.8
  294.6 32.8 reduce-scatter.6
  330.3 40.9 reduce-scatter.10
  375.0 317.4 all-reduce.21
where the time goes:
time: 715 us; the launch traced here: 710 us
  waiting for transfers between devices  452 us (63%)
  blocking collectives  101 us (14%)
  matrix products  64.8 us (9%)
  other arithmetic  41.7 us (6%)
  local copies, waits for them, and re-layouts  21.4 us (3%)
  between operations  17.9 us (3%)
  starting transfers between devices  11 us (2%)
    psum x1, waiting for transfers between devices, body(): lax.psum(shares[0].astype(jnp.bfloat16), 'seq').astype(jnp.float32)  216 us
    psum x1, blocking collectives, body(): lax.psum(shares[7].astype(jnp.bfloat16), 'seq').astype(jnp.float32)  83.3 us
    reduce_scatter x2, waiting for transfers between devices, side_by_side_2(): lax.psum_scatter(both, axis, scatter_dimension=dim, tiled=True)  79.6 us
    all_gather x2, waiting for transfers between devices, side_by_side(): lax.all_gather(both, axis, axis=dim, tiled=True)  50 us
    reduce_scatter x1, waiting for transfers between devices, body(): lax.psum_scatter(grad_down.astype(jnp.bfloat16), 'fsdp', scatter_dimensio...  43.9 us
    reduce_scatter x1, waiting for transfers between devices, body(): lax.psum_scatter(grad_output.astype(jnp.bfloat16), 'fsdp', scatter_dimens...  33.7 us
    dot_general x7, matrix products, forward_dot(): return jnp.dot(left, right, preferred_element_type=jnp.float32)  21.6 us
    all_gather x1, waiting for transfers between devices, body(): lax.all_gather(w_down, 'fsdp', axis=0, tiled=True)  20.2 us
  transfers between devices with their start and end apart: 13, of which 9 were waited for; matrix products, arithmetic and copies ran while one was open for 11% of the time, Pallas kernels for 0%

commit v1 on v0

v1 whole, which is shorter than its diff:
```python
import jax
import jax.numpy as jnp
from jax import lax
from jax.experimental import pallas as pl
from jax.experimental.pallas import tpu as pltpu
from jax.sharding import PartitionSpec as P

WINDOW = 512


epsilon = 1e-06
rope_base = 10000.0
masked_value = -1e30


def from_behind(shard, axis, by):
    count = lax.axis_size(axis)
    pairs = [(i, i + by) for i in range(count) if 0 <= i + by < count]
    return lax.ppermute(shard, axis, pairs)


MESH = pl.DeviceIdType.MESH
DIMS = ("C", "X1", "X0", "Y1", "Y0", "Z1", "Z0")


def place():
    return lax.axis_index("seq"), lax.axis_index("fsdp")


def bit_of(dim, s, f):
    if dim == "C":
        return lax.rem(f, 2)
    if dim == "X1":
        return lax.div(f, 2)
    if dim == "X0":
        return lax.rem(lax.rem(lax.div(s, 4), 2) + lax.div(f, 2), 2)
    at = lax.rem(s, 4) if dim[0] == "Y" else lax.div(s, 8)
    if dim[1] == "1":
        return lax.div(at, 2)
    return lax.rem(lax.rem(at, 2) + lax.div(at, 2), 2)


def partner(dim, s, f):
    if dim == "C":
        return (s, f + 1 - 2 * lax.rem(f, 2))
    step = 1 - 2 * lax.rem(lax.div(s, 4), 2)
    if dim == "X0":
        return (s + 4 * step, f)
    if dim == "X1":
        return (s + 4 * step, f + 2 - 4 * lax.div(f, 2))
    at, scale = (lax.rem(s, 4), 1) if dim[0] == "Y" else (lax.div(s, 8), 8)
    if dim[1] == "1":
        return (s + scale * (3 - 2 * at), f)
    return (s + scale * (1 - 2 * lax.rem(at, 2)), f)


def greet(s, f):
    barrier = pltpu.get_barrier_semaphore()
    for dim in DIMS:
        pl.semaphore_signal(barrier, inc=1, device_id=partner(dim, s, f), device_id_type=MESH)
    pl.semaphore_wait(barrier, len(DIMS))


def span(start, size, tile):
    if isinstance(start, int):
        return pl.ds(start, size)
    return pl.ds(pl.multiple_of(start, tile), size)


class Region:
    def __init__(self, q, r, c):
        self.q, self.r, self.c = q, r, c

    def of(self, ref):
        return ref.at[pl.ds(*self.q), span(*self.r, 16), span(*self.c, 128)]

    def flat(self, ref, r0=0, c0=0):
        return ref.at[span(self.r[0] + r0, self.r[1], 16), span(self.c[0] + c0, self.c[1], 128)]

    def halved(self, axis, bit):
        start, size = getattr(self, axis)
        half = size // 2
        mine = Region(self.q, self.r, self.c)
        setattr(mine, axis, (start + bit * half, half))
        theirs = Region(self.q, self.r, self.c)
        setattr(theirs, axis, (start + (1 - bit) * half, half))
        return mine, theirs

    @property
    def shape(self):
        return (self.q[1], self.r[1], self.c[1])


def rows_per_step(rows, cols):
    best = 16
    for n in (32, 48, 64, 80, 96, 128, 160):
        if rows % n == 0 and n * cols <= 48 * 2048:
            best = n
    return best


def add_blocks(out, first, second, shape):
    quarters, rows, cols = shape
    step = rows_per_step(rows, cols)
    for q in range(quarters):

        def body(i, carry, q=q):
            at = i * step
            ref, index = out(q, at, step)
            ref_a, index_a = first(q, at, step)
            ref_b, index_b = second(q, at, step)
            ref[index] = ref_a[index_a] + ref_b[index_b]
            return carry

        lax.fori_loop(0, rows // step, body, 0)


def view(ref, region):
    def pick(q, at, step):
        rows = span(region.r[0] + at, step, 16)
        return ref, (region.q[0] + q, rows, span(region.c[0], region.c[1], 128))

    return pick


def flat_view(ref, region, r0, c0):
    def pick(q, at, step):
        return ref, (span(region.r[0] + r0 + at, step, 16), span(region.c[0] + c0, region.c[1], 128))

    return pick


def whole_view(ref):
    def pick(q, at, step):
        return ref, (q, span(at, step, 16), slice(None))

    return pick


ORDERS = (
    ("X1", "Y1", "Z1", "X0", "Y0", "Z0"),
    ("Y1", "Z1", "X0", "X1", "Y0", "Z0"),
    ("Z1", "X0", "Y0", "X1", "Z0", "Y1"),
    ("X0", "Y0", "Z0", "X1", "Y1", "Z1"),
    ("Y0", "Z0", "X1", "Y1", "Z1", "X0"),
    ("Z0", "X1", "Y1", "Z1", "X0", "Y0"),
)
PARTS = (
    (0, 0, 384, 0, 640, ORDERS[0], "rrr"),
    (1, 0, 160, 0, 1536, ORDERS[1], "ccr"),
    (1, 0, 160, 1536, 1536, ORDERS[2], "ccr"),
    (1, 0, 160, 3072, 1024, ORDERS[3], "ccc"),
    (0, 384, 128, 0, 640, ORDERS[3], "rrr"),
    (2, 0, 256, 0, 640, ORDERS[4], "rrr"),
    (3, 0, 160, 0, 1536, ORDERS[5], "ccr"),
)
SHARES = ((512, 640), (160, 4096), (256, 640), (160, 1536))


def part_shapes(part):
    _, _, rows, _, cols, order, splits = part
    shapes, shape, cut = [], [2, rows, cols], iter(splits)
    for dim in order[:4]:
        axis = 0 if dim == "X1" else {"r": 1, "c": 2}[next(cut)]
        shape[axis] //= 2
        shapes.append(tuple(shape))
    return shapes


def reduce_kernel(*refs):
    n = len(SHARES)
    grads, gains = refs[:n], refs[n]
    totals, gain_total = refs[n + 1 : 2 * n + 1], refs[2 * n + 1]
    scratch = list(refs[2 * n + 2 :])
    acc, from_core, inbox, extra = [], [], [], []
    for _ in PARTS:
        acc.append(scratch.pop(0))
        from_core.append(scratch.pop(0))
        inbox.append([scratch.pop(0) for _ in range(4)])
        extra.append([scratch.pop(0) for _ in range(3)])
    gain_in, gain_sum, send_sem, recv_sem, local_sem = scratch

    s, f = place()
    greet(s, f)
    pending, count = [], [0]

    def send(src, dst, dim):
        copy = pltpu.make_async_remote_copy(
            src_ref=src,
            dst_ref=dst,
            send_sem=send_sem.at[count[0]],
            recv_sem=recv_sem.at[count[0]],
            device_id=partner(dim, s, f),
            device_id_type=MESH,
        )
        copy.start()
        count[0] += 1
        pending.append(copy)
        return copy

    core = bit_of("C", s, f)
    flights, loads, where = [], [], []
    gain_flight = send(gains, gain_in.at[0], "C")
    for p, (tensor, r0, rows, c0, cols, order, splits) in enumerate(PARTS):
        block = (pl.ds(0, 2), pl.ds(r0, rows), pl.ds(c0, cols))
        flights.append(send(grads[tensor].at[block[0], 1 - core, block[1], block[2]], from_core[p], "C"))
        load = pltpu.make_async_copy(
            grads[tensor].at[block[0], core, block[1], block[2]], acc[p], local_sem.at[p]
        )
        load.start()
        loads.append(load)
        where.append(Region((0, 2), (0, rows), (0, cols)))
    cuts = [iter(part[6]) for part in PARTS]
    trail = [[] for _ in PARTS]

    gain_dims = ("C", "X1", "X0", "Y1", "Y0", "Z1", "Z0")

    def gain_step(step):
        gain_flight.wait_recv()
        before = gains if step == 0 else gain_sum.at[step - 1]
        gain_sum[step] = before[...] + gain_in[step]
        if step < 6:
            return send(gain_sum.at[step], gain_in.at[step + 1], gain_dims[step + 1])
        return None

    for step in range(5):
        for p, part in enumerate(PARTS):
            order = part[5]
            flights[p].wait_recv()
            if step == 0:
                loads[p].wait()
                source = whole_view(from_core[p])
            else:
                source = whole_view(inbox[p][step - 1])
            add_blocks(view(acc[p], where[p]), view(acc[p], where[p]), source, where[p].shape)
            if step == 4:
                flights[p] = send(where[p].of(acc[p]), extra[p][0], order[4])
                continue
            dim = order[step]
            axis = "q" if dim == "X1" else next(cuts[p])
            trail[p].append((dim, axis))
            where[p], theirs = where[p].halved(axis, bit_of(dim, s, f))
            flights[p] = send(theirs.of(acc[p]), inbox[p][step], dim)
        gain_flight = gain_step(step)
    for p, part in enumerate(PARTS):
        flights[p].wait_recv()
        add_blocks(whole_view(extra[p][1]), view(acc[p], where[p]), whole_view(extra[p][0]), where[p].shape)
        flights[p] = send(extra[p][1], extra[p][2], part[5][5])
    gain_flight = gain_step(5)
    back = []
    for p, part in enumerate(PARTS):
        tensor, r0, _, c0, _, _, _ = part
        flights[p].wait_recv()
        add_blocks(
            flat_view(totals[tensor], where[p], r0, c0),
            whole_view(extra[p][1]),
            whole_view(extra[p][2]),
            where[p].shape,
        )
        back.append([move for move in reversed(trail[p]) if move[1] != "q"])
        region = where[p].flat(totals[tensor], r0, c0)
        flights[p] = send(region, region, back[p][0][0])
    gain_step(6)
    for step in range(3):
        for p, part in enumerate(PARTS):
            tensor, r0, _, c0, _, _, _ = part
            dim, axis = back[p][step]
            flights[p].wait_recv()
            start, size = getattr(where[p], axis)
            setattr(where[p], axis, (start - bit_of(dim, s, f) * size, 2 * size))
            if step < 2:
                region = where[p].flat(totals[tensor], r0, c0)
                flights[p] = send(region, region, back[p][step + 1][0])
    gain_total[...] = gain_sum[6, bit_of("X1", s, f) * 2 + core]
    for copy in pending:
        copy.wait_send()


def reduce_gradients(grads, gains):
    scratch, sends = [], 7
    for part in PARTS:
        shapes = part_shapes(part)
        scratch += [pltpu.VMEM((2, part[2], part[4]), jnp.bfloat16)] * 2
        scratch += [pltpu.VMEM(shape, jnp.bfloat16) for shape in shapes]
        scratch += [pltpu.VMEM(shapes[-1], jnp.bfloat16)] * 3
        sends += 10
    scratch += [
        pltpu.VMEM((7, 4, 8, 128), jnp.float32),
        pltpu.VMEM((7, 4, 8, 128), jnp.float32),
        pltpu.SemaphoreType.DMA((sends,)),
        pltpu.SemaphoreType.DMA((sends,)),
        pltpu.SemaphoreType.DMA((len(PARTS),)),
    ]
    return pl.pallas_call(
        reduce_kernel,
        out_shape=[jax.ShapeDtypeStruct(shape, jnp.bfloat16) for shape in SHARES]
        + [jax.ShapeDtypeStruct((8, 128), jnp.float32)],
        in_specs=[pl.BlockSpec(memory_space=pl.ANY)] * len(SHARES)
        + [pl.BlockSpec(memory_space=pltpu.VMEM)],
        out_specs=[pl.BlockSpec(memory_space=pltpu.VMEM)] * (len(SHARES) + 1),
        scratch_shapes=scratch,
        compiler_params=pltpu.CompilerParams(
            collective_id=1, has_side_effects=True, vmem_limit_bytes=48 << 20
        ),
        name="reduce_gradients",
    )(*grads, gains)


PIECES = (
    (0, 0, 0, 160, 1024, "X0", "Z0", "c"),
    (1, 0, 1024, 160, 256, "Z0", "X0", "c"),
    (2, 0, 1280, 160, 256, "Z0", "X0", "c"),
    (3, 1, 0, 256, 640, "Y0", "X0", "r"),
    (4, 2, 0, 160, 2048, "Z1", "Y1", "c"),
    (5, 2, 2048, 160, 2048, "Z0", "Y0", "c"),
    (6, 3, 0, 512, 640, "Y1", "Z1", "r"),
)
WHOLES = ((4, 160, 1536), (4, 256, 640), (4, 160, 4096), (4, 512, 640))


def gather_kernel(*refs):
    shards, gains = refs[:7], refs[7]
    outs, gain_out = refs[8:12], refs[12]
    send_sem, recv_sem, local_sem = refs[13:]
    s, f = place()
    greet(s, f)
    copies, count = [], [0]

    def send(src, dst, dim):
        copy = pltpu.make_async_remote_copy(
            src_ref=src,
            dst_ref=dst,
            send_sem=send_sem.at[count[0]],
            recv_sem=recv_sem.at[count[0]],
            device_id=partner(dim, s, f),
            device_id_type=MESH,
        )
        copy.start()
        count[0] += 1
        copies.append(copy)
        return copy

    core, high = bit_of("C", s, f), bit_of("X1", s, f)
    far = 2 * (1 - high) + core
    own, locals_ = f, []
    flights = []
    gain_flight = send(gains, gain_out.at[own], "X1")
    load = pltpu.make_async_copy(gains, gain_out.at[own], local_sem.at[7])
    load.start()
    locals_.append(load)
    sides = [send(gains, gain_out.at[own], "C")]

    def boxes(piece, bit_one, bit_two):
        _, _, c0, rows, cols, _, _, cut = piece
        half = rows // 2
        if cut == "c":
            quarter = ((bit_two * half, half), (bit_one * (cols // 2), cols // 2))
        else:
            quarter = ((bit_two * half + bit_one * (half // 2), half // 2), (0, cols))
        return quarter, ((bit_two * half, half), (0, cols))

    def cut_of(ref, box, c0=0):
        (r, nr), (c, nc) = box
        return ref.at[span(r, nr, 16), span(c + c0, nc, 128)]

    for i, piece in enumerate(PIECES):
        quarter, _ = boxes(piece, bit_of(piece[5], s, f), bit_of(piece[6], s, f))
        flights.append(send(cut_of(shards[i], quarter), cut_of(outs[piece[1]].at[own], quarter, piece[2]), "X1"))
    for i, piece in enumerate(PIECES):
        out, c0, cols = outs[piece[1]].at[own], piece[2], piece[4]
        sides.append(send(shards[i], out.at[:, pl.ds(c0, cols)], "C"))
        load = pltpu.make_async_copy(shards[i], out.at[:, pl.ds(c0, cols)], local_sem.at[i])
        load.start()
        locals_.append(load)
    gain_flight.wait_recv()
    sides.append(send(gain_out.at[far], gain_out.at[far], "C"))
    for step in range(3):
        for i, piece in enumerate(PIECES):
            out, c0 = outs[piece[1]].at[far], piece[2]
            one, two = bit_of(piece[5], s, f), bit_of(piece[6], s, f)
            quarter, half = boxes(piece, one, two)
            flights[i].wait_recv()
            if step == 0:
                flights[i] = send(cut_of(out, quarter, c0), cut_of(out, quarter, c0), piece[5])
                sides.append(send(cut_of(out, quarter, c0), cut_of(out, quarter, c0), "C"))
            elif step == 1:
                other, _ = boxes(piece, 1 - one, two)
                flights[i] = send(cut_of(out, half, c0), cut_of(out, half, c0), piece[6])
                sides.append(send(cut_of(out, other, c0), cut_of(out, other, c0), "C"))
            else:
                _, other = boxes(piece, one, 1 - two)
                sides.append(send(cut_of(out, other, c0), cut_of(out, other, c0), "C"))
    for copy in sides:
        copy.wait_recv()
    for copy in copies:
        copy.wait_send()
    for load in locals_:
        load.wait()


def gather_weights(shards, gains):
    sends = 7 * len(PIECES) + 3
    return pl.pallas_call(
        gather_kernel,
        out_shape=[jax.ShapeDtypeStruct(shape, jnp.bfloat16) for shape in WHOLES]
        + [jax.ShapeDtypeStruct((4, 8, 128), jnp.float32)],
        in_specs=[pl.BlockSpec(memory_space=pl.ANY)] * 8,
        out_specs=[pl.BlockSpec(memory_space=pl.ANY)] * 5,
        scratch_shapes=[
            pltpu.SemaphoreType.DMA((sends,)),
            pltpu.SemaphoreType.DMA((sends,)),
            pltpu.SemaphoreType.DMA((8,)),
        ],
        compiler_params=pltpu.CompilerParams(collective_id=0, has_side_effects=True),
        name="gather_weights",
    )(*shards, gains)


def rms_scale(values, gains):
    return values * lax.rsqrt(jnp.mean(values * values, -1, keepdims=True) + epsilon) * gains


def rope_tables(positions, head_width):
    half_width = head_width // 2
    frequency = rope_base ** (-(jnp.arange(half_width, dtype=jnp.float32) * (2.0 / head_width)))
    angles = positions[:, None] * frequency[None, :]
    cosine = jnp.cos(angles)
    sine_part = jnp.sin(angles)
    return (jnp.concatenate([cosine, cosine], -1), jnp.concatenate([sine_part, sine_part], -1))


def rotate(values, cosine, sine_part):
    half_width = values.shape[-1] // 2
    turned = jnp.concatenate([-values[..., half_width:], values[..., :half_width]], -1)
    return values * cosine + turned * sine_part


def forward_dot(left, right):
    return jnp.dot(left, right, preferred_element_type=jnp.float32)


def contract_rows(left, right):
    return lax.dot_general(
        left, right, (((0,), (0,)), ((), ())), preferred_element_type=jnp.float32
    )


def contract_cols(left, right):
    return lax.dot_general(
        left, right, (((1,), (1,)), ((), ())), preferred_element_type=jnp.float32
    )


def gated_product(gate_value, up_value):
    return jax.nn.gelu(gate_value, approximate=True) * up_value


def body(
    inputs,
    doc_start,
    w_query,
    w_key,
    w_value,
    w_output,
    w_gate,
    w_up,
    w_down,
    norm_attn_in,
    norm_attn_out,
    norm_ffn_in,
    norm_ffn_out,
    norm_query,
    norm_key,
    cotangent,
):
    gain_shards = jnp.concatenate(
        [norm_attn_in, norm_attn_out, norm_ffn_in, norm_ffn_out, norm_query, norm_key]
    ).astype(jnp.float32)
    gain_shards = jnp.pad(gain_shards, (0, 256)).reshape(8, 128)
    full_qkv, full_output, full_gate_up, full_down, all_gains = gather_weights(
        (w_query, w_key, w_value, w_output, w_gate, w_up, w_down), gain_shards
    )
    full_qkv = full_qkv.reshape(640, 1536)
    full_output = full_output.reshape(1024, 640)
    full_gate_up = full_gate_up.reshape(640, 4096)
    full_down = full_down.reshape(2048, 640)
    all_gains = all_gains.reshape(4, 1024)
    gain_attn_in, gain_attn_out, gain_ffn_in, gain_ffn_out = [
        all_gains[:, 160 * i : 160 * (i + 1)].reshape(640) for i in range(4)
    ]
    gain_query = all_gains[:, 640:704].reshape(256)
    gain_key = all_gains[:, 704:768].reshape(256)
    length = inputs.shape[1]
    head_width, head_count = 256, 4
    span_count = -(-(WINDOW - 1) // length)
    block_index = lax.axis_index("seq")
    row_index = block_index * length + jnp.arange(length, dtype=jnp.int32)
    doc_local = doc_start[0]
    positions = (row_index - doc_local).astype(jnp.float32)
    cosine, sine_part = rope_tables(positions, head_width)
    source = inputs[0].astype(jnp.float32)
    normed, pull_attn_in = jax.vjp(rms_scale, source, gain_attn_in)
    normed_low = normed.astype(jnp.bfloat16)
    raw = forward_dot(normed_low, full_qkv)
    query_raw, key_raw, value_raw = raw[:, :1024], raw[:, 1024:1280], raw[:, 1280:]

    def shape_query(raw_rows, gains):
        return rotate(
            rms_scale(raw_rows.reshape(length, head_count, head_width), gains),
            cosine[:, None, :],
            sine_part[:, None, :],
        )

    def shape_key(raw_rows, gains):
        return rotate(rms_scale(raw_rows, gains), cosine, sine_part)

    query_rows, pull_query = jax.vjp(shape_query, query_raw, gain_query)
    key_rows, pull_key = jax.vjp(shape_key, key_raw, gain_key)
    query_low = query_rows.astype(jnp.bfloat16)
    key_low = key_rows.astype(jnp.bfloat16)
    value_low = value_raw.astype(jnp.bfloat16)
    pair = jnp.concatenate([key_low, value_low], 1)
    pair = jnp.concatenate([from_behind(pair, "seq", 1), pair], 0)
    all_keys, all_values = pair[:, :256], pair[:, 256:]
    key_index = (block_index - span_count) * length + jnp.arange(
        (span_count + 1) * length, dtype=jnp.int32
    )
    visible = (
        (key_index[None, :] >= doc_local[:, None])
        & (key_index[None, :] <= row_index[:, None])
        & (row_index[:, None] - key_index[None, :] < WINDOW)
    )
    score_scale = head_width ** (-0.5)

    def score_rows():
        raw_scores = (
            jnp.einsum("thd,kd->htk", query_low, all_keys, preferred_element_type=jnp.float32)
            * score_scale
        )
        return jnp.where(visible[None], raw_scores, masked_value)

    scores = score_rows()
    row_max = jnp.max(scores, -1, keepdims=True)
    shifted = jnp.exp(scores - row_max)
    row_total = jnp.sum(shifted, -1, keepdims=True)
    soft_weights = shifted / row_total
    log_total = row_max + jnp.log(row_total)
    weights_low = soft_weights.astype(jnp.bfloat16)
    attended = jnp.einsum(
        "htk,kd->thd", weights_low, all_values, preferred_element_type=jnp.float32
    )
    attended = attended.reshape(length, head_count * head_width).astype(jnp.bfloat16)
    projected = forward_dot(attended, full_output)
    branch_one, pull_attn_out = jax.vjp(rms_scale, projected, gain_attn_out)
    hidden_one = source + branch_one
    normed_two, pull_ffn_in = jax.vjp(rms_scale, hidden_one, gain_ffn_in)
    normed_two_low = normed_two.astype(jnp.bfloat16)
    gate_up = forward_dot(normed_two_low, full_gate_up)
    gate_value, up_value = gate_up[:, :2048], gate_up[:, 2048:]
    product, pull_product = jax.vjp(gated_product, gate_value, up_value)
    product_low = product.astype(jnp.bfloat16)
    down_value = forward_dot(product_low, full_down)
    branch_two, pull_ffn_out = jax.vjp(rms_scale, down_value, gain_ffn_out)
    layer_out = (hidden_one + branch_two).astype(jnp.bfloat16)[None]
    upstream = cotangent[0].astype(jnp.float32)
    d_down, grad_ffn_out = pull_ffn_out(upstream)
    d_down_low = d_down.astype(jnp.bfloat16)
    grad_down = contract_rows(product_low, d_down_low)
    d_product = contract_cols(d_down_low, full_down)
    d_gate, d_up = pull_product(d_product)
    d_gate_up = jnp.concatenate([d_gate.astype(jnp.bfloat16), d_up.astype(jnp.bfloat16)], 1)
    grad_gate_up = contract_rows(normed_two_low, d_gate_up)
    d_normed_two = contract_cols(d_gate_up, full_gate_up)
    d_hidden_part, grad_ffn_in = pull_ffn_in(d_normed_two)
    d_hidden = upstream + d_hidden_part
    d_projected, grad_attn_out = pull_attn_out(d_hidden)
    d_projected_low = d_projected.astype(jnp.bfloat16)
    grad_output = contract_rows(attended, d_projected_low)
    d_attended = (
        contract_cols(d_projected_low, full_output)
        .astype(jnp.bfloat16)
        .reshape(length, head_count, head_width)
    )
    soft_again = jnp.exp(score_rows() - log_total)
    d_soft = jnp.einsum("thd,kd->htk", d_attended, all_values, preferred_element_type=jnp.float32)
    inner_sum = jnp.sum(soft_again * d_soft, -1, keepdims=True)
    d_scores = (soft_again * (d_soft - inner_sum)).astype(jnp.bfloat16)
    d_queries = (
        jnp.einsum("htk,kd->thd", d_scores, all_keys, preferred_element_type=jnp.float32)
        * score_scale
    )
    d_keys = (
        jnp.einsum("htk,thd->kd", d_scores, query_low, preferred_element_type=jnp.float32)
        * score_scale
    )
    d_values = jnp.einsum(
        "htk,thd->kd",
        soft_again.astype(jnp.bfloat16),
        d_attended,
        preferred_element_type=jnp.float32,
    )
    d_key_own = d_keys[span_count * length :]
    d_value_own = d_values[span_count * length :]
    first = jnp.concatenate([d_keys[:length], d_values[:length]], 1).astype(jnp.bfloat16)
    back = from_behind(first, "seq", -1).astype(jnp.float32)
    key_back, value_back = back[:, :256], back[:, 256:]
    d_key_own = d_key_own + key_back
    d_value_own = d_value_own + value_back
    d_key_raw, grad_key_norm = pull_key(d_key_own)
    d_query_raw, grad_query_norm = pull_query(d_queries)
    d_raw = jnp.concatenate(
        [
            d_query_raw.astype(jnp.bfloat16),
            d_key_raw.astype(jnp.bfloat16),
            d_value_own.astype(jnp.bfloat16),
        ],
        1,
    )
    grad_qkv = contract_rows(normed_low, d_raw)
    d_normed = contract_cols(d_raw, full_qkv)
    d_source, grad_attn_in = pull_attn_in(d_normed)
    input_grad = (d_hidden + d_source)[None]
    gain_grads = jnp.concatenate(
        [g.reshape(4, -1) for g in (grad_attn_in, grad_attn_out, grad_ffn_in, grad_ffn_out, grad_query_norm, grad_key_norm)],
        1,
    )
    gain_grads = jnp.pad(gain_grads, ((0, 0), (0, 256))).reshape(4, 8, 128)
    down, gate_up_share, output, qkv, gains = reduce_gradients(
        [
            grad.astype(jnp.bfloat16).reshape(2, 2, grad.shape[0] // 4, grad.shape[1])
            for grad in (grad_down, grad_gate_up, grad_output, grad_qkv)
        ],
        gain_grads,
    )
    gains = gains.reshape(1024)
    return (
        layer_out,
        input_grad,
        qkv[:, :1024].astype(jnp.float32),
        qkv[:, 1024:1280].astype(jnp.float32),
        qkv[:, 1280:].astype(jnp.float32),
        output.astype(jnp.float32),
        gate_up_share[:, :2048].astype(jnp.float32),
        gate_up_share[:, 2048:].astype(jnp.float32),
        down.astype(jnp.float32),
        gains[:160],
        gains[160:320],
        gains[320:480],
        gains[480:640],
        gains[640:704],
        gains[704:768],
    )


def solution(mesh):
    in_specs = (
        P("fsdp", "seq", None),
        P("fsdp", "seq"),
        P("fsdp", None),
        P("fsdp", None),
        P("fsdp", None),
        P("fsdp", None),
        P("fsdp", None),
        P("fsdp", None),
        P("fsdp", None),
        P("fsdp"),
        P("fsdp"),
        P("fsdp"),
        P("fsdp"),
        P("fsdp"),
        P("fsdp"),
        P("fsdp", "seq", None),
    )
    out_specs = (
        P("fsdp", "seq", None),
        P("fsdp", "seq", None),
        P("fsdp", None),
        P("fsdp", None),
        P("fsdp", None),
        P("fsdp", None),
        P("fsdp", None),
        P("fsdp", None),
        P("fsdp", None),
        P("fsdp"),
        P("fsdp"),
        P("fsdp"),
        P("fsdp"),
        P("fsdp"),
        P("fsdp"),
    )
    return jax.shard_map(body, mesh=mesh, in_specs=in_specs, out_specs=out_specs, check_vma=False)
```

time: 715 us -> 312 us (0.44)
  waiting for transfers between devices: 452 us -> 5.03 us
  Pallas kernels: 0 us -> 159 us
  blocking collectives: 101 us -> 0 us
  between operations: 17.9 us -> 1.57 us
  local copies, waits for them, and re-layouts: 21.4 us -> 35.4 us
    psum x1 -> x0, waiting for transfers between devices: 216 us -> none  [body(): lax.psum(shares[0].astype(jnp.bfloat16), 'seq').astype(jnp.float32)]
    pallas_call x0 -> x2, Pallas kernels: none -> 159 us  [the longest x1 90.8 us: gather_weights(): pl.pallas_call(gather_kernel, out_shape=[jax.ShapeDtypeStruct(shape, jnp....]
    reduce_scatter x4 -> x0, waiting for transfers between devices: 157 us -> none  [the longest x2 79.6 us: side_by_side_2(): lax.psum_scatter(both, axis, scatter_dimension=dim, tiled=True)]
    psum x1 -> x0, blocking collectives: 83.3 us -> none  [body(): lax.psum(shares[7].astype(jnp.bfloat16), 'seq').astype(jnp.float32)]
    all_gather x4 -> x0, waiting for transfers between devices: 70.2 us -> none  [the longest x2 50 us: side_by_side(): lax.all_gather(both, axis, axis=dim, tiled=True)]
    unnamed x2 -> x0, blocking collectives: 17.7 us -> none
    dot_general x7 -> x4, matrix products: 21.6 us -> 9.72 us  [forward_dot(): return jnp.dot(left, right, preferred_element_type=jnp.float32)]
    reshape x0 -> x9, local copies, waits for them, and re-layouts: none -> 7.42 us  [the longest x2 4.29 us: shape_query(): raw_rows.reshape(length, head_count, head_width)]
  transfers between devices with their start and end apart: 13 -> 2, of which waited for: 9 -> 1; matrix products, arithmetic and copies ran while one was open for 11% -> 8% of each run, Pallas kernels for 0% -> 0%
where the time goes in v1:
time: 312 us; the launch traced here: 306 us
  Pallas kernels  159 us (51%)
  matrix products  59.6 us (19%)
  other arithmetic  40.7 us (13%)
  local copies, waits for them, and re-layouts  35.4 us (11%)
  starting transfers between devices  5.6 us (2%)
  waiting for transfers between devices  5.03 us (2%)
    pallas_call x1, Pallas kernels, gather_weights(): pl.pallas_call(gather_kernel, out_shape=[jax.ShapeDtypeStruct(shape, jnp....  90.8 us
    pallas_call x1, Pallas kernels, reduce_gradients(): pl.pallas_call(reduce_kernel, out_shape=[jax.ShapeDtypeStruct(shape, jnp....  67.8 us
    dot_general x4, matrix products, contract_cols(): lax.dot_general(left, right, (((1,), (1,)), ((), ())), preferred_element_...  15.7 us
    dot_general x4, matrix products, contract_rows(): lax.dot_general(left, right, (((0,), (0,)), ((), ())), preferred_element_...  13.5 us
    unnamed x97, local copies, waits for them, and re-layouts  9.96 us
    dot_general x4, matrix products, forward_dot(): return jnp.dot(left, right, preferred_element_type=jnp.float32)  9.72 us
    dot_general x1, matrix products, body(): jnp.einsum('thd,kd->htk', d_attended, all_values, preferred_element_type=...  8.12 us
    convert_element_type x1, other arithmetic, body(): d_scores = (soft_again * (d_soft - inner_sum)).astype(jnp.bfloat16)  6.72 us
  transfers between devices with their start and end apart: 2, of which 1 were waited for; matrix products, arithmetic and copies ran while one was open for 8% of the time, Pallas kernels for 0%

profile of v1, /device:TPU:0, one launch (start us, length us, event | category | flops | bytes accessed | tf_op | source)
XLA Modules:
  0.0 306.5 jit_solution(10259444464442713942)
XLA Ops:
  0.7 4.2 %concatenate.34 = bf16[768]{0:T(1024)(128)(2,1)S(1)} concatenate(bf16[160]{0:T(256)(128)(2,1)} %param.25, bf16[160]{0:T(256)(128)(2,1)} %param.26, bf16[160]{0:T(256)(128)(2,1)} %param.27, bf16[160]{0:T(256)(128)(2,1)} %param.28, bf16[64]{0:T(256)(128)(2,1)} %param.29, bf16[64]{0:T(256)(128)(2,1)} %param.30), dimensions={0} | concatenate | bytes 3072 | tf_op jit(solution)/shard_map/concatenate | solution.py:476
  5.4 90.8 %gather_weights.1 = (bf16[4,160,1536]{2,1,0:T(8,128)(2,1)}, bf16[4,256,640]{2,1,0:T(8,128)(2,1)}, bf16[4,160,4096]{2,1,0:T(8,128)(2,1)}, bf16[4,512,640]{2,1,0:T(8,128)(2,1)}, f32[4,8,128]{2,1,0:T(8,128)}) custom-call(bf16[160,1024]{1,0:T(8,128)(2,1)} %refs_0_.1, bf16[160,256]{1,0:T(8,128)(2,1)} %refs_1_.1, bf16[160,256]{1,0:T(8,128)(2,1)} %refs_2_.1, ...), custom_call_target="tpu_custom_call" | custom-call | tf_op jit(solution)/shard_map/gather_weights/pallas_call | solution.py:403
  96.2 0.7 copy.147
  97.4 3.2 %fusion.52 = f32[512,1536]{1,0:T(8,128)S(1)} fusion(bf16[640,1536]{1,0:T(8,128)(2,1)} %bitcast.165, bf16[1,512,640]{2,1,0:T(8,128)(2,1)} %param.16, f32[640]{0:T(1024)S(1)} %mul.499, f32[512]{0:T(512)S(1)} %fusion.68), kind=kOutput, calls=%fused_computation.100 | convolution fusion | flops 1007943680 | bytes 5771776 | tf_op jit(solution)/shard_map/dot_general | solution.py:439
  100.8 1.0 slice.212
  102.0 0.8 slice_negate_fusion.3
  102.8 1.0 multiply_cosine_fusion
  103.8 2.7 broadcast_multiply_fusion.1
  106.6 0.8 pad_maximum_fusion.8
  107.4 4.3 %collective-permute-start = (bf16[512,512]{1,0:T(8,128)(2,1)}, bf16[512,512]{1,0:T(8,128)(2,1)}, u32[]{:S(2)}, u32[]{:S(2)}) collective-permute-start(bf16[512,512]{1,0:T(8,128)(2,1)} %pad_maximum_fusion.8), channel_id=1, source_target_pairs={{0,4},{4,8},{8,12},{12,16},{16,20},{20,24},{24,28},{28,32},{32,36}... | collective-permute-start | bytes 1572872 | tf_op jit(solution)/shard_map/ppermute | solution.py:19
  111.7 1.5 slice.147
  113.2 2.2 reshape.365
  115.4 1.3 copy-done.3
  116.8 1.3 multiply_reduce_fusion.2
  118.1 2.1 copy.104
  120.5 2.1 copy.114
  122.6 2.0 copy.115
  124.6 1.0 copy.106
  125.8 1.1 copy.103
  128.2 0.8 fusion.19
  129.2 1.3 maximum_maximum_fusion
  130.5 1.5 fusion.86
  132.1 1.2 fusion.3
  133.3 3.0 copy-done
  136.3 1.5 fusion.32
  137.9 1.1 multiply_reduce_fusion.9
  139.8 3.5 %fusion.77 = f32[512,4096]{1,0:T(8,128)S(1)} fusion(bf16[640,4096]{1,0:T(8,128)(2,1)S(1)} %bitcast.151, f32[512,640]{1,0:T(8,128)S(1)} %get-tuple-element.51, f32[640]{0:T(1024)S(1)} %mul.538, f32[512]{0:T(512)S(1)} %fusion.71), kind=kOutput, calls=%fused_computation.172 | convolution fusion | flops 2685337600 | bytes 14946816 | tf_op jit(solution)/shard_map/dot_general | solution.py:439
  143.3 1.7 multiply_convert_fusion.1
  145.1 1.9 multiply_reduce_fusion.7
  147.5 1.3 fusion.44
  148.9 5.5 %fusion.11 = (bf16[512,2048]{1,0:T(8,128)(2,1)S(1)}, bf16[512,2048]{1,0:T(8,128)(2,1)}) fusion(f32[512,4096]{1,0:T(8,128)S(1)} %fusion.77, bf16[512,640]{1,0:T(8,128)(2,1)S(1)} %get-tuple-element.58, bf16[2048,640]{1,0:T(8,128)(2,1)S(1)} %bitcast.164), kind=kOutput, calls=%fused_computation.20 | convolution fusion | flops 1367343104 | bytes 15859712 | tf_op jit(solution)/shard_map/dot_general | solution.py:449
  154.4 3.4 %convolution_convert_fusion.1 = bf16[2048,640]{1,0:T(8,128)(2,1)} fusion(bf16[512,2048]{1,0:T(8,128)(2,1)S(1)} %multiply_convert_fusion.1, bf16[512,640]{1,0:T(8,128)(2,1)S(1)} %get-tuple-element.58), kind=kOutput, calls=%fused_computation.28 | convolution fusion | flops 1343488000 | bytes 5373952 | tf_op jit(solution)/shard_map/dot_general | solution.py:443
  157.8 3.5 %multiply_reduce_fusion.3 = (f32[640]{0:T(1024)S(1)}, f32[512]{0:T(512)S(1)}, f32[512,640]{1,0:T(8,128)S(1)}) fusion(f32[512,640]{1,0:T(8,128)S(1)} %get-tuple-element.51, f32[512]{0:T(512)S(1)} %fusion.71, f32[640]{0:T(1024)S(1)} %mul.538, bf16[640,4096]{1,0:T(8,128)(2,1)S(1)} %bitcast.152, bf16[512,2048]{1,0:T(8,128)(2,1)S(1)} %copy-done.28, ...), kind=kOutput, calls=%fused_computation.84 | convolution fusion | flops 2694708224 | bytes 12067840 | tf_op jit(solution)/shard_map/dot_general | solution.py:449
  161.3 0.8 multiply_reduce_fusion.4
  163.2 0.8 copy-done.36
  164.0 2.0 convolution_convert_fusion.4
  166.0 2.7 copy.141
  168.7 6.0 %fusion.33 = f32[1024,256]{1,0:T(8,128)} fusion(bf16[512,4,256]{0,2,1:T(8,128)(2,1)} %bitcast.153, f32[4,512,1024]{1,2,0:T(8,128)} %copy-done, f32[4,512]{1,0:T(4,128)S(1)} %log_add_fusion), kind=kOutput, calls=%fused_computation.69 | convolution fusion | flops 1077936128 | bytes 10493952 | tf_op jit(solution)/shard_map/htk,thd->kd/dot_general | solution.py:596
  174.6 8.1 %fusion = (f32[4,512]{1,0:T(4,128)S(1)}, f32[1024,512,4]{1,0,2:T(8,128)}) fusion(f32[4,512,1024]{1,2,0:T(8,128)} %copy-done, f32[4,512]{1,0:T(4,128)S(1)} %log_add_fusion, bf16[512,4,256]{0,2,1:T(8,128)(2,1)S(1)} %bitcast.154, bf16[1024,512]{1,0:T(8,128)(2,1)S(1)} %maximum_maximum_fusion), kind=kOutput, calls=%fused_computation.2 | convolution fusion | flops 1080031232 | bytes 18366464 | tf_op jit(solution)/shard_map/thd,kd->htk/dot_general | solution.py:585
  183.0 2.4 convolution_convert_fusion.3
  185.4 1.8 slice.210
  187.1 6.7 %fusion.2 = bf16[4,512,1024]{1,2,0:T(8,128)(2,1)S(1)} fusion(f32[1024,512,4]{1,0,2:T(8,128)} %get-tuple-element.96, f32[4,512,1024]{1,2,0:T(8,128)} %copy-done, f32[4,512]{1,0:T(4,128)S(1)} %get-tuple-element.95, f32[4,512]{1,0:T(4,128)S(1)} %log_add_fusion), kind=kLoop, calls=%fused_computation.4 | loop fusion | flops 8388608 | bytes 20987904 | tf_op jit(solution)/shard_map/convert_element_type | solution.py:587
  193.9 2.2 fusion.36
  196.1 1.3 bitcast_multiply_fusion.1
  197.7 0.8 copy-done.22
  198.5 2.0 multiply_reduce_fusion
  200.6 1.1 slice.211
  201.7 1.1 pad_maximum_fusion.9
  202.8 1.3 collective-permute-start.1
  204.1 3.4 %fusion.17 = bf16[512,4,256]{0,2,1:T(8,128)(2,1)} fusion(f32[512,4,256]{0,2,1:T(8,128)S(1)} %copy.104, f32[512,4,256]{0,2,1:T(8,128)} %get-tuple-element.47, f32[512,4]{0,1:T(4,128)S(1)} %multiply_multiply_fusion.5, f32[256]{0:T(256)S(1)} %mul.520, f32[512,4]{0,1:T(4,128)S(1)} %fusion.67), kind=kLoop, calls=%fused_computation.32 | loop fusion | flops 3145728 | bytes 5260288 | tf_op jit(solution)/shard_map/convert_element_type | solution.py:613
  207.5 5.3 %convolution_convert_fusion = bf16[640,4096]{1,0:T(8,128)(2,1)} fusion(bf16[512,2048]{1,0:T(8,128)(2,1)S(1)} %copy-done.29, bf16[512,2048]{1,0:T(8,128)(2,1)S(1)} %copy-done.27, f32[512,640]{1,0:T(8,128)S(1)} %copy-done.2, f32[640]{0:T(1024)S(1)} %mul.538, f32[512]{0:T(512)S(1)} %fusion.71), kind=kOutput, calls=%fused_computation.11 | convolution fusion | flops 2696347648 | bytes 10752512 | tf_op jit(solution)/shard_map/dot_general | solution.py:443
  212.8 5.0 %collective-permute-done.1 = bf16[512,512]{1,0:T(8,128)(2,1)S(1)} collective-permute-done((bf16[512,512]{1,0:T(8,128)(2,1)S(1)}, bf16[512,512]{1,0:T(8,128)(2,1)S(1)}, u32[]{:S(2)}, u32[]{:S(2)}) %collective-permute-start.1) | collective-permute-done | bytes 524320 | tf_op jit(solution)/shard_map/ppermute | solution.py:19
  218.1 1.4 multiply_reduce_fusion.10
  219.6 1.3 fusion.60
  221.9 4.7 %fusion.39 = (f32[640]{0:T(1024)S(1)}, f32[512]{0:T(512)S(1)}, f32[512,640]{1,0:T(8,128)}) fusion(bf16[1,512,640]{2,1,0:T(8,128)(2,1)S(1)} %copy-done.10, f32[512]{0:T(512)S(1)} %fusion.68, f32[640]{0:T(1024)S(1)} %mul.499, bf16[640,1536]{1,0:T(8,128)(2,1)} %bitcast.166, bf16[512,256]{0,1:T(8,128)(2,1)S(1)} %copy.125, bf16[512,256]{0,1:T(8,128)(2,1)S(1)} %copy.124, ...), kind=kOutput, calls=%fused_computation.74 | convolution fusion | flops 1013644160 | bytes 5514240 | tf_op jit(solution)/shard_map/dot_general | solution.py:449
  226.6 2.5 convolution_convert_fusion.2
  229.3 67.8 %reduce_gradients.1 = (bf16[512,640]{1,0:T(8,128)(2,1)S(1)}, bf16[160,4096]{1,0:T(8,128)(2,1)S(1)}, bf16[256,640]{1,0:T(8,128)(2,1)S(1)}, bf16[160,1536]{1,0:T(8,128)(2,1)S(1)}, f32[8,128]{1,0:T(8,128)S(1)}) custom-call(bf16[2,2,512,640]{3,2,1,0:T(8,128)(2,1)} %bitcast.155, bf16[2,2,160,4096]{3,2,1,0:T(8,128)(2,1)} %bitcast.148, ...), custom_call_target="tpu_custom_call" | custom-call | tf_op jit(solution)/shard_map/reduce_gradients/pallas_call | solution.py:294
  298.4 0.7 slice_convert_fusion.6
  299.1 0.9 slice_convert_fusion.5
  300.0 0.9 convert_element_type.172
  300.9 1.1 convert_element_type.175
  302.0 1.8 slice_convert_fusion
  304.2 0.7 copy-done.32
  304.9 1.4 fusion.47
  (144 shorter events, 9.6 us)
Async XLA Ops:
  0.6 96.4 %copy-start.8 = (bf16[1,512,640]{2,1,0:T(8,128)(2,1)S(1)}, bf16[1,512,640]{2,1,0:T(8,128)(2,1)}, u32[]{:S(2)}) copy-start(bf16[1,512,640]{2,1,0:T(8,128)(2,1)} %param.16) | copy-start | bytes 1966084
  100.6 11.1 %copy-start.6 = (f32[512,1536]{1,0:T(8,128)}, f32[512,1536]{1,0:T(8,128)S(1)}, u32[]{:S(2)}) copy-start(f32[512,1536]{1,0:T(8,128)S(1)} %fusion.52) | copy-start | bytes 9437188
  100.6 2.2 copy-start.40
  103.8 3.6 %copy-start.16 = (f32[512,128]{1,0:T(8,128)}, f32[512,128]{1,0:T(8,128)S(1)}, u32[]{:S(2)}) copy-start(f32[512,128]{1,0:T(8,128)S(1)} %get-tuple-element.86) | copy-start | bytes 786436
  103.8 3.6 %copy-start.18 = (f32[512,128]{1,0:T(8,128)}, f32[512,128]{1,0:T(8,128)S(1)}, u32[]{:S(2)}) copy-start(f32[512,128]{1,0:T(8,128)S(1)} %get-tuple-element.87) | copy-start | bytes 786436
  103.8 2.7 copy-start.20
  107.4 21.6 %collective-permute-start = (bf16[512,512]{1,0:T(8,128)(2,1)}, bf16[512,512]{1,0:T(8,128)(2,1)}, u32[]{:S(2)}, u32[]{:S(2)}) collective-permute-start(bf16[512,512]{1,0:T(8,128)(2,1)} %pad_maximum_fusion.8), channel_id=1, source_target_pairs={{0,4},{4,8},{8,12},{12,16},{16,20},{20,24},{24,28},{28,32},{32,36}... | collective-permute-start | bytes 1572872 | tf_op jit(solution)/shard_map/ppermute | solution.py:19
  115.4 1.3 copy-start.3
  120.2 4.5 %copy-start.25 = (f32[512,256]{1,0:T(8,128)S(1)}, f32[512,256]{1,0:T(8,128)}, u32[]{:S(2)}) copy-start(f32[512,256]{1,0:T(8,128)} %get-tuple-element.72) | copy-start | bytes 1572868
  120.2 5.4 %copy-start.24 = (f32[512,256]{1,0:T(8,128)S(1)}, f32[512,256]{1,0:T(8,128)}, u32[]{:S(2)}) copy-start(f32[512,256]{1,0:T(8,128)} %get-tuple-element.73) | copy-start | bytes 1572868
  127.2 1.0 copy-start.30
  128.2 0.9 copy-start.21
  129.0 3.1 %copy-start.33 = (bf16[512,4,256]{0,2,1:T(8,128)(2,1)}, bf16[512,4,256]{0,2,1:T(8,128)(2,1)S(1)}, u32[]{:S(2)}) copy-start(bf16[512,4,256]{0,2,1:T(8,128)(2,1)S(1)} %fusion.19) | copy-start | bytes 3145732
  130.5 44.1 %copy-start.13 = (bf16[1024,512]{1,0:T(8,128)(2,1)}, bf16[1024,512]{1,0:T(8,128)(2,1)S(1)}, u32[]{:S(2)}) copy-start(bf16[1024,512]{1,0:T(8,128)(2,1)S(1)} %maximum_maximum_fusion) | copy-start | bytes 3145732
  132.1 4.3 %copy-start = (f32[4,512,1024]{1,2,0:T(8,128)}, f32[4,512,1024]{1,2,0:T(8,128)S(1)}, u32[]{:S(2)}) copy-start(f32[4,512,1024]{1,2,0:T(8,128)S(1)} %get-tuple-element.89) | copy-start | bytes 25165828
  132.1 7.7 %slice-start = ((s8[5242880]{0:T(1024)(128)(4,1)}), s8[4194304]{0:T(1024)(128)(4,1)S(1)}, s32[]{:S(2)}) async-start(s8[5242880]{0:T(1024)(128)(4,1)} %bitcast.149), calls=%async_computation | async-start | bytes 8388608
  136.3 1.5 copy-start.42
  136.3 3.5 %slice-start.1 = ((s8[5242880]{0:T(1024)(128)(4,1)}), s8[1048576]{0:T(1024)(128)(4,1)S(1)}, s32[]{:S(2)}) async-start(s8[5242880]{0:T(1024)(128)(4,1)} %bitcast.149), calls=%async_computation.1 | async-start | bytes 2097152
  137.9 1.1 copy-start.44
  137.9 1.5 copy-start.9
  139.8 21.6 %copy-start.1 = (f32[512,640]{1,0:T(8,128)}, f32[512,640]{1,0:T(8,128)S(1)}, u32[]{:S(2)}) copy-start(f32[512,640]{1,0:T(8,128)S(1)} %get-tuple-element.51) | copy-start | bytes 3932164
  143.3 1.7 copy-start.41
  145.1 1.9 copy-start.7
  154.4 3.4 %copy-start.26 = (bf16[512,2048]{1,0:T(8,128)(2,1)}, bf16[512,2048]{1,0:T(8,128)(2,1)S(1)}, u32[]{:S(2)}) copy-start(bf16[512,2048]{1,0:T(8,128)(2,1)S(1)} %get-tuple-element.52) | copy-start | bytes 6291460
  154.4 3.4 %copy-start.28 = (bf16[512,2048]{1,0:T(8,128)(2,1)S(1)}, bf16[512,2048]{1,0:T(8,128)(2,1)}, u32[]{:S(2)}) copy-start(bf16[512,2048]{1,0:T(8,128)(2,1)} %get-tuple-element.53) | copy-start | bytes 6291460
  162.1 1.1 copy-start.4
  162.1 1.9 copy-start.43
  163.2 0.8 copy-start.36
  168.6 6.0 %copy-start.15 = (bf16[512,1024]{0,1:T(8,128)(2,1)S(1)}, bf16[512,1024]{0,1:T(8,128)(2,1)}, u32[]{:S(2)}) copy-start(bf16[512,1024]{0,1:T(8,128)(2,1)} %copy.141) | copy-start | bytes 3145732
  187.1 6.7 %copy-start.34 = (bf16[512,4,256]{0,2,1:T(8,128)(2,1)S(1)}, bf16[512,4,256]{0,2,1:T(8,128)(2,1)}, u32[]{:S(2)}) copy-start(bf16[512,4,256]{0,2,1:T(8,128)(2,1)} %copy-done.33) | copy-start | bytes 3145732
  193.9 2.3 copy-start.14
  193.9 2.3 copy-start.23
  197.4 1.0 copy-start.22
  201.6 5.8 %copy-start.29 = (bf16[512,2048]{1,0:T(8,128)(2,1)S(1)}, bf16[512,2048]{1,0:T(8,128)(2,1)}, u32[]{:S(2)}) copy-start(bf16[512,2048]{1,0:T(8,128)(2,1)} %get-tuple-element.53) | copy-start | bytes 6291460
  202.8 15.0 %collective-permute-start.1 = (bf16[512,512]{1,0:T(8,128)(2,1)S(1)}, bf16[512,512]{1,0:T(8,128)(2,1)S(1)}, u32[]{:S(2)}, u32[]{:S(2)}) collective-permute-start(bf16[512,512]{1,0:T(8,128)(2,1)S(1)} %pad_maximum_fusion.9), channel_id=1, source_target_pairs={{4,0},{8,4},{12,8},{16,12},{20,16},{24,20},{28,24},{32,28},{36,32}... | collective-permute-start | bytes 1572872 | tf_op jit(solution)/shard_map/ppermute | solution.py:19
  204.1 3.4 %copy-start.2 = (f32[512,640]{1,0:T(8,128)S(1)}, f32[512,640]{1,0:T(8,128)}, u32[]{:S(2)}) copy-start(f32[512,640]{1,0:T(8,128)} %copy-done.1) | copy-start | bytes 3932164
  204.1 3.4 %copy-start.27 = (bf16[512,2048]{1,0:T(8,128)(2,1)S(1)}, bf16[512,2048]{1,0:T(8,128)(2,1)}, u32[]{:S(2)}) copy-start(bf16[512,2048]{1,0:T(8,128)(2,1)} %copy-done.26) | copy-start | bytes 6291460
  207.5 10.4 %copy-start.19 = (f32[512,128]{1,0:T(8,128)S(1)}, f32[512,128]{1,0:T(8,128)}, u32[]{:S(2)}) copy-start(f32[512,128]{1,0:T(8,128)} %copy-done.18) | copy-start | bytes 786436
  207.5 10.4 %copy-start.31 = (f32[1024,256]{1,0:T(8,128)S(1)}, f32[1024,256]{1,0:T(8,128)}, u32[]{:S(2)}) copy-start(f32[1024,256]{1,0:T(8,128)} %fusion.36) | copy-start | bytes 3145732
  212.8 5.4 %copy-start.17 = (f32[512,128]{1,0:T(8,128)S(1)}, f32[512,128]{1,0:T(8,128)}, u32[]{:S(2)}) copy-start(f32[512,128]{1,0:T(8,128)} %copy-done.16) | copy-start | bytes 786436
  212.8 5.4 %copy-start.37 = (f32[1024,256]{1,0:T(8,128)S(1)}, f32[1024,256]{1,0:T(8,128)}, u32[]{:S(2)}) copy-start(f32[1024,256]{1,0:T(8,128)} %fusion.33) | copy-start | bytes 3145732
  219.5 2.4 copy-start.10
  221.0 0.7 copy-start.38
  221.2 0.7 copy-start.39
  221.9 4.7 %copy-start.11 = (bf16[1,512,640]{2,1,0:T(8,128)(2,1)S(1)}, bf16[1,512,640]{2,1,0:T(8,128)(2,1)}, u32[]{:S(2)}) copy-start(bf16[1,512,640]{2,1,0:T(8,128)(2,1)} %param.16) | copy-start | bytes 1966084
  221.9 4.7 %copy-start.35 = (bf16[512,4,256]{0,2,1:T(8,128)(2,1)S(1)}, bf16[512,4,256]{0,2,1:T(8,128)(2,1)}, u32[]{:S(2)}) copy-start(bf16[512,4,256]{0,2,1:T(8,128)(2,1)} %fusion.17) | copy-start | bytes 3145732
  302.0 1.8 copy-start.5
  302.0 2.1 copy-start.12
  302.0 2.9 copy-start.32

commit v2 on v1

v2 whole, which is shorter than its diff:
```python
import jax
import jax.numpy as jnp
from jax import lax
from jax.experimental import pallas as pl
from jax.experimental.pallas import tpu as pltpu
from jax.sharding import PartitionSpec as P

epsilon = 1e-06
rope_base = 10000.0


MESH = pl.DeviceIdType.MESH
DIMS = ("C", "X1", "X0", "Y1", "Y0", "Z1", "Z0")


def place():
    return lax.axis_index("seq"), lax.axis_index("fsdp")


def bit_of(dim, s, f):
    if dim == "C":
        return lax.rem(f, 2)
    if dim == "X1":
        return lax.div(f, 2)
    if dim == "X0":
        return lax.rem(lax.rem(lax.div(s, 4), 2) + lax.div(f, 2), 2)
    at = lax.rem(s, 4) if dim[0] == "Y" else lax.div(s, 8)
    if dim[1] == "1":
        return lax.div(at, 2)
    return lax.rem(lax.rem(at, 2) + lax.div(at, 2), 2)


def partner(dim, s, f):
    if dim == "C":
        return (s, f + 1 - 2 * lax.rem(f, 2))
    step = 1 - 2 * lax.rem(lax.div(s, 4), 2)
    if dim == "X0":
        return (s + 4 * step, f)
    if dim == "X1":
        return (s + 4 * step, f + 2 - 4 * lax.div(f, 2))
    at, scale = (lax.rem(s, 4), 1) if dim[0] == "Y" else (lax.div(s, 8), 8)
    if dim[1] == "1":
        return (s + scale * (3 - 2 * at), f)
    return (s + scale * (1 - 2 * lax.rem(at, 2)), f)


def greet(s, f):
    barrier = pltpu.get_barrier_semaphore()
    for dim in DIMS:
        pl.semaphore_signal(barrier, inc=1, device_id=partner(dim, s, f), device_id_type=MESH)
    pl.semaphore_wait(barrier, len(DIMS))


def span(start, size, tile):
    if isinstance(start, int):
        return pl.ds(start, size)
    return pl.ds(pl.multiple_of(start, tile), size)


class Region:
    def __init__(self, q, r, c):
        self.q, self.r, self.c = q, r, c

    def of(self, ref):
        return ref.at[pl.ds(*self.q), span(*self.r, 16), span(*self.c, 128)]

    def flat(self, ref, r0=0, c0=0):
        return ref.at[span(self.r[0] + r0, self.r[1], 16), span(self.c[0] + c0, self.c[1], 128)]

    def halved(self, axis, bit):
        start, size = getattr(self, axis)
        half = size // 2
        mine = Region(self.q, self.r, self.c)
        setattr(mine, axis, (start + bit * half, half))
        theirs = Region(self.q, self.r, self.c)
        setattr(theirs, axis, (start + (1 - bit) * half, half))
        return mine, theirs

    @property
    def shape(self):
        return (self.q[1], self.r[1], self.c[1])


def rows_per_step(rows, cols):
    best = 16
    for n in (32, 48, 64, 80, 96, 128, 160):
        if rows % n == 0 and n * cols <= 48 * 2048:
            best = n
    return best


def add_blocks(out, first, second, shape):
    quarters, rows, cols = shape
    step = rows_per_step(rows, cols)
    for q in range(quarters):

        def body(i, carry, q=q):
            at = i * step
            ref, index = out(q, at, step)
            ref_a, index_a = first(q, at, step)
            ref_b, index_b = second(q, at, step)
            ref[index] = ref_a[index_a] + ref_b[index_b]
            return carry

        lax.fori_loop(0, rows // step, body, 0)


def view(ref, region):
    def pick(q, at, step):
        rows = span(region.r[0] + at, step, 16)
        return ref, (region.q[0] + q, rows, span(region.c[0], region.c[1], 128))

    return pick


def flat_view(ref, region, r0, c0):
    def pick(q, at, step):
        return ref, (span(region.r[0] + r0 + at, step, 16), span(region.c[0] + c0, region.c[1], 128))

    return pick


def whole_view(ref):
    def pick(q, at, step):
        return ref, (q, span(at, step, 16), slice(None))

    return pick


ORDERS = (
    ("X1", "Y1", "Z1", "X0", "Y0", "Z0"),
    ("Y1", "Z1", "X0", "X1", "Y0", "Z0"),
    ("Z1", "X0", "Y0", "X1", "Z0", "Y1"),
    ("X0", "Y0", "Z0", "X1", "Y1", "Z1"),
    ("Y0", "Z0", "X1", "Y1", "Z1", "X0"),
    ("Z0", "X1", "Y1", "Z1", "X0", "Y0"),
)
PARTS = (
    (0, 0, 384, 0, 640, ORDERS[0], "rrr"),
    (1, 0, 160, 0, 1536, ORDERS[1], "ccr"),
    (1, 0, 160, 1536, 1536, ORDERS[2], "ccr"),
    (1, 0, 160, 3072, 1024, ORDERS[3], "ccc"),
    (0, 384, 128, 0, 640, ORDERS[3], "rrr"),
    (2, 0, 256, 0, 640, ORDERS[4], "rrr"),
    (3, 0, 160, 0, 1536, ORDERS[5], "ccr"),
)
SHARES = ((512, 640), (160, 4096), (256, 640), (160, 1536))


def part_shapes(part):
    _, _, rows, _, cols, order, splits = part
    shapes, shape, cut = [], [2, rows, cols], iter(splits)
    for dim in order[:4]:
        axis = 0 if dim == "X1" else {"r": 1, "c": 2}[next(cut)]
        shape[axis] //= 2
        shapes.append(tuple(shape))
    return shapes


def reduce_kernel(*refs):
    n = len(SHARES)
    grads, gains = refs[:n], refs[n]
    totals, gain_total = refs[n + 1 : 2 * n + 1], refs[2 * n + 1]
    scratch = list(refs[2 * n + 2 :])
    acc, from_core, inbox, extra = [], [], [], []
    for _ in PARTS:
        acc.append(scratch.pop(0))
        from_core.append(scratch.pop(0))
        inbox.append([scratch.pop(0) for _ in range(4)])
        extra.append([scratch.pop(0) for _ in range(3)])
    gain_in, gain_sum, send_sem, recv_sem, local_sem = scratch

    s, f = place()
    greet(s, f)
    pending, count = [], [0]

    def send(src, dst, dim):
        copy = pltpu.make_async_remote_copy(
            src_ref=src,
            dst_ref=dst,
            send_sem=send_sem.at[count[0]],
            recv_sem=recv_sem.at[count[0]],
            device_id=partner(dim, s, f),
            device_id_type=MESH,
        )
        copy.start()
        count[0] += 1
        pending.append(copy)
        return copy

    core = bit_of("C", s, f)
    flights, loads, where = [], [], []
    gain_flight = send(gains, gain_in.at[0], "C")
    for p, (tensor, r0, rows, c0, cols, order, splits) in enumerate(PARTS):
        block = (pl.ds(0, 2), pl.ds(r0, rows), pl.ds(c0, cols))
        flights.append(send(grads[tensor].at[block[0], 1 - core, block[1], block[2]], from_core[p], "C"))
        load = pltpu.make_async_copy(
            grads[tensor].at[block[0], core, block[1], block[2]], acc[p], local_sem.at[p]
        )
        load.start()
        loads.append(load)
        where.append(Region((0, 2), (0, rows), (0, cols)))
    cuts = [iter(part[6]) for part in PARTS]
    trail = [[] for _ in PARTS]

    gain_dims = ("C", "X1", "X0", "Y1", "Y0", "Z1", "Z0")

    def gain_step(step):
        gain_flight.wait_recv()
        before = gains if step == 0 else gain_sum.at[step - 1]
        gain_sum[step] = before[...] + gain_in[step]
        if step < 6:
            return send(gain_sum.at[step], gain_in.at[step + 1], gain_dims[step + 1])
        return None

    for step in range(5):
        for p, part in enumerate(PARTS):
            order = part[5]
            flights[p].wait_recv()
            if step == 0:
                loads[p].wait()
                source = whole_view(from_core[p])
            else:
                source = whole_view(inbox[p][step - 1])
            add_blocks(view(acc[p], where[p]), view(acc[p], where[p]), source, where[p].shape)
            if step == 4:
                flights[p] = send(where[p].of(acc[p]), extra[p][0], order[4])
                continue
            dim = order[step]
            axis = "q" if dim == "X1" else next(cuts[p])
            trail[p].append((dim, axis))
            where[p], theirs = where[p].halved(axis, bit_of(dim, s, f))
            flights[p] = send(theirs.of(acc[p]), inbox[p][step], dim)
        gain_flight = gain_step(step)
    for p, part in enumerate(PARTS):
        flights[p].wait_recv()
        add_blocks(whole_view(extra[p][1]), view(acc[p], where[p]), whole_view(extra[p][0]), where[p].shape)
        flights[p] = send(extra[p][1], extra[p][2], part[5][5])
    gain_flight = gain_step(5)
    back = []
    for p, part in enumerate(PARTS):
        tensor, r0, _, c0, _, _, _ = part
        flights[p].wait_recv()
        add_blocks(
            flat_view(totals[tensor], where[p], r0, c0),
            whole_view(extra[p][1]),
            whole_view(extra[p][2]),
            where[p].shape,
        )
        back.append([move for move in reversed(trail[p]) if move[1] != "q"])
        region = where[p].flat(totals[tensor], r0, c0)
        flights[p] = send(region, region, back[p][0][0])
    gain_step(6)
    for step in range(3):
        for p, part in enumerate(PARTS):
            tensor, r0, _, c0, _, _, _ = part
            dim, axis = back[p][step]
            flights[p].wait_recv()
            start, size = getattr(where[p], axis)
            setattr(where[p], axis, (start - bit_of(dim, s, f) * size, 2 * size))
            if step < 2:
                region = where[p].flat(totals[tensor], r0, c0)
                flights[p] = send(region, region, back[p][step + 1][0])
    gain_total[...] = gain_sum[6]
    for copy in pending:
        copy.wait_send()


def reduce_gradients(grads, gains):
    scratch, sends = [], 7
    for part in PARTS:
        shapes = part_shapes(part)
        scratch += [pltpu.VMEM((2, part[2], part[4]), jnp.bfloat16)] * 2
        scratch += [pltpu.VMEM(shape, jnp.bfloat16) for shape in shapes]
        scratch += [pltpu.VMEM(shapes[-1], jnp.bfloat16)] * 3
        sends += 10
    scratch += [
        pltpu.VMEM((7, 8, 640), jnp.float32),
        pltpu.VMEM((7, 8, 640), jnp.float32),
        pltpu.SemaphoreType.DMA((sends,)),
        pltpu.SemaphoreType.DMA((sends,)),
        pltpu.SemaphoreType.DMA((len(PARTS),)),
    ]
    return pl.pallas_call(
        reduce_kernel,
        out_shape=[jax.ShapeDtypeStruct(shape, jnp.bfloat16) for shape in SHARES]
        + [jax.ShapeDtypeStruct((8, 640), jnp.float32)],
        in_specs=[pl.BlockSpec(memory_space=pl.ANY)] * len(SHARES)
        + [pl.BlockSpec(memory_space=pltpu.VMEM)],
        out_specs=[pl.BlockSpec(memory_space=pltpu.VMEM)] * (len(SHARES) + 1),
        scratch_shapes=scratch,
        compiler_params=pltpu.CompilerParams(
            collective_id=1, has_side_effects=True, vmem_limit_bytes=48 << 20
        ),
        name="reduce_gradients",
    )(*grads, gains)


PIECES = (
    (0, 0, 0, 160, 1024, "X0", "Z0", "c"),
    (1, 0, 1024, 160, 256, "Z0", "X0", "c"),
    (2, 0, 1280, 160, 256, "Z0", "X0", "c"),
    (3, 1, 0, 256, 640, "Y0", "X0", "r"),
    (4, 2, 0, 160, 2048, "Z1", "Y1", "c"),
    (5, 2, 2048, 160, 2048, "Z0", "Y0", "c"),
    (6, 3, 0, 512, 640, "Y1", "Z1", "r"),
)
WHOLES = ((640, 1536), (1024, 640), (640, 4096), (2048, 640))


def own_gains(gain_shards, gain_own, f):
    gain_own[...] = jnp.zeros_like(gain_own)
    for i, shard in enumerate(gain_shards):
        share = shard.shape[1]
        shift = lax.broadcasted_iota(jnp.int32, (share, 4 * share), 1) - lax.broadcasted_iota(
            jnp.int32, (share, 4 * share), 0
        )
        chosen = jnp.where(shift == share * f, 1.0, 0.0).astype(jnp.bfloat16)
        row = jnp.dot(shard[...], chosen, preferred_element_type=jnp.float32)
        if i < 4:
            gain_own[i : i + 1, :] = row
        else:
            gain_own[4:5, 256 * (i - 4) : 256 * (i - 3)] = row


class Gather:
    def __init__(self, s, f, shards, outs, send_sem, recv_sem, local_sem):
        self.s, self.f, self.shards, self.outs = s, f, shards, outs
        self.send_sem, self.recv_sem, self.local_sem = send_sem, recv_sem, local_sem
        self.copies, self.count = [], 0
        self.core, high = bit_of("C", s, f), bit_of("X1", s, f)
        self.far = 2 * (1 - high) + self.core
        self.flights, self.sides, self.loads = {}, {}, {}

    def send(self, src, dst, dim):
        copy = pltpu.make_async_remote_copy(
            src_ref=src,
            dst_ref=dst,
            send_sem=self.send_sem.at[self.count],
            recv_sem=self.recv_sem.at[self.count],
            device_id=partner(dim, self.s, self.f),
            device_id_type=MESH,
        )
        copy.start()
        self.count += 1
        self.copies.append(copy)
        return copy

    def boxes(self, piece, bit_one, bit_two):
        _, _, c0, rows, cols, _, _, cut = piece
        half = rows // 2
        if cut == "c":
            quarter = ((bit_two * half, half), (bit_one * (cols // 2), cols // 2))
        else:
            quarter = ((bit_two * half + bit_one * (half // 2), half // 2), (0, cols))
        return quarter, ((bit_two * half, half), (0, cols))

    def spot(self, piece, share, box):
        (r, nr), (c, nc) = box
        return self.outs[piece[1]].at[span(r + share * piece[3], nr, 16), span(c + piece[2], nc, 128)]

    def begin(self):
        for i, piece in enumerate(PIECES):
            (r, nr), (c, nc) = quarter = self.boxes(
                piece, bit_of(piece[5], self.s, self.f), bit_of(piece[6], self.s, self.f)
            )[0]
            src = self.shards[i].at[span(r, nr, 16), span(c, nc, 128)]
            self.flights[i] = self.send(src, self.spot(piece, self.f, quarter), "X1")
        for i, piece in enumerate(PIECES):
            dst = self.spot(piece, self.f, ((0, piece[3]), (0, piece[4])))
            self.sides[i] = [self.send(self.shards[i], dst, "C")]
            self.loads[i] = pltpu.make_async_copy(self.shards[i], dst, self.local_sem.at[i])
            self.loads[i].start()

    def step(self, i, number):
        piece, s, f, far = PIECES[i], self.s, self.f, self.far
        one, two = bit_of(piece[5], s, f), bit_of(piece[6], s, f)
        quarter, half = self.boxes(piece, one, two)
        self.flights[i].wait_recv()
        if number == 0:
            here = self.spot(piece, far, quarter)
            self.flights[i] = self.send(here, here, piece[5])
        elif number == 1:
            here = self.spot(piece, far, half)
            self.flights[i] = self.send(here, here, piece[6])
            here = self.spot(piece, far, self.boxes(piece, 1 - one, two)[0])
        else:
            here = self.spot(piece, far, self.boxes(piece, one, 1 - two)[1])
        self.sides[i].append(self.send(here, here, "C"))

    def arrive(self, i):
        for copy in self.sides[i]:
            copy.wait_recv()
        self.loads[i].wait()


def gather_kernel(*refs):
    shards, gain_shards = refs[:7], refs[7:13]
    outs, gain_out = refs[13:17], refs[17]
    gain_own, gain_mid, gain_in, send_sem, recv_sem, local_sem = refs[18:]
    s, f = place()
    greet(s, f)
    gather = Gather(s, f, shards, outs, send_sem, recv_sem, local_sem)
    gather.begin()
    own_gains(gain_shards, gain_own, f)
    flight = gather.send(gain_own, gain_in.at[0], "C")
    for i in range(7):
        gather.step(i, 0)
    flight.wait_recv()
    gain_mid[...] = gain_own[...] + gain_in[0]
    flight = gather.send(gain_mid, gain_in.at[1], "X1")
    for number in (1, 2):
        for i in range(7):
            gather.step(i, number)
    flight.wait_recv()
    gain_out[...] = gain_mid[...] + gain_in[1]
    for i in range(7):
        gather.arrive(i)
    for copy in gather.copies:
        copy.wait_send()


SENDS = 7 * len(PIECES) + 2


def gather_weights(shards, gain_shards):
    return pl.pallas_call(
        gather_kernel,
        out_shape=[jax.ShapeDtypeStruct(shape, jnp.bfloat16) for shape in WHOLES]
        + [jax.ShapeDtypeStruct((8, 640), jnp.float32)],
        in_specs=[pl.BlockSpec(memory_space=pl.ANY)] * 7 + [pl.BlockSpec(memory_space=pltpu.VMEM)] * 6,
        out_specs=[pl.BlockSpec(memory_space=pltpu.VMEM)] * 5,
        scratch_shapes=[
            pltpu.VMEM((8, 640), jnp.float32),
            pltpu.VMEM((8, 640), jnp.float32),
            pltpu.VMEM((2, 8, 640), jnp.float32),
            pltpu.SemaphoreType.DMA((SENDS,)),
            pltpu.SemaphoreType.DMA((SENDS,)),
            pltpu.SemaphoreType.DMA((7,)),
        ],
        compiler_params=pltpu.CompilerParams(
            collective_id=0, has_side_effects=True, vmem_limit_bytes=24 << 20
        ),
        name="gather_weights",
    )(*shards, *gain_shards)


NT = (((1,), (1,)), ((), ()))


def dot(left, right):
    return jnp.dot(left, right, preferred_element_type=jnp.float32)


def dot_nt(left, right):
    return lax.dot_general(left, right, NT, preferred_element_type=jnp.float32)


def block(i, size):
    return pl.ds(pl.multiple_of(i * size, size), size)


def each(count, body):
    def step(i, carry):
        body(i)
        return carry

    lax.fori_loop(0, count, step, 0)


def scale_of(y):
    return lax.rsqrt(jnp.mean(y * y, -1, keepdims=True) + epsilon)


def norm_back(dz, y, r, g):
    gained = g * dz
    return r * gained - y * (r * r * r) * jnp.mean(gained * y, -1, keepdims=True)


def fold(terms):
    rows, cols = terms.shape
    return jnp.sum(terms.reshape(rows // 8, 8, cols), 0)


def turn(v, cosine, sine):
    a, b = v[:, :128], v[:, 128:]
    return jnp.concatenate([a * cosine - b * sine, b * cosine + a * sine], 1)


def turn_back(v, cosine, sine):
    a, b = v[:, :128], v[:, 128:]
    return jnp.concatenate([a * cosine + b * sine, b * cosine - a * sine], 1)


def neighbour(s, f, by):
    return (lax.rem(s + 32 + by, 32), f)


def meet(s, f):
    barrier = pltpu.get_barrier_semaphore()
    for by in (1, -1):
        pl.semaphore_signal(barrier, inc=1, device_id=neighbour(s, f, by), device_id_type=MESH)
    pl.semaphore_wait(barrier, 2)


def forward_kernel(
    x, cot, cosine, sine, doc, gains, w_qkv, w_output, w_gate_up, w_down,
    layer_out, d_hidden, d_att, queries, pair, soft, raw, normed,
    grad_down, grad_gate_up, grad_output, gain_grads,
    turned_v, att, att_t, projected, hidden, normed_two, normed_two_t,
    product, slope, level, gate, up, down, d_down, d_proj, sums, send_sem, recv_sem,
):
    s, f = place()
    meet(s, f)
    lanes = lambda i: gains[pl.ds(i, 1), :]

    def norm_in(i):
        rows = block(i, 64)
        y = x[rows, :].astype(jnp.float32)
        normed[rows, :] = (y * scale_of(y) * lanes(0)).astype(jnp.bfloat16)

    each(8, norm_in)
    pair_raw = dot(normed[...], w_qkv[:, 1024:1536])
    raw[:, 1024:1280] = pair_raw[:, :256]
    pair[512:1024, 256:512] = pair_raw[:, 256:].astype(jnp.bfloat16)

    def shape_key(i):
        rows = block(i, 128)
        y = raw[rows, 1024:1280]
        y = turn(y * scale_of(y) * gains[pl.ds(4, 1), 256:512], cosine[rows, :], sine[rows, :])
        pair[pl.ds(pl.multiple_of(512 + i * 128, 128), 128), 0:256] = y.astype(jnp.bfloat16)

    each(4, shape_key)
    pass_on = pltpu.make_async_remote_copy(
        src_ref=pair.at[pl.ds(512, 512), :],
        dst_ref=pair.at[pl.ds(0, 512), :],
        send_sem=send_sem,
        recv_sem=recv_sem,
        device_id=neighbour(s, f, 1),
        device_id_type=MESH,
    )
    pass_on.start()

    def shape_query(h):
        raw[:, block(h, 256)] = dot(normed[...], w_qkv[:, block(h, 256)])

        def rows_of(i):
            rows = block(i, 128)
            y = raw[rows, block(h, 256)]
            y = turn(y * scale_of(y) * gains[pl.ds(4, 1), 0:256], cosine[rows, :], sine[rows, :])
            at = pl.ds(pl.multiple_of(h * 256 + lax.rem(i, 2) * 128, 128), 128)
            queries[lax.div(i, 2), at, :] = (y * 0.0625).astype(jnp.bfloat16)

        each(4, rows_of)

    each(4, shape_query)
    pass_on.wait_recv()
    turned_v[...] = pair[:, 256:512].T

    def attend(n):
        i, h = lax.div(n, 4), lax.rem(n, 4)
        keys = pl.ds(pl.multiple_of(i * 256, 256), 768)
        own = block(i, 256)
        gate[0:384, :] = dot_nt(pair[pl.ds(pl.multiple_of(i * 256, 256), 384), 0:256], queries[i, block(h, 256), :])
        gate[384:768, :] = dot_nt(
            pair[pl.ds(pl.multiple_of(i * 256 + 384, 128), 384), 0:256], queries[i, block(h, 256), :]
        )
        row = lax.broadcasted_iota(jnp.int32, (1, 256), 1) + i * 256
        lowest = jnp.maximum(row + 1, doc[0:1, own] - (s - 1) * 512)

        def weigh(c, total):
            rows = block(c, 128)
            key = lax.broadcasted_iota(jnp.int32, (128, 256), 0) + (i * 256 + c * 128)
            seen = (key >= lowest) & (key <= row + 512)
            p = jnp.where(seen, jnp.exp(gate[rows, :]), 0.0)
            gate[rows, :] = p
            return total + fold(p)

        total = lax.fori_loop(0, 6, weigh, jnp.zeros((8, 256), jnp.float32))
        inverse = 1.0 / jnp.sum(total, 0, keepdims=True)

        def settle(c):
            rows = block(c, 128)
            soft[i, rows, block(h, 256)] = (gate[rows, :] * inverse).astype(jnp.bfloat16)

        each(6, settle)
        mixed = dot(turned_v[:, keys], soft[i, :, block(h, 256)])
        att_t[block(h, 256), own] = mixed.astype(jnp.bfloat16)
        att[own, block(h, 256)] = mixed.T.astype(jnp.bfloat16)

    each(8, attend)
    projected[...] = dot(att[...], w_output[...])

    def mid(i):
        rows = block(i, 64)
        y = projected[rows, :]
        z = x[rows, :].astype(jnp.float32) + y * scale_of(y) * lanes(1)
        hidden[rows, :] = z
        normed_two[rows, :] = (z * scale_of(z) * lanes(2)).astype(jnp.bfloat16)

    each(8, mid)
    normed_two_t[...] = normed_two[...].T

    def feed(j):
        cols = block(j, 256)
        gate[0:512, :] = dot(normed_two[...], w_gate_up[:, cols])
        up[...] = dot(normed_two[...], w_gate_up[:, pl.ds(pl.multiple_of(2048 + j * 256, 256), 256)])

        def bend(i):
            rows = block(i, 64)
            g, u = gate[rows, :], up[rows, :]
            square = g * g
            t = jnp.tanh(0.7978845608028654 * g * (1.0 + 0.044715 * square))
            half = 0.5 * (1.0 + t)
            gelu = g * half
            rise = half + 0.5 * g * (1.0 - t * t) * (0.7978845608028654 * (1.0 + 0.134145 * square))
            product[rows, cols] = (gelu * u).astype(jnp.bfloat16)
            slope[rows, cols] = (rise * u).astype(jnp.bfloat16)
            level[rows, cols] = gelu.astype(jnp.bfloat16)

        each(8, bend)

    each(8, feed)
    down[...] = dot(product[...], w_down[...])
    sums[...] = jnp.zeros_like(sums)

    def end(i):
        rows = block(i, 64)
        y, dz = down[rows, :], cot[rows, :].astype(jnp.float32)
        r = scale_of(y)
        layer_out[rows, :] = (hidden[rows, :] + y * r * lanes(3)).astype(jnp.bfloat16)
        d_down[rows, :] = norm_back(dz, y, r, lanes(3)).astype(jnp.bfloat16)
        sums[2] += fold(dz * y * r)

    each(8, end)

    def feed_back(j):
        cols = block(j, 256)
        gate[0:512, :] = dot_nt(d_down[...], w_down[cols, :])
        grad_down[cols, :] = dot(product[:, cols].T, d_down[...]).astype(jnp.bfloat16)

        def bend(i):
            rows = block(i, 128)
            d = gate[rows, :]
            slope[rows, cols] = (d * slope[rows, cols].astype(jnp.float32)).astype(jnp.bfloat16)
            level[rows, cols] = (d * level[rows, cols].astype(jnp.float32)).astype(jnp.bfloat16)

        each(4, bend)
        grad_gate_up[:, cols] = dot(normed_two_t[...], slope[:, cols]).astype(jnp.bfloat16)
        grad_gate_up[:, pl.ds(pl.multiple_of(2048 + j * 256, 256), 256)] = dot(
            normed_two_t[...], level[:, cols]
        ).astype(jnp.bfloat16)

    each(8, feed_back)
    down[...] = dot_nt(slope[...], w_gate_up[:, 0:2048])
    down[...] += dot_nt(level[...], w_gate_up[:, 2048:4096])

    def mid_back(i):
        rows = block(i, 64)
        dz, y = down[rows, :], hidden[rows, :]
        r = scale_of(y)
        total = cot[rows, :].astype(jnp.float32) + norm_back(dz, y, r, lanes(2))
        sums[1] += fold(dz * y * r)
        d_hidden[rows, :] = total
        y = projected[rows, :]
        r = scale_of(y)
        d_proj[rows, :] = norm_back(total, y, r, lanes(1)).astype(jnp.bfloat16)
        sums[0] += fold(total * y * r)

    each(8, mid_back)

    def attend_back(h):
        grad_output[block(h, 256), :] = dot(att_t[block(h, 256), :], d_proj[...]).astype(jnp.bfloat16)
        back = dot_nt(d_proj[...], w_output[block(h, 256), :]).astype(jnp.bfloat16)
        d_att[0, block(h, 256), :] = back[:256, :]
        d_att[1, block(h, 256), :] = back[256:, :]

    each(4, attend_back)
    gain_grads[...] = jnp.zeros_like(gain_grads)
    for i in range(3):
        gain_grads[pl.ds(i + 1, 1), :] = jnp.sum(sums[i], 0, keepdims=True)
    pass_on.wait_send()


def forward(x, cot, cosine, sine, doc, gains, w_qkv, w_output, w_gate_up, w_down):
    b, f32 = jnp.bfloat16, jnp.float32
    outs = [
        ((512, 640), b), ((512, 640), f32), ((2, 1024, 256), b), ((2, 1024, 256), b), ((1024, 512), b),
        ((2, 768, 1024), b), ((512, 1280), f32), ((512, 640), b),
        ((2048, 640), b), ((640, 4096), b), ((1024, 640), b), ((8, 640), f32),
    ]
    scratch = [
        ((256, 1024), b), ((512, 1024), b), ((1024, 512), b), ((512, 640), f32), ((512, 640), f32),
        ((512, 640), b), ((640, 512), b), ((512, 2048), b), ((512, 2048), b), ((512, 2048), b),
        ((768, 256), f32), ((512, 256), f32), ((512, 640), f32), ((512, 640), b), ((512, 640), b),
        ((3, 8, 640), f32),
    ]
    return pl.pallas_call(
        forward_kernel,
        out_shape=[jax.ShapeDtypeStruct(*o) for o in outs],
        in_specs=[pl.BlockSpec(memory_space=pltpu.VMEM)] * 10,
        out_specs=[pl.BlockSpec(memory_space=pltpu.VMEM)] * len(outs),
        scratch_shapes=[pltpu.VMEM(*o) for o in scratch] + [pltpu.SemaphoreType.DMA] * 2,
        compiler_params=pltpu.CompilerParams(
            collective_id=2, has_side_effects=True, vmem_limit_bytes=60 << 20
        ),
        name="forward",
    )(x, cot, cosine, sine, doc, gains, w_qkv, w_output, w_gate_up, w_down)


def backward_kernel(
    x, d_hidden, cosine, sine, gains, w_qkv, d_att, queries, pair, soft, raw, normed, gain_grads,
    input_grad, grad_qkv, gain_sums,
    turned_k, d_soft, d_scores, d_queries, d_pair, first, other, d_raw, normed_t, d_normed,
    sums, head_sums, send_sem, recv_sem,
):
    s, f = place()
    meet(s, f)
    turned_k[...] = pair[:, 0:256].T
    d_pair[...] = jnp.zeros_like(d_pair)
    sums[...] = jnp.zeros_like(sums)
    head_sums[...] = jnp.zeros_like(head_sums)

    def attend_back(i):
        keys = pl.ds(pl.multiple_of(i * 256, 256), 768)

        def one_head(h):
            cols = block(h, 256)
            d_soft[0:384, :] = dot_nt(pair[pl.ds(pl.multiple_of(i * 256, 256), 384), 256:512], d_att[i, cols, :])
            d_soft[384:768, :] = dot_nt(
                pair[pl.ds(pl.multiple_of(i * 256 + 384, 128), 384), 256:512], d_att[i, cols, :]
            )

            def weigh(c, total):
                rows = block(c, 128)
                p = soft[i, rows, cols].astype(jnp.float32) * d_soft[rows, :]
                return total + fold(p)

            total = lax.fori_loop(0, 6, weigh, jnp.zeros((8, 256), jnp.float32))
            inner = jnp.sum(total, 0, keepdims=True)

            def settle(c):
                rows = block(c, 128)
                p = soft[i, rows, cols].astype(jnp.float32)
                d_scores[rows, cols] = (p * (d_soft[rows, :] - inner)).astype(jnp.bfloat16)

            each(6, settle)
            mixed = dot(turned_k[:, keys], d_scores[:, cols]) * 0.0625
            d_queries[block(i, 256), cols] = mixed.T

        each(4, one_head)
        for half in range(2):
            at = pl.ds(pl.multiple_of(i * 256 + half * 384, 128), 384)
            part = pl.ds(half * 384, 384)
            d_pair[at, 0:256] += dot(d_scores[part, :], queries[i])
            d_pair[at, 256:512] += dot(soft[i, part, :], d_att[i])

    each(2, attend_back)
    first[...] = d_pair[0:512, :].astype(jnp.bfloat16)
    pass_back = pltpu.make_async_remote_copy(
        src_ref=first,
        dst_ref=other,
        send_sem=send_sem,
        recv_sem=recv_sem,
        device_id=neighbour(s, f, -1),
        device_id_type=MESH,
    )
    pass_back.start()
    normed_t[...] = normed[...].T

    def query_back(n):
        h, i = lax.div(n, 4), lax.rem(n, 4)
        rows, cols = block(i, 128), block(h, 256)
        dz = turn_back(d_queries[rows, cols], cosine[rows, :], sine[rows, :])
        y = raw[rows, cols]
        r = scale_of(y)
        d_raw[rows, cols] = norm_back(dz, y, r, gains[pl.ds(4, 1), 0:256]).astype(jnp.bfloat16)
        head_sums[0] += fold(dz * y * r)

    each(16, query_back)
    pass_back.wait_recv()

    def key_back(i):
        rows = block(i, 128)
        own = pl.ds(pl.multiple_of(512 + i * 128, 128), 128)
        dz = d_pair[own, 0:256] + other[rows, 0:256].astype(jnp.float32)
        dz = turn_back(dz, cosine[rows, :], sine[rows, :])
        y = raw[rows, 1024:1280]
        r = scale_of(y)
        d_raw[rows, 1024:1280] = norm_back(dz, y, r, gains[pl.ds(4, 1), 256:512]).astype(jnp.bfloat16)
        head_sums[1] += fold(dz * y * r)
        d_value = d_pair[own, 256:512] + other[rows, 256:512].astype(jnp.float32)
        d_raw[rows, 1280:1536] = d_value.astype(jnp.bfloat16)

    each(4, key_back)

    def weigh_in(j):
        cols = block(j, 256)
        grad_qkv[:, cols] = dot(normed_t[...], d_raw[:, cols]).astype(jnp.bfloat16)

    each(6, weigh_in)
    d_normed[...] = dot_nt(d_raw[...], w_qkv[...])

    def norm_in_back(i):
        rows = block(i, 64)
        y, dz = x[rows, :].astype(jnp.float32), d_normed[rows, :]
        r = scale_of(y)
        input_grad[rows, :] = d_hidden[rows, :] + norm_back(dz, y, r, lanes_in)
        sums[...] += fold(dz * y * r)

    lanes_in = gains[pl.ds(0, 1), :]
    each(8, norm_in_back)
    gain_sums[...] = gain_grads[...]
    gain_sums[pl.ds(0, 1), :] = jnp.sum(sums[...], 0, keepdims=True)
    gain_sums[pl.ds(4, 1), 0:256] = jnp.sum(head_sums[0], 0, keepdims=True)
    gain_sums[pl.ds(4, 1), 256:512] = jnp.sum(head_sums[1], 0, keepdims=True)
    pass_back.wait_send()


def backward(*args):
    b, f32 = jnp.bfloat16, jnp.float32
    outs = [((512, 640), f32), ((640, 1536), b), ((8, 640), f32)]
    scratch = [
        ((256, 1024), b), ((768, 256), f32), ((768, 1024), b), ((512, 1024), f32), ((1024, 512), f32),
        ((512, 512), b), ((512, 512), b), ((512, 1536), b), ((640, 512), b), ((512, 640), f32),
        ((8, 640), f32), ((2, 8, 256), f32),
    ]
    return pl.pallas_call(
        backward_kernel,
        out_shape=[jax.ShapeDtypeStruct(*o) for o in outs],
        in_specs=[pl.BlockSpec(memory_space=pltpu.VMEM)] * len(args),
        out_specs=[pl.BlockSpec(memory_space=pltpu.VMEM)] * len(outs),
        scratch_shapes=[pltpu.VMEM(*o) for o in scratch] + [pltpu.SemaphoreType.DMA] * 2,
        compiler_params=pltpu.CompilerParams(
            collective_id=3, has_side_effects=True, vmem_limit_bytes=60 << 20
        ),
        name="backward",
    )(*args)


def rope_tables(positions):
    frequency = rope_base ** (-(jnp.arange(128, dtype=jnp.float32) * (2.0 / 256)))
    angles = positions[:, None] * frequency[None, :]
    return jnp.cos(angles), jnp.sin(angles)


def body(
    inputs,
    doc_start,
    w_query,
    w_key,
    w_value,
    w_output,
    w_gate,
    w_up,
    w_down,
    norm_attn_in,
    norm_attn_out,
    norm_ffn_in,
    norm_ffn_out,
    norm_query,
    norm_key,
    cotangent,
):
    row_index = lax.axis_index("seq") * 512 + jnp.arange(512, dtype=jnp.int32)
    cosine, sine = rope_tables((row_index - doc_start[0]).astype(jnp.float32))
    w_qkv, w_out, w_gate_up, w_dn, gains = gather_weights(
        (w_query, w_key, w_value, w_output, w_gate, w_up, w_down),
        [
            g.reshape(1, -1)
            for g in (norm_attn_in, norm_attn_out, norm_ffn_in, norm_ffn_out, norm_query, norm_key)
        ],
    )
    (
        layer_out, d_hidden, d_att, queries, pair, soft, raw, normed,
        grad_down, grad_gate_up, grad_output, gain_grads,
    ) = forward(
        inputs[0], cotangent[0], cosine, sine, doc_start, gains, w_qkv, w_out, w_gate_up, w_dn
    )
    input_grad, grad_qkv, gain_grads = backward(
        inputs[0], d_hidden, cosine, sine, gains, w_qkv, d_att, queries, pair, soft, raw, normed, gain_grads
    )
    down, gate_up_share, output, qkv, gain_grads = reduce_gradients(
        [
            grad.reshape(2, 2, grad.shape[0] // 4, grad.shape[1])
            for grad in (grad_down, grad_gate_up, grad_output, grad_qkv)
        ],
        gain_grads,
    )
    at = lax.axis_index("fsdp")
    wide = lax.dynamic_slice(gain_grads, (0, at * 160), (4, 160))
    return (
        layer_out[None],
        input_grad[None],
        qkv[:, :1024].astype(jnp.float32),
        qkv[:, 1024:1280].astype(jnp.float32),
        qkv[:, 1280:].astype(jnp.float32),
        output.astype(jnp.float32),
        gate_up_share[:, :2048].astype(jnp.float32),
        gate_up_share[:, 2048:].astype(jnp.float32),
        down.astype(jnp.float32),
        wide[0],
        wide[1],
        wide[2],
        wide[3],
        lax.dynamic_slice(gain_grads[4, :256], (at * 64,), (64,)),
        lax.dynamic_slice(gain_grads[4, 256:512], (at * 64,), (64,)),
    )


def solution(mesh):
    in_specs = (
        P("fsdp", "seq", None),
        P("fsdp", "seq"),
        P("fsdp", None),
        P("fsdp", None),
        P("fsdp", None),
        P("fsdp", None),
        P("fsdp", None),
        P("fsdp", None),
        P("fsdp", None),
        P("fsdp"),
        P("fsdp"),
        P("fsdp"),
        P("fsdp"),
        P("fsdp"),
        P("fsdp"),
        P("fsdp", "seq", None),
    )
    out_specs = (
        P("fsdp", "seq", None),
        P("fsdp", "seq", None),
        P("fsdp", None),
        P("fsdp", None),
        P("fsdp", None),
        P("fsdp", None),
        P("fsdp", None),
        P("fsdp", None),
        P("fsdp", None),
        P("fsdp"),
        P("fsdp"),
        P("fsdp"),
        P("fsdp"),
        P("fsdp"),
        P("fsdp"),
    )
    return jax.shard_map(body, mesh=mesh, in_specs=in_specs, out_specs=out_specs, check_vma=False)
```

time: 312 us -> 246 us (0.79); the launches traced: 306 us -> 245 us
  matrix products: 59.6 us -> 0 us
  Pallas kernels: 159 us -> 214 us
  other arithmetic: 40.7 us -> 7.3 us
  local copies, waits for them, and re-layouts: 35.4 us -> 23.2 us
  starting transfers between devices: 5.6 us -> 0 us
  waiting for transfers between devices: 5.03 us -> 0 us
    pallas_call x0 -> x2, Pallas kernels: none -> 111 us  [the longest x1 74.2 us: forward(): pl.pallas_call(forward_kernel, out_shape=[jax.ShapeDtypeStruct(*o) for o...]
    dot_general x18 -> x0, matrix products: 59.6 us -> none  [the longest x4 15.7 us: contract_cols(): lax.dot_general(left, right, (((1,), (1,)), ((), ())), preferred_element_...]
    pallas_call x1, Pallas kernels: 90.8 us -> 38.7 us  [gather_weights(): pl.pallas_call(gather_kernel, out_shape=[jax.ShapeDtypeStruct(shape, jnp....]
    convert_element_type x9 -> x1, other arithmetic: 15.6 us -> 0.01 us  [body(): cosine, sine = rope_tables((row_index - doc_start[0]).astype(jnp.float32))]
    unnamed x97 -> x42, local copies, waits for them, and re-layouts: 9.96 us -> 19.3 us
    reduce_sum x9 -> x0, other arithmetic: 7.91 us -> none  [the longest x4 4.66 us: rms_scale(): values * lax.rsqrt(jnp.mean(values * values, -1, keepdims=True) + epsilon)]
    slice x8 -> x2, local copies, waits for them, and re-layouts: 6.71 us -> 0.66 us  [the longest x1 0.65 us: body(): wide[3]]
    ppermute x2 -> x0, starting transfers between devices: 5.6 us -> none  [from_behind(): return lax.ppermute(shard, axis, pairs)]
  transfers between devices with their start and end apart: 2 -> 0, of which waited for: 1 -> 0; matrix products, arithmetic and copies ran while one was open for 8% -> 0% of each run, Pallas kernels for 0% -> 0%
where the time goes in v2:
time: 246 us; the launch traced here: 245 us
  Pallas kernels  214 us (87%)
  local copies, waits for them, and re-layouts  23.2 us (9%)
  other arithmetic  7.3 us (3%)
    pallas_call x1, Pallas kernels, forward(): pl.pallas_call(forward_kernel, out_shape=[jax.ShapeDtypeStruct(*o) for o...  74.2 us
    pallas_call x1, Pallas kernels, reduce_gradients(): pl.pallas_call(reduce_kernel, out_shape=[jax.ShapeDtypeStruct(shape, jnp....  64.2 us
    pallas_call x1, Pallas kernels, gather_weights(): pl.pallas_call(gather_kernel, out_shape=[jax.ShapeDtypeStruct(shape, jnp....  38.7 us
    pallas_call x1, Pallas kernels, backward(): pl.pallas_call(backward_kernel, out_shape=[jax.ShapeDtypeStruct(*o) for o...  36.7 us
    unnamed x42, local copies, waits for them, and re-layouts  19.3 us

profile of v2, /device:TPU:0, one launch (start us, length us, event | category | flops | bytes accessed | tf_op | source)
XLA Modules:
  0.0 245.1 jit_solution(13850381371497786156)
XLA Ops:
  0.6 0.7 reshape.78.refs_7_
  1.3 0.7 reshape.79.refs_8_
  2.0 0.7 reshape.80.refs_9_
  2.6 0.7 reshape.81.refs_10_
  3.3 0.0 copy-start.6
  3.3 1.1 copy-done.6
  4.4 0.0 copy-start.7
  4.4 1.1 copy-done.7
  5.5 0.0 copy-start.8
  5.5 1.1 copy-done.8
  6.5 0.0 copy-start.9
  6.5 1.0 copy-done.9
  7.5 0.0 copy-start.10
  7.5 1.0 copy-done.10
  8.5 0.0 copy-start.12
  8.5 0.9 copy-done.12
  9.4 0.0 copy-start.13
  9.4 0.9 copy-done.13
  10.3 0.0 copy-start.15
  10.3 0.7 copy-done.15
  10.9 0.0 copy-start.16
  10.9 0.7 copy-done.16
  11.6 0.0 copy-start.19
  11.6 38.7 %gather_weights.1 = (bf16[640,1536]{1,0:T(8,128)(2,1)S(1)}, bf16[1024,640]{1,0:T(8,128)(2,1)S(1)}, bf16[640,4096]{1,0:T(8,128)(2,1)S(1)}, bf16[2048,640]{1,0:T(8,128)(2,1)S(1)}, f32[8,640]{1,0:T(8,128)S(1)}) custom-call(bf16[160,1024]{1,0:T(8,128)(2,1)S(1)} %copy-done.9, bf16[160,256]{1,0:T(8,128)(2,1)S(1)} %copy-done.12, bf16[160,256]{1,0:T(8,128)(2,1)S(1)} %copy-done.13, ...), custom_call_target="tpu_custom_call" | custom-call | tf_op jit(solution)/shard_map/gather_weights/pallas_call | solution.py:427
  50.3 0.0 copy-start
  50.3 1.3 copy-done
  51.6 0.0 copy-start.1
  51.6 2.4 copy-done.1
  54.0 0.0 copy-start.2
  54.0 1.5 copy-done.2
  55.5 0.0 copy-start.4
  55.5 1.1 copy-done.4
  56.6 0.0 copy-start.11
  56.6 0.6 copy-done.11
  57.2 0.0 copy-done.19
  57.2 1.8 multiply_sine_fusion
  59.0 74.2 %forward.1 = (bf16[512,640]{1,0:T(8,128)(2,1)}, f32[512,640]{1,0:T(8,128)}, bf16[2,1024,256]{2,1,0:T(8,128)(2,1)}, bf16[2,1024,256]{2,1,0:T(8,128)(2,1)}, bf16[1...) custom-call(bf16[512,640]{1,0:T(8,128)(2,1)} %bitcast.24, ...), custom_call_target="tpu_custom_call" | custom-call | tf_op jit(solution)/shard_map/forward/pallas_call | solution.py:698
  133.2 0.0 copy-start.5
  133.2 36.7 %backward.1 = (f32[512,640]{1,0:T(8,128)}, bf16[640,1536]{1,0:T(8,128)(2,1)}, f32[8,640]{1,0:T(8,128)}) custom-call(bf16[512,640]{1,0:T(8,128)(2,1)} %bitcast.25, f32[512,640]{1,0:T(8,128)} %get-tuple-element.46.d_hidden, f32[512,128]{1,0:T(8,128)} %get-tuple-element.76.cosine, f32[512,128]{1,0:T(8,128)} %get-tuple-element.75.sine, f32[8,640]{1,0:T(8,128)} %copy-done.11, ...), custom_call_target="tpu_custom_call" | custom-call | tf_op jit(solution)/shard_map/backward/pallas_call | solution.py:828
  169.9 0.0 copy-done.5
  170.0 0.0 copy-start.3
  170.0 1.5 copy-done.3
  171.5 0.0 copy-start.14
  171.5 0.7 copy-done.14
  172.2 64.2 %reduce_gradients.1 = (bf16[512,640]{1,0:T(8,128)(2,1)S(1)}, bf16[160,4096]{1,0:T(8,128)(2,1)S(1)}, bf16[256,640]{1,0:T(8,128)(2,1)S(1)}, bf16[160,1536]{1,0:T(8,128)(2,1)S(1)}, f32[8,640]{1,0:T(8,128)S(1)}) custom-call(bf16[2,2,512,640]{3,2,1,0:T(8,128)(2,1)} %bitcast.26, bf16[2,2,160,4096]{3,2,1,0:T(8,128)(2,1)} %bitcast.23, ...), custom_call_target="tpu_custom_call" | custom-call | tf_op jit(solution)/shard_map/reduce_gradients/pallas_call | solution.py:284
  236.5 0.6 fusion
  237.0 1.8 slice_convert_fusion
  238.8 1.1 convert_element_type.35
  240.0 0.0 copy-start.18
  240.0 0.9 convert_element_type.32
  240.9 0.0 copy-start.17
  240.9 0.9 slice_convert_fusion.2
  241.8 0.7 slice_convert_fusion.3
  242.5 0.7 fusion.3
  243.2 0.0 copy-done.18
  243.2 0.8 copy.33
  244.0 0.0 copy-done.17
  244.0 1.1 copy.34
  (3 shorter events, 0.0 us)
Async XLA Ops:
  3.3 1.1 copy-start.6
  4.4 1.1 copy-start.7
  5.5 1.1 copy-start.8
  6.5 1.0 copy-start.9
  7.5 1.0 copy-start.10
  8.5 0.9 copy-start.12
  9.4 0.9 copy-start.13
  10.3 0.7 copy-start.15
  10.9 0.7 copy-start.16
  11.6 45.6 %copy-start.19 = (s32[1,512]{1,0:T(1,128)S(1)}, s32[1,512]{1,0:T(1,128)}, u32[]{:S(2)}) copy-start(s32[1,512]{1,0:T(1,128)} %doc.1) | copy-start | bytes 6148
  50.3 1.3 copy-start
  51.6 2.4 copy-start.1
  54.0 1.5 copy-start.2
  55.5 1.1 copy-start.4
  56.6 0.6 copy-start.11
  133.2 36.7 %copy-start.5 = (bf16[1024,640]{1,0:T(8,128)(2,1)S(1)}, bf16[1024,640]{1,0:T(8,128)(2,1)}, u32[]{:S(2)}) copy-start(bf16[1024,640]{1,0:T(8,128)(2,1)} %get-tuple-element.57) | copy-start | bytes 3932164
  170.0 1.5 copy-start.3
  171.5 0.7 copy-start.14
  240.0 3.2 %copy-start.18 = (bf16[512,640]{1,0:T(8,128)(2,1)S(1)}, bf16[512,640]{1,0:T(8,128)(2,1)}, u32[]{:S(2)}) copy-start(bf16[512,640]{1,0:T(8,128)(2,1)} %get-tuple-element.45) | copy-start | bytes 1966084
  240.9 3.1 %copy-start.17 = (f32[512,640]{1,0:T(8,128)S(1)}, f32[512,640]{1,0:T(8,128)}, u32[]{:S(2)}) copy-start(f32[512,640]{1,0:T(8,128)} %get-tuple-element.54) | copy-start | bytes 3932164

commit v3 on v2

v3 whole, which is shorter than its diff:
```python
import jax
import jax.numpy as jnp
from jax import lax
from jax.experimental import pallas as pl
from jax.experimental.pallas import tpu as pltpu
from jax.sharding import PartitionSpec as P

epsilon = 1e-06
rope_base = 10000.0


MESH = pl.DeviceIdType.MESH
DIMS = ("C", "X1", "X0", "Y1", "Y0", "Z1", "Z0")


def place():
    return lax.axis_index("seq"), lax.axis_index("fsdp")


def bit_of(dim, s, f):
    if dim == "C":
        return lax.rem(f, 2)
    if dim == "X1":
        return lax.div(f, 2)
    if dim == "X0":
        return lax.rem(lax.rem(lax.div(s, 4), 2) + lax.div(f, 2), 2)
    at = lax.rem(s, 4) if dim[0] == "Y" else lax.div(s, 8)
    if dim[1] == "1":
        return lax.div(at, 2)
    return lax.rem(lax.rem(at, 2) + lax.div(at, 2), 2)


def partner(dim, s, f):
    if dim == "C":
        return (s, f + 1 - 2 * lax.rem(f, 2))
    step = 1 - 2 * lax.rem(lax.div(s, 4), 2)
    if dim == "X0":
        return (s + 4 * step, f)
    if dim == "X1":
        return (s + 4 * step, f + 2 - 4 * lax.div(f, 2))
    at, scale = (lax.rem(s, 4), 1) if dim[0] == "Y" else (lax.div(s, 8), 8)
    if dim[1] == "1":
        return (s + scale * (3 - 2 * at), f)
    return (s + scale * (1 - 2 * lax.rem(at, 2)), f)


def neighbour(s, f, by):
    return (lax.rem(s + 32 + by, 32), f)


def greet(s, f):
    barrier = pltpu.get_barrier_semaphore()
    for dim in DIMS:
        pl.semaphore_signal(barrier, inc=1, device_id=partner(dim, s, f), device_id_type=MESH)
    for by in (1, -1):
        pl.semaphore_signal(barrier, inc=1, device_id=neighbour(s, f, by), device_id_type=MESH)
    pl.semaphore_wait(barrier, len(DIMS) + 2)


def span(start, size, tile):
    if isinstance(start, int):
        return pl.ds(start, size)
    return pl.ds(pl.multiple_of(start, tile), size)


class Region:
    def __init__(self, q, r, c):
        self.q, self.r, self.c = q, r, c

    def of(self, ref):
        return ref.at[pl.ds(*self.q), span(*self.r, 16), span(*self.c, 128)]

    def flat(self, ref, r0=0, c0=0):
        return ref.at[span(self.r[0] + r0, self.r[1], 16), span(self.c[0] + c0, self.c[1], 128)]

    def halved(self, axis, bit):
        start, size = getattr(self, axis)
        half = size // 2
        mine = Region(self.q, self.r, self.c)
        setattr(mine, axis, (start + bit * half, half))
        theirs = Region(self.q, self.r, self.c)
        setattr(theirs, axis, (start + (1 - bit) * half, half))
        return mine, theirs

    @property
    def shape(self):
        return (self.q[1], self.r[1], self.c[1])


def rows_per_step(rows, cols):
    best = 16
    for n in (32, 48, 64, 80, 96, 128, 160):
        if rows % n == 0 and n * cols <= 48 * 2048:
            best = n
    return best


def add_blocks(out, first, second, shape):
    quarters, rows, cols = shape
    step = rows_per_step(rows, cols)
    for q in range(quarters):

        def body(i, carry, q=q):
            at = i * step
            ref, index = out(q, at, step)
            ref_a, index_a = first(q, at, step)
            ref_b, index_b = second(q, at, step)
            ref[index] = ref_a[index_a] + ref_b[index_b]
            return carry

        lax.fori_loop(0, rows // step, body, 0)


def view(ref, region):
    def pick(q, at, step):
        rows = span(region.r[0] + at, step, 16)
        return ref, (region.q[0] + q, rows, span(region.c[0], region.c[1], 128))

    return pick


def flat_view(ref, region, r0, c0):
    def pick(q, at, step):
        return ref, (span(region.r[0] + r0 + at, step, 16), span(region.c[0] + c0, region.c[1], 128))

    return pick


def whole_view(ref):
    def pick(q, at, step):
        return ref, (q, span(at, step, 16), slice(None))

    return pick


ORDERS = (
    ("X1", "Y1", "Z1", "X0", "Y0", "Z0"),
    ("Y1", "Z1", "X0", "X1", "Y0", "Z0"),
    ("Z1", "X0", "Y0", "X1", "Z0", "Y1"),
    ("X0", "Y0", "Z0", "X1", "Y1", "Z1"),
    ("Y0", "Z0", "X1", "Y1", "Z1", "X0"),
    ("Z0", "X1", "Y1", "Z1", "X0", "Y0"),
)
PARTS = (
    (0, 0, 384, 0, 640, ORDERS[0], "rrr"),
    (1, 0, 160, 0, 1536, ORDERS[1], "ccr"),
    (1, 0, 160, 1536, 1536, ORDERS[2], "ccr"),
    (1, 0, 160, 3072, 1024, ORDERS[3], "ccc"),
    (0, 384, 128, 0, 640, ORDERS[5], "rrr"),
    (2, 0, 256, 0, 640, ORDERS[4], "rrr"),
    (3, 0, 160, 0, 512, ORDERS[5], "ccr"),
    (3, 0, 160, 512, 512, ORDERS[3], "ccr"),
    (3, 0, 160, 1024, 512, ORDERS[1], "ccr"),
)
EARLY, LATE = tuple(range(6)), (6, 7, 8)
SHARES = ((512, 640), (160, 4096), (256, 640), (160, 1536))


def part_shapes(part):
    _, _, rows, _, cols, order, splits = part
    shapes, shape, cut = [], [2, rows, cols], iter(splits)
    for dim in order[:4]:
        axis = 0 if dim == "X1" else {"r": 1, "c": 2}[next(cut)]
        shape[axis] //= 2
        shapes.append(tuple(shape))
    return shapes


class Reduce:
    STAGES = 10

    def __init__(self, s, f, grads, totals, scratch, send_sem, recv_sem, local_sem):
        self.s, self.f, self.grads, self.totals = s, f, grads, totals
        self.send_sem, self.recv_sem, self.local_sem = send_sem, recv_sem, local_sem
        self.acc, self.from_core, self.inbox, self.extra = [], [], [], []
        for _ in PARTS:
            self.acc.append(scratch.pop(0))
            self.from_core.append(scratch.pop(0))
            self.inbox.append([scratch.pop(0) for _ in range(4)])
            self.extra.append([scratch.pop(0) for _ in range(3)])
        n = len(PARTS)
        self.pending, self.count = [], 0
        self.flights, self.loads, self.where = [None] * n, [None] * n, [None] * n
        self.cuts = [iter(part[6]) for part in PARTS]
        self.trail, self.stage = [[] for _ in PARTS], [0] * n

    def send(self, src, dst, dim):
        copy = pltpu.make_async_remote_copy(
            src_ref=src,
            dst_ref=dst,
            send_sem=self.send_sem.at[self.count],
            recv_sem=self.recv_sem.at[self.count],
            device_id=partner(dim, self.s, self.f),
            device_id_type=MESH,
        )
        copy.start()
        self.count += 1
        self.pending.append(copy)
        return copy

    def begin(self, p):
        tensor, r0, rows, c0, cols, _, _ = PARTS[p]
        core = bit_of("C", self.s, self.f)
        grad = self.grads[tensor]
        if len(grad.shape) == 2:
            deep = grad.shape[0] // 4
            pick = lambda high, low: grad.at[span((2 * high + low) * deep + r0, rows, 16), pl.ds(c0, cols)]
            self.flights[p] = [
                self.send(pick(high, 1 - core), self.from_core[p].at[high], "C") for high in range(2)
            ]
            self.mine = getattr(self, "mine", {})
            self.mine[p] = [(span((2 * high + core) * deep + r0, rows, 16)) for high in range(2)]
        else:
            block_ = (pl.ds(0, 2), pl.ds(r0, rows), pl.ds(c0, cols))
            self.flights[p] = [
                self.send(grad.at[block_[0], 1 - core, block_[1], block_[2]], self.from_core[p], "C")
            ]
            self.loads[p] = pltpu.make_async_copy(
                grad.at[block_[0], core, block_[1], block_[2]], self.acc[p], self.local_sem.at[p]
            )
            self.loads[p].start()
        self.where[p] = Region((0, 2), (0, rows), (0, cols))

    def advance(self, p):
        part, stage, s, f = PARTS[p], self.stage[p], self.s, self.f
        tensor, r0, rows, c0, cols, order, _ = part
        acc, where, extra = self.acc[p], self.where[p], self.extra[p]
        self.stage[p] += 1
        for flight in self.flights[p]:
            flight.wait_recv()
        if stage < 5:
            if stage == 0 and self.loads[p] is None:
                grad, deep = self.grads[tensor], self.mine[p]
                for high in range(2):
                    acc[high] = grad[deep[high], pl.ds(c0, cols)] + self.from_core[p][high]
            else:
                if stage == 0:
                    self.loads[p].wait()
                source = self.from_core[p] if stage == 0 else self.inbox[p][stage - 1]
                add_blocks(view(acc, where), view(acc, where), whole_view(source), where.shape)
            if stage == 4:
                self.flights[p] = [self.send(where.of(acc), extra[0], order[4])]
                return
            dim = order[stage]
            axis = "q" if dim == "X1" else next(self.cuts[p])
            self.trail[p].append((dim, axis))
            self.where[p], theirs = where.halved(axis, bit_of(dim, s, f))
            self.flights[p] = [self.send(theirs.of(acc), self.inbox[p][stage], dim)]
        elif stage == 5:
            add_blocks(whole_view(extra[1]), view(acc, where), whole_view(extra[0]), where.shape)
            self.flights[p] = [self.send(extra[1], extra[2], order[5])]
        elif stage == 6:
            total = self.totals[tensor]
            add_blocks(flat_view(total, where, r0, c0), whole_view(extra[1]), whole_view(extra[2]), where.shape)
            self.trail[p] = [move for move in reversed(self.trail[p]) if move[1] != "q"]
            self.spread(p)
        else:
            dim, axis = self.trail[p].pop(0)
            start, size = getattr(where, axis)
            setattr(where, axis, (start - bit_of(dim, s, f) * size, 2 * size))
            if self.trail[p]:
                self.spread(p)

    def spread(self, p):
        tensor, r0, _, c0, _, _, _ = PARTS[p]
        region = self.where[p].flat(self.totals[tensor], r0, c0)
        self.flights[p] = [self.send(region, region, self.trail[p][0][0])]


def reduce_scratch():
    scratch, sends = [], 7
    for part in PARTS:
        shapes = part_shapes(part)
        scratch += [pltpu.VMEM((2, part[2], part[4]), jnp.bfloat16)] * 2
        scratch += [pltpu.VMEM(shape, jnp.bfloat16) for shape in shapes]
        scratch += [pltpu.VMEM(shapes[-1], jnp.bfloat16)] * 3
        sends += 11
    return scratch, sends


PIECES = (
    (0, 0, 0, 160, 1024, "X0", "Z0", "c"),
    (1, 0, 1024, 160, 256, "Z0", "X0", "c"),
    (2, 0, 1280, 160, 256, "Z0", "X0", "c"),
    (3, 1, 0, 256, 640, "Y0", "X0", "r"),
    (4, 2, 0, 160, 2048, "Z1", "Y1", "c"),
    (5, 2, 2048, 160, 2048, "Z0", "Y0", "c"),
    (6, 3, 0, 512, 640, "Y1", "Z1", "r"),
)
WHOLES = ((640, 1536), (1024, 640), (640, 4096), (2048, 640))


def own_gains(gain_shards, gain_own, f):
    gain_own[...] = jnp.zeros_like(gain_own)
    for i, shard in enumerate(gain_shards):
        share = shard.shape[1]
        shift = lax.broadcasted_iota(jnp.int32, (share, 4 * share), 1) - lax.broadcasted_iota(
            jnp.int32, (share, 4 * share), 0
        )
        chosen = jnp.where(shift == share * f, 1.0, 0.0).astype(jnp.bfloat16)
        row = jnp.dot(shard[...], chosen, preferred_element_type=jnp.float32)
        if i < 4:
            gain_own[i : i + 1, :] = row
        else:
            gain_own[4:5, 256 * (i - 4) : 256 * (i - 3)] = row


class Gather:
    def __init__(self, s, f, shards, outs, send_sem, recv_sem, local_sem):
        self.s, self.f, self.shards, self.outs = s, f, shards, outs
        self.send_sem, self.recv_sem, self.local_sem = send_sem, recv_sem, local_sem
        self.copies, self.count = [], 0
        self.core, high = bit_of("C", s, f), bit_of("X1", s, f)
        self.far = 2 * (1 - high) + self.core
        self.flights, self.sides, self.loads = {}, {}, {}

    def send(self, src, dst, dim):
        copy = pltpu.make_async_remote_copy(
            src_ref=src,
            dst_ref=dst,
            send_sem=self.send_sem.at[self.count],
            recv_sem=self.recv_sem.at[self.count],
            device_id=partner(dim, self.s, self.f),
            device_id_type=MESH,
        )
        copy.start()
        self.count += 1
        self.copies.append(copy)
        return copy

    def boxes(self, piece, bit_one, bit_two):
        _, _, c0, rows, cols, _, _, cut = piece
        half = rows // 2
        if cut == "c":
            quarter = ((bit_two * half, half), (bit_one * (cols // 2), cols // 2))
        else:
            quarter = ((bit_two * half + bit_one * (half // 2), half // 2), (0, cols))
        return quarter, ((bit_two * half, half), (0, cols))

    def spot(self, piece, share, box):
        (r, nr), (c, nc) = box
        return self.outs[piece[1]].at[span(r + share * piece[3], nr, 16), span(c + piece[2], nc, 128)]

    def begin(self, pieces):
        for i in pieces:
            piece = PIECES[i]
            (r, nr), (c, nc) = quarter = self.boxes(
                piece, bit_of(piece[5], self.s, self.f), bit_of(piece[6], self.s, self.f)
            )[0]
            src = self.shards[i].at[span(r, nr, 16), span(c, nc, 128)]
            self.flights[i] = self.send(src, self.spot(piece, self.f, quarter), "X1")
        for i in pieces:
            piece = PIECES[i]
            dst = self.spot(piece, self.f, ((0, piece[3]), (0, piece[4])))
            self.sides[i] = [self.send(self.shards[i], dst, "C")]
            self.loads[i] = pltpu.make_async_copy(self.shards[i], dst, self.local_sem.at[i])
            self.loads[i].start()

    def step(self, i, number):
        piece, s, f, far = PIECES[i], self.s, self.f, self.far
        one, two = bit_of(piece[5], s, f), bit_of(piece[6], s, f)
        quarter, half = self.boxes(piece, one, two)
        self.flights[i].wait_recv()
        if number == 0:
            here = self.spot(piece, far, quarter)
            self.flights[i] = self.send(here, here, piece[5])
        elif number == 1:
            here = self.spot(piece, far, half)
            self.flights[i] = self.send(here, here, piece[6])
            here = self.spot(piece, far, self.boxes(piece, 1 - one, two)[0])
        else:
            here = self.spot(piece, far, self.boxes(piece, one, 1 - two)[1])
        self.sides[i].append(self.send(here, here, "C"))

    def arrive(self, i):
        for copy in self.sides[i]:
            copy.wait_recv()
        self.loads[i].wait()


SENDS = 7 * len(PIECES) + 2


NT = (((1,), (1,)), ((), ()))


def dot(left, right):
    return jnp.dot(left, right, preferred_element_type=jnp.float32)


def dot_nt(left, right):
    return lax.dot_general(left, right, NT, preferred_element_type=jnp.float32)


def block(i, size):
    return pl.ds(pl.multiple_of(i * size, size), size)


def each(count, body):
    def step(i, carry):
        body(i)
        return carry

    lax.fori_loop(0, count, step, 0)


def scale_of(y):
    return lax.rsqrt(jnp.mean(y * y, -1, keepdims=True) + epsilon)


def norm_back(dz, y, r, g):
    gained = g * dz
    return r * gained - y * (r * r * r) * jnp.mean(gained * y, -1, keepdims=True)


def fold(terms):
    rows, cols = terms.shape
    return jnp.sum(terms.reshape(rows // 8, 8, cols), 0)


def turn(v, cosine, sine):
    a, b = v[:, :128], v[:, 128:]
    return jnp.concatenate([a * cosine - b * sine, b * cosine + a * sine], 1)


def turn_back(v, cosine, sine):
    a, b = v[:, :128], v[:, 128:]
    return jnp.concatenate([a * cosine + b * sine, b * cosine - a * sine], 1)


def forward_kernel(*refs):
    x_far, cot_far, cosine, sine, doc = refs[:5]
    shards, gain_shards = refs[5:12], refs[12:18]
    outs, gains, gain_grads, weight = refs[18:31], refs[31], refs[32], refs[33]
    (
        x, cot, d_hidden, d_att, d_att_scaled, queries, pair, soft, raw, normed,
        grad_down, grad_gate_up, grad_output, w_qkv, w_output, w_gate_up, w_down,
        turned_v, att, att_t, projected, hidden, normed_two, normed_two_t,
        product, slope, level, gate, up, down, d_down, d_proj, layer_out, sums, weight_sums,
        gain_own, gain_mid, gain_in,
        send_sem, recv_sem, local_sem, out_sem, in_sem, pair_sem,
    ) = refs[34:]
    s, f = place()
    greet(s, f)
    gather = Gather(s, f, shards, (w_qkv, w_output, w_gate_up, w_down), send_sem, recv_sem, local_sem)
    gather.begin((1, 2, 0))
    load_x = pltpu.make_async_copy(x_far, x, in_sem.at[0])
    load_x.start()
    load_cot = pltpu.make_async_copy(cot_far, cot, in_sem.at[1])
    load_cot.start()
    own_gains(gain_shards, gain_own, f)
    flight = gather.send(gain_own, gain_in.at[0], "C")
    lanes = lambda i: gains[pl.ds(i, 1), :]
    written = []

    def write(src, number):
        copy = pltpu.make_async_copy(src, outs[number], out_sem.at[number])
        copy.start()
        written.append(copy)

    flight.wait_recv()
    gain_mid[...] = gain_own[...] + gain_in[0]
    flight = gather.send(gain_mid, gain_in.at[1], "X1")
    for i in (1, 2, 0):
        gather.step(i, 0)
    gather.begin((3, 4, 5, 6))
    for i in (1, 2, 0):
        gather.step(i, 1)
    flight.wait_recv()
    gains[...] = gain_mid[...] + gain_in[1]
    load_x.wait()

    def norm_in(i):
        rows = block(i, 64)
        y = x[rows, :].astype(jnp.float32)
        normed[rows, :] = (y * scale_of(y) * lanes(0)).astype(jnp.bfloat16)

    each(8, norm_in)
    write(normed, 7)
    for i in (1, 2, 0):
        gather.step(i, 2)
    gather.arrive(1)
    gather.arrive(2)
    pair_raw = dot(normed[...], w_qkv[:, 1024:1536])
    raw[:, 1024:1280] = pair_raw[:, :256]
    pair[512:1024, 256:512] = pair_raw[:, 256:].astype(jnp.bfloat16)

    def shape_key(i):
        rows = block(i, 128)
        y = raw[rows, 1024:1280]
        y = turn(y * scale_of(y) * gains[pl.ds(4, 1), 256:512], cosine[rows, :], sine[rows, :])
        pair[pl.ds(pl.multiple_of(512 + i * 128, 128), 128), 0:256] = y.astype(jnp.bfloat16)

    each(4, shape_key)
    pass_on = pltpu.make_async_remote_copy(
        src_ref=pair.at[pl.ds(512, 512), :],
        dst_ref=pair.at[pl.ds(0, 512), :],
        send_sem=pair_sem.at[0],
        recv_sem=pair_sem.at[1],
        device_id=neighbour(s, f, 1),
        device_id_type=MESH,
    )
    pass_on.start()
    gather.arrive(0)
    write(w_qkv, 11)

    def shape_query(h):
        raw[:, block(h, 256)] = dot(normed[...], w_qkv[:, block(h, 256)])

        def rows_of(i):
            rows = block(i, 128)
            y = raw[rows, block(h, 256)]
            y = turn(y * scale_of(y) * gains[pl.ds(4, 1), 0:256], cosine[rows, :], sine[rows, :])
            at = pl.ds(pl.multiple_of(h * 256 + lax.rem(i, 2) * 128, 128), 128)
            queries[lax.div(i, 2), at, :] = (y * 0.0625).astype(jnp.bfloat16)

        each(4, rows_of)

    each(4, shape_query)
    write(raw, 6)
    write(queries, 3)
    for i in (3, 4, 5, 6):
        gather.step(i, 0)
    row = [lax.broadcasted_iota(jnp.int32, (1, 256), 1) + i * 256 for i in range(2)]
    lowest = [
        jnp.maximum(row[i] + 1, doc[0:1, 256 * i : 256 * (i + 1)] - (s - 1) * 512) for i in range(2)
    ]

    def weigh(i, h, first, count):
        total = None
        query = queries[i, block(h, 256), :]
        for c in range(first, first + count, 2):
            low = i * 256 + c * 128
            score = dot_nt(pair[low : low + 256, 0:256], query)
            key = lax.broadcasted_iota(jnp.int32, (256, 256), 0) + low
            seen = (key >= lowest[i]) & (key <= row[i] + 512)
            p = jnp.where(seen, jnp.exp(score), 0.0)
            soft[i, c * 128 : c * 128 + 256, block(h, 256)] = p.astype(jnp.bfloat16)
            total = fold(p) if total is None else total + fold(p)
        return total

    for i, first, count in ((0, 4, 2), (1, 2, 4)):

        def own_keys(h, i=i, first=first, count=count):
            weight_sums[i, h] = weigh(i, h, first, count)

        each(4, own_keys)
    for i in (3, 4, 5, 6):
        gather.step(i, 1)
    pass_on.wait_recv()
    write(pair, 4)
    turned_v[...] = pair[:, 256:512].T
    for i, first, count in ((0, 0, 4), (1, 0, 2)):

        def attend(h, i=i, first=first, count=count):
            total = weight_sums[i, h] + weigh(i, h, first, count)
            inverse = 1.0 / jnp.sum(total, 0, keepdims=True)
            weight[pl.ds(4 * i + h, 1), :] = inverse
            mixed = dot(turned_v[:, 256 * i : 256 * i + 768], soft[i, :, block(h, 256)]) * inverse
            att_t[block(h, 256), 256 * i : 256 * (i + 1)] = mixed.astype(jnp.bfloat16)
            att[256 * i : 256 * (i + 1), block(h, 256)] = mixed.T.astype(jnp.bfloat16)

        each(4, attend)
    write(soft, 5)
    for i in (3, 4, 5, 6):
        gather.step(i, 2)
    gather.arrive(3)
    projected[...] = dot(att[...], w_output[...])

    def mid(i):
        rows = block(i, 64)
        y = projected[rows, :]
        z = x[rows, :].astype(jnp.float32) + y * scale_of(y) * lanes(1)
        hidden[rows, :] = z
        normed_two[rows, :] = (z * scale_of(z) * lanes(2)).astype(jnp.bfloat16)

    each(8, mid)
    normed_two_t[...] = normed_two[...].T
    gather.arrive(4)
    gather.arrive(5)

    def feed(j):
        cols = block(j, 256)
        gate[...] = dot(normed_two[...], w_gate_up[:, cols])
        up[...] = dot(normed_two[...], w_gate_up[:, pl.ds(pl.multiple_of(2048 + j * 256, 256), 256)])

        def bend(i):
            rows = block(i, 64)
            g, u = gate[rows, :], up[rows, :]
            square = g * g
            t = jnp.tanh(0.7978845608028654 * g * (1.0 + 0.044715 * square))
            half = 0.5 * (1.0 + t)
            gelu = g * half
            rise = half + 0.5 * g * (1.0 - t * t) * (0.7978845608028654 * (1.0 + 0.134145 * square))
            product[rows, cols] = (gelu * u).astype(jnp.bfloat16)
            slope[rows, cols] = (rise * u).astype(jnp.bfloat16)
            level[rows, cols] = gelu.astype(jnp.bfloat16)

        each(8, bend)

    each(8, feed)
    gather.arrive(6)
    down[...] = dot(product[...], w_down[...])
    sums[...] = jnp.zeros_like(sums)
    load_cot.wait()

    def end(i):
        rows = block(i, 64)
        y, dz = down[rows, :], cot[rows, :].astype(jnp.float32)
        r = scale_of(y)
        layer_out[rows, :] = (hidden[rows, :] + y * r * lanes(3)).astype(jnp.bfloat16)
        d_down[rows, :] = norm_back(dz, y, r, lanes(3)).astype(jnp.bfloat16)
        sums[2] += fold(dz * y * r)

    each(8, end)
    write(layer_out, 0)

    def feed_back(j):
        cols = block(j, 256)
        gate[...] = dot_nt(d_down[...], w_down[cols, :])
        grad_down[cols, :] = dot(product[:, cols].T, d_down[...]).astype(jnp.bfloat16)

        def bend(i):
            rows = block(i, 128)
            d = gate[rows, :]
            slope[rows, cols] = (d * slope[rows, cols].astype(jnp.float32)).astype(jnp.bfloat16)
            level[rows, cols] = (d * level[rows, cols].astype(jnp.float32)).astype(jnp.bfloat16)

        each(4, bend)
        grad_gate_up[:, cols] = dot(normed_two_t[...], slope[:, cols]).astype(jnp.bfloat16)
        grad_gate_up[:, pl.ds(pl.multiple_of(2048 + j * 256, 256), 256)] = dot(
            normed_two_t[...], level[:, cols]
        ).astype(jnp.bfloat16)

    each(8, feed_back)
    write(grad_down, 8)
    write(grad_gate_up, 9)
    down[...] = dot_nt(slope[...], w_gate_up[:, 0:2048])
    down[...] += dot_nt(level[...], w_gate_up[:, 2048:4096])

    def mid_back(i):
        rows = block(i, 64)
        dz, y = down[rows, :], hidden[rows, :]
        r = scale_of(y)
        total = cot[rows, :].astype(jnp.float32) + norm_back(dz, y, r, lanes(2))
        sums[1] += fold(dz * y * r)
        d_hidden[rows, :] = total
        y = projected[rows, :]
        r = scale_of(y)
        d_proj[rows, :] = norm_back(total, y, r, lanes(1)).astype(jnp.bfloat16)
        sums[0] += fold(total * y * r)

    each(8, mid_back)
    write(d_hidden, 1)
    columns = weight[...].T
    for h in range(4):
        part = pl.ds(256 * h, 256)
        back = dot_nt(d_proj[...], w_output[part, :])
        for i in range(2):
            mine = back[256 * i : 256 * (i + 1), :]
            n = 4 * i + h
            d_att[i, part, :] = mine.astype(jnp.bfloat16)
            d_att_scaled[i, part, :] = (mine * columns[:, n : n + 1]).astype(jnp.bfloat16)
    write(d_att, 2)
    write(d_att_scaled, 10)

    def output_back(h):
        grad_output[block(h, 256), :] = dot(att_t[block(h, 256), :], d_proj[...]).astype(jnp.bfloat16)

    each(4, output_back)
    write(grad_output, 12)
    gain_grads[...] = jnp.zeros_like(gain_grads)
    for i in range(3):
        gain_grads[pl.ds(i + 1, 1), :] = jnp.sum(sums[i], 0, keepdims=True)
    for copy in written:
        copy.wait()
    pass_on.wait_send()
    for copy in gather.copies:
        copy.wait_send()


def forward(x, cot, cosine, sine, doc, shards, gain_shards):
    b, f32 = jnp.bfloat16, jnp.float32
    outs = [
        ((512, 640), b), ((512, 640), f32), ((2, 1024, 256), b), ((2, 1024, 256), b), ((1024, 512), b),
        ((2, 768, 1024), b), ((512, 1280), f32), ((512, 640), b),
        ((2048, 640), b), ((640, 4096), b), ((2, 1024, 256), b), ((640, 1536), b), ((1024, 640), b),
    ]
    near = [((8, 640), f32), ((8, 640), f32), ((8, 256), f32)]
    scratch = [
        ((512, 640), b), ((512, 640), b), ((512, 640), f32), ((2, 1024, 256), b), ((2, 1024, 256), b),
        ((2, 1024, 256), b), ((1024, 512), b), ((2, 768, 1024), b), ((512, 1280), f32), ((512, 640), b),
        ((2048, 640), b), ((640, 4096), b), ((1024, 640), b),
        ((640, 1536), b), ((1024, 640), b), ((640, 4096), b), ((2048, 640), b),
        ((256, 1024), b), ((512, 1024), b), ((1024, 512), b), ((512, 640), f32), ((512, 640), f32),
        ((512, 640), b), ((640, 512), b), ((512, 2048), b), ((512, 2048), b), ((512, 2048), b),
        ((512, 256), f32), ((512, 256), f32), ((512, 640), f32), ((512, 640), b), ((512, 640), b),
        ((512, 640), b), ((3, 8, 640), f32), ((2, 4, 8, 256), f32),
        ((8, 640), f32), ((8, 640), f32), ((2, 8, 640), f32),
    ]
    sems = (SENDS, SENDS, 7, len(outs), 2, 2)
    far, vmem = pl.BlockSpec(memory_space=pl.ANY), pl.BlockSpec(memory_space=pltpu.VMEM)
    return pl.pallas_call(
        forward_kernel,
        out_shape=[jax.ShapeDtypeStruct(*o) for o in outs + near],
        in_specs=[far] * 2 + [vmem] * 3 + [far] * 7 + [vmem] * 6,
        out_specs=[far] * len(outs) + [vmem] * len(near),
        scratch_shapes=[pltpu.VMEM(*o) for o in scratch] + [pltpu.SemaphoreType.DMA((n,)) for n in sems],
        compiler_params=pltpu.CompilerParams(
            collective_id=2, has_side_effects=True, vmem_limit_bytes=60 << 20
        ),
        name="forward",
    )(x, cot, cosine, sine, doc, *shards, *gain_shards)


def backward_kernel(*refs):
    fars, near = refs[:10], refs[10:15]
    cosine, sine, gains, gain_grads, weight = near
    grads, refs = refs[15:18], refs[18:]
    input_grad, totals, gain_total = refs[0], refs[1:5], refs[5]
    (
        d_att, d_att_scaled, soft, pair, queries, raw, normed, w_qkv, x, d_hidden, *rest
    ) = refs[6:]
    (
        turned_k, d_soft, d_scores, d_queries, d_pair, first, other, d_raw, normed_t, d_normed,
        grad_qkv, sums, head_sums, gain_in, gain_sum, *rest
    ) = rest
    in_sem, pair_sem, send_sem, recv_sem, local_sem = rest[-5:]
    s, f = place()
    greet(s, f)
    reduce = Reduce(s, f, (*grads, grad_qkv), totals, list(rest[:-5]), send_sem, recv_sem, local_sem)
    loads = []
    for i, (src, dst) in enumerate(
        zip(fars, (d_att, pair, soft, d_att_scaled, queries, raw, normed, w_qkv, x, d_hidden))
    ):
        loads.append(pltpu.make_async_copy(src, dst, in_sem.at[i]))
        loads[-1].start()
    for p in EARLY:
        reduce.begin(p)

    def all_of(parts):
        for p in parts:
            reduce.advance(p)

    d_pair[...] = jnp.zeros_like(d_pair)
    sums[...] = jnp.zeros_like(sums)
    head_sums[...] = jnp.zeros_like(head_sums)
    for load in loads[:5]:
        load.wait()
    turned_k[...] = pair[:, 0:256].T
    for i in range(2):

        def one_head(h, i=i):
            cols = block(h, 256)
            inverse = weight[pl.ds(4 * i + h, 1), :]
            total = None
            for c in range(3):
                low = 256 * (i + c)
                back = dot_nt(pair[low : low + 256, 256:512], d_att[i, cols, :])
                d_soft[256 * c : 256 * (c + 1), :] = back
                part = fold(soft[i, 256 * c : 256 * (c + 1), cols].astype(jnp.float32) * back)
                total = part if total is None else total + part
            inner = jnp.sum(total, 0, keepdims=True) * inverse
            for c in range(3):
                rows = pl.ds(256 * c, 256)
                p = soft[i, rows, cols].astype(jnp.float32)
                d_scores[i, rows, cols] = (p * ((d_soft[rows, :] - inner) * inverse)).astype(jnp.bfloat16)

        each(4, one_head)

    def to_pair(i, low, count):
        at, here = pl.ds(low, count), pl.ds(low - 256 * i, count)
        d_pair[at, 0:256] += dot(d_scores[i, here, :], queries[i])
        d_pair[at, 256:512] += dot(soft[i, here, :], d_att_scaled[i])

    to_pair(0, 0, 512)
    to_pair(1, 256, 256)
    first[...] = d_pair[0:512, :].astype(jnp.bfloat16)
    pass_back = pltpu.make_async_remote_copy(
        src_ref=first,
        dst_ref=other,
        send_sem=pair_sem.at[0],
        recv_sem=pair_sem.at[1],
        device_id=neighbour(s, f, -1),
        device_id_type=MESH,
    )
    pass_back.start()
    all_of(EARLY)
    to_pair(0, 512, 256)
    to_pair(1, 512, 512)
    for load in loads[5:]:
        load.wait()
    normed_t[...] = normed[...].T
    for i in range(2):

        def query_back(h, i=i):
            cols = block(h, 256)
            mixed = dot(turned_k[:, 256 * i : 256 * i + 768], d_scores[i, :, cols]) * 0.0625
            d_queries[...] = mixed.T

            def rows_of(n):
                rows = pl.ds(pl.multiple_of(256 * i + n * 128, 128), 128)
                dz = turn_back(d_queries[block(n, 128), :], cosine[rows, :], sine[rows, :])
                y = raw[rows, cols]
                r = scale_of(y)
                d_raw[rows, cols] = norm_back(dz, y, r, gains[pl.ds(4, 1), 0:256]).astype(jnp.bfloat16)
                head_sums[0] += fold(dz * y * r)

            each(2, rows_of)

        each(4, query_back)
    pass_back.wait_recv()

    def key_back(i):
        rows = block(i, 128)
        own = pl.ds(pl.multiple_of(512 + i * 128, 128), 128)
        dz = d_pair[own, 0:256] + other[rows, 0:256].astype(jnp.float32)
        dz = turn_back(dz, cosine[rows, :], sine[rows, :])
        y = raw[rows, 1024:1280]
        r = scale_of(y)
        d_raw[rows, 1024:1280] = norm_back(dz, y, r, gains[pl.ds(4, 1), 256:512]).astype(jnp.bfloat16)
        head_sums[1] += fold(dz * y * r)
        d_value = d_pair[own, 256:512] + other[rows, 256:512].astype(jnp.float32)
        d_raw[rows, 1280:1536] = d_value.astype(jnp.bfloat16)

    each(4, key_back)

    def weigh_in(j):
        cols = block(j, 256)
        grad_qkv[:, cols] = dot(normed_t[...], d_raw[:, cols]).astype(jnp.bfloat16)

    each(6, weigh_in)
    for p in LATE:
        reduce.begin(p)
    all_of(EARLY)
    d_normed[...] = dot_nt(d_raw[...], w_qkv[...])
    lanes_in = gains[pl.ds(0, 1), :]

    def norm_in_back(i):
        rows = block(i, 64)
        y, dz = x[rows, :].astype(jnp.float32), d_normed[rows, :]
        r = scale_of(y)
        input_grad[rows, :] = d_hidden[rows, :] + norm_back(dz, y, r, lanes_in)
        sums[...] += fold(dz * y * r)

    each(8, norm_in_back)
    gain_sum[0] = gain_grads[...]
    gain_sum[0, pl.ds(0, 1), :] = jnp.sum(sums[...], 0, keepdims=True)
    gain_sum[0, pl.ds(4, 1), 0:256] = jnp.sum(head_sums[0], 0, keepdims=True)
    gain_sum[0, pl.ds(4, 1), 256:512] = jnp.sum(head_sums[1], 0, keepdims=True)
    gain_dims = ("C", "X1", "X0", "Y1", "Y0", "Z1", "Z0")
    flight = reduce.send(gain_sum.at[0], gain_in.at[0], gain_dims[0])
    for stage in range(Reduce.STAGES):
        all_of(LATE)
        if stage < 7:
            flight.wait_recv()
            gain_sum[stage + 1] = gain_sum[stage] + gain_in[stage]
            if stage < 6:
                flight = reduce.send(gain_sum.at[stage + 1], gain_in.at[stage + 1], gain_dims[stage + 1])
        if stage < Reduce.STAGES - 2:
            all_of(EARLY)
    gain_total[...] = gain_sum[7]
    pass_back.wait_send()
    for copy in reduce.pending:
        copy.wait_send()


def backward(fars, near, grads):
    b, f32 = jnp.bfloat16, jnp.float32
    outs = [((512, 640), f32)] + [(shape, b) for shape in SHARES] + [((8, 640), f32)]
    held = [
        ((2, 1024, 256), b), ((2, 1024, 256), b), ((2, 768, 1024), b), ((1024, 512), b), ((2, 1024, 256), b),
        ((512, 1280), f32), ((512, 640), b), ((640, 1536), b), ((512, 640), b), ((512, 640), f32),
    ]
    scratch = [
        ((256, 1024), b), ((768, 256), f32), ((2, 768, 1024), b), ((256, 256), f32), ((1024, 512), f32),
        ((512, 512), b), ((512, 512), b), ((512, 1536), b), ((640, 512), b), ((512, 640), f32),
        ((640, 1536), b), ((8, 640), f32), ((2, 8, 256), f32), ((7, 8, 640), f32), ((8, 8, 640), f32),
    ]
    parts, sends = reduce_scratch()
    sems = (len(held), 2, sends, sends, len(PARTS))
    far, vmem = pl.BlockSpec(memory_space=pl.ANY), pl.BlockSpec(memory_space=pltpu.VMEM)
    return pl.pallas_call(
        backward_kernel,
        out_shape=[jax.ShapeDtypeStruct(*o) for o in outs],
        in_specs=[far] * 10 + [vmem] * 5 + [far] * 3,
        out_specs=[vmem] * len(outs),
        scratch_shapes=[pltpu.VMEM(*o) for o in held + scratch]
        + parts
        + [pltpu.SemaphoreType.DMA((n,)) for n in sems],
        compiler_params=pltpu.CompilerParams(
            collective_id=3, has_side_effects=True, vmem_limit_bytes=60 << 20
        ),
        name="backward",
    )(*fars, *near, *grads)


def rope_tables(positions):
    frequency = rope_base ** (-(jnp.arange(128, dtype=jnp.float32) * (2.0 / 256)))
    angles = positions[:, None] * frequency[None, :]
    return jnp.cos(angles), jnp.sin(angles)


def body(
    inputs,
    doc_start,
    w_query,
    w_key,
    w_value,
    w_output,
    w_gate,
    w_up,
    w_down,
    norm_attn_in,
    norm_attn_out,
    norm_ffn_in,
    norm_ffn_out,
    norm_query,
    norm_key,
    cotangent,
):
    row_index = lax.axis_index("seq") * 512 + jnp.arange(512, dtype=jnp.int32)
    cosine, sine = rope_tables((row_index - doc_start[0]).astype(jnp.float32))
    (
        layer_out, d_hidden, d_att, queries, pair, soft, raw, normed,
        grad_down, grad_gate_up, d_att_scaled, w_qkv, grad_output, gains, gain_grads, weight,
    ) = forward(
        inputs[0], cotangent[0], cosine, sine, doc_start,
        (w_query, w_key, w_value, w_output, w_gate, w_up, w_down),
        [
            g.reshape(1, -1)
            for g in (norm_attn_in, norm_attn_out, norm_ffn_in, norm_ffn_out, norm_query, norm_key)
        ],
    )
    input_grad, down, gate_up_share, output, qkv, gain_grads = backward(
        (d_att, pair, soft, d_att_scaled, queries, raw, normed, w_qkv, inputs[0], d_hidden),
        (cosine, sine, gains, gain_grads, weight),
        [
            grad.reshape(2, 2, grad.shape[0] // 4, grad.shape[1])
            for grad in (grad_down, grad_gate_up, grad_output)
        ],
    )
    at = lax.axis_index("fsdp")
    wide = lax.dynamic_slice(gain_grads, (0, at * 160), (4, 160))
    return (
        layer_out[None],
        input_grad[None],
        qkv[:, :1024].astype(jnp.float32),
        qkv[:, 1024:1280].astype(jnp.float32),
        qkv[:, 1280:].astype(jnp.float32),
        output.astype(jnp.float32),
        gate_up_share[:, :2048].astype(jnp.float32),
        gate_up_share[:, 2048:].astype(jnp.float32),
        down.astype(jnp.float32),
        wide[0],
        wide[1],
        wide[2],
        wide[3],
        lax.dynamic_slice(gain_grads[4, :256], (at * 64,), (64,)),
        lax.dynamic_slice(gain_grads[4, 256:512], (at * 64,), (64,)),
    )


def solution(mesh):
    in_specs = (
        P("fsdp", "seq", None),
        P("fsdp", "seq"),
        P("fsdp", None),
        P("fsdp", None),
        P("fsdp", None),
        P("fsdp", None),
        P("fsdp", None),
        P("fsdp", None),
        P("fsdp", None),
        P("fsdp"),
        P("fsdp"),
        P("fsdp"),
        P("fsdp"),
        P("fsdp"),
        P("fsdp"),
        P("fsdp", "seq", None),
    )
    out_specs = (
        P("fsdp", "seq", None),
        P("fsdp", "seq", None),
        P("fsdp", None),
        P("fsdp", None),
        P("fsdp", None),
        P("fsdp", None),
        P("fsdp", None),
        P("fsdp", None),
        P("fsdp", None),
        P("fsdp"),
        P("fsdp"),
        P("fsdp"),
        P("fsdp"),
        P("fsdp"),
        P("fsdp"),
    )
    return jax.shard_map(body, mesh=mesh, in_specs=in_specs, out_specs=out_specs, check_vma=False)
```

time: 246 us -> 193 us (0.78)
  Pallas kernels: 214 us -> 171 us
  local copies, waits for them, and re-layouts: 23.2 us -> 9.61 us
  other arithmetic: 7.3 us -> 10.9 us
    pallas_call x2 -> x0, Pallas kernels: 103 us -> none  [the longest x1 64.2 us: reduce_gradients(): pl.pallas_call(reduce_kernel, out_shape=[jax.ShapeDtypeStruct(shape, jnp....]
    pallas_call x1, Pallas kernels: 36.7 us -> 87.4 us  [backward(): pl.pallas_call(backward_kernel, out_shape=[jax.ShapeDtypeStruct(*o) for o...]
    unnamed x42 -> x10, local copies, waits for them, and re-layouts: 19.3 us -> 1.91 us
    pallas_call x1, Pallas kernels: 74.2 us -> 84 us  [forward(): pl.pallas_call(forward_kernel, out_shape=[jax.ShapeDtypeStruct(*o) for o...]
where the time goes in v3:
time: 193 us
  Pallas kernels  171 us (89%)
  other arithmetic  10.9 us (6%)
  local copies, waits for them, and re-layouts  9.61 us (5%)
    pallas_call x1, Pallas kernels, backward(): pl.pallas_call(backward_kernel, out_shape=[jax.ShapeDtypeStruct(*o) for o...  87.4 us
    pallas_call x1, Pallas kernels, forward(): pl.pallas_call(forward_kernel, out_shape=[jax.ShapeDtypeStruct(*o) for o...  84 us
    reshape x4, local copies, waits for them, and re-layouts, body(): g.reshape(1, -1)  4.88 us

profile of v3, /device:TPU:0, one launch (start us, length us, event | category | flops | bytes accessed | tf_op | source)
XLA Modules:
  0.0 192.6 jit_solution(15892488394113731283)
XLA Ops:
  0.7 0.7 subtract_convert_fusion
  1.4 1.8 multiply_sine_fusion
  3.1 1.2 reshape.75.refs_12_
  4.4 1.2 reshape.76.refs_13_
  5.6 1.2 reshape.77.refs_14_
  6.8 1.2 reshape.78.refs_15_
  8.0 84.0 %forward.1 = (bf16[512,640]{1,0:T(8,128)(2,1)}, f32[512,640]{1,0:T(8,128)}, bf16[2,1024,256]{2,1,0:T(8,128)(2,1)}, bf16[2,1024,256]{2,1,0:T(8,128)(2,1)}, bf16[1...) custom-call(bf16[512,640]{1,0:T(8,128)(2,1)} %bitcast.20, ...), custom_call_target="tpu_custom_call" | custom-call | tf_op jit(solution)/shard_map/forward/pallas_call | solution.py:703
  92.0 87.4 %backward.1 = (f32[512,640]{1,0:T(8,128)}, bf16[512,640]{1,0:T(8,128)(2,1)}, bf16[160,4096]{1,0:T(8,128)(2,1)}, bf16[256,640]{1,0:T(8,128)(2,1)}, bf16[160,1536]{1,0:T(8,128)(2,1)}, /*index=5*/f32[8,640]{1,0:T(8,128)}) custom-call(bf16[2,1024,256]{2,1,0:T(8,128)(2,1)} %get-tuple-element.38.refs_0_, bf16[1024,512]{1,0:T(8,128)(2,1)} %get-tuple-element.39.refs_1_, ...), custom_call_target="tpu_custom_call" | custom-call | tf_op jit(solution)/shard_map/backward/pallas_call | solution.py:883
  179.4 0.0 copy-start.1
  179.5 2.0 %slice_convert_fusion.2 = f32[160,1024]{1,0:T(8,128)} fusion(bf16[160,1536]{1,0:T(8,128)(2,1)} %get-tuple-element.54), kind=kLoop, calls=%fused_computation.4 | loop fusion | flops 163840 | bytes 983040 | tf_op jit(solution)/shard_map/convert_element_type | solution.py:948
  181.4 1.7 slice_convert_fusion.3
  183.1 1.9 convert_element_type.32
  185.0 0.0 copy-done.1
  185.0 0.0 copy-start.3
  185.0 1.8 slice_convert_fusion
  186.8 0.0 copy-start.2
  186.8 0.0 copy-done.3
  186.8 0.0 copy-start
  186.8 1.1 convert_element_type.35
  187.9 1.5 fusion.3
  189.4 0.7 fusion.2
  190.2 0.6 fusion
  190.7 0.0 copy-done.2
  190.7 0.8 copy.33
  191.6 0.0 copy-done
  191.6 1.1 copy.34
  (1 shorter events, 0.0 us)
Async XLA Ops:
  179.4 5.5 %copy-start.1 = (bf16[160,4096]{1,0:T(8,128)(2,1)S(1)}, bf16[160,4096]{1,0:T(8,128)(2,1)}, u32[]{:S(2)}) copy-start(bf16[160,4096]{1,0:T(8,128)(2,1)} %get-tuple-element.56) | copy-start | bytes 3932164
  185.0 1.8 copy-start.3
  186.8 4.0 %copy-start.2 = (bf16[512,640]{1,0:T(8,128)(2,1)S(1)}, bf16[512,640]{1,0:T(8,128)(2,1)}, u32[]{:S(2)}) copy-start(bf16[512,640]{1,0:T(8,128)(2,1)} %get-tuple-element.37) | copy-start | bytes 1966084
  186.8 4.8 %copy-start = (f32[512,640]{1,0:T(8,128)S(1)}, f32[512,640]{1,0:T(8,128)}, u32[]{:S(2)}) copy-start(f32[512,640]{1,0:T(8,128)} %get-tuple-element.53) | copy-start | bytes 3932164

commit v4 on v3

--- a/solution.py
+++ b/solution.py
@@ -1,5 +1,6 @@
 import jax
 import jax.numpy as jnp
+import numpy as np
 from jax import lax
 from jax.experimental import pallas as pl
 from jax.experimental.pallas import tpu as pltpu
@@ -11,6 +12,8 @@
 
 MESH = pl.DeviceIdType.MESH
 DIMS = ("C", "X1", "X0", "Y1", "Y0", "Z1", "Z0")
+AXES = {"X": ("X1", "X0"), "Y": ("Y1", "Y0"), "Z": ("Z1", "Z0")}
+CORNERS = (("Y0", "Z0"), ("X0", "Z1"), ("Z1", "Y1"), ("X0", "Y1"))
 
 
 def place():
@@ -44,17 +47,26 @@
     return (s + scale * (1 - 2 * lax.rem(at, 2)), f)
 
 
+def target(dims, s, f):
+    for dim in (dims,) if isinstance(dims, str) else dims:
+        s, f = partner(dim, s, f)
+    return s, f
+
+
 def neighbour(s, f, by):
     return (lax.rem(s + 32 + by, 32), f)
 
 
-def greet(s, f):
+def greet(s, f, corners):
     barrier = pltpu.get_barrier_semaphore()
     for dim in DIMS:
         pl.semaphore_signal(barrier, inc=1, device_id=partner(dim, s, f), device_id_type=MESH)
     for by in (1, -1):
         pl.semaphore_signal(barrier, inc=1, device_id=neighbour(s, f, by), device_id_type=MESH)
-    pl.semaphore_wait(barrier, len(DIMS) + 2)
+    for one, two in corners:
+        corner = partner(two, *partner(one, s, f))
+        pl.semaphore_signal(barrier, inc=1, device_id=corner, device_id_type=MESH)
+    pl.semaphore_wait(barrier, len(DIMS) + 2 + len(corners))
 
 
 def span(start, size, tile):
@@ -142,17 +154,15 @@
     ("Z0", "X1", "Y1", "Z1", "X0", "Y0"),
 )
 PARTS = (
-    (0, 0, 384, 0, 640, ORDERS[0], "rrr"),
-    (1, 0, 160, 0, 1536, ORDERS[1], "ccr"),
-    (1, 0, 160, 1536, 1536, ORDERS[2], "ccr"),
-    (1, 0, 160, 3072, 1024, ORDERS[3], "ccc"),
-    (0, 384, 128, 0, 640, ORDERS[5], "rrr"),
-    (2, 0, 256, 0, 640, ORDERS[4], "rrr"),
-    (3, 0, 160, 0, 512, ORDERS[5], "ccr"),
-    (3, 0, 160, 512, 512, ORDERS[3], "ccr"),
-    (3, 0, 160, 1024, 512, ORDERS[1], "ccr"),
+    (0, 0, 256, 0, 640, ORDERS[3], "rrr"),
+    (1, 0, 160, 0, 1536, ORDERS[0], "ccr"),
+    (1, 0, 160, 1536, 1536, ORDERS[1], "ccr"),
+    (1, 0, 160, 3072, 1024, ORDERS[2], "ccc"),
+    (0, 256, 256, 0, 640, ORDERS[4], "rrr"),
+    (2, 0, 256, 0, 640, ORDERS[5], "rrr"),
 )
-EARLY, LATE = tuple(range(6)), (6, 7, 8)
+EARLY = (1, 2, 3, 0, 4, 5)
+LATE = ((0, "XYZ"), (512, "YXZ"), (1024, "ZXY"))
 SHARES = ((512, 640), (160, 4096), (256, 640), (160, 1536))
 
 
@@ -172,10 +182,9 @@
     def __init__(self, s, f, grads, totals, scratch, send_sem, recv_sem, local_sem):
         self.s, self.f, self.grads, self.totals = s, f, grads, totals
         self.send_sem, self.recv_sem, self.local_sem = send_sem, recv_sem, local_sem
-        self.acc, self.from_core, self.inbox, self.extra = [], [], [], []
+        self.acc, self.inbox, self.extra = [], [], []
         for _ in PARTS:
             self.acc.append(scratch.pop(0))
-            self.from_core.append(scratch.pop(0))
             self.inbox.append([scratch.pop(0) for _ in range(4)])
             self.extra.append([scratch.pop(0) for _ in range(3)])
         n = len(PARTS)
@@ -190,7 +199,7 @@
             dst_ref=dst,
             send_sem=self.send_sem.at[self.count],
             recv_sem=self.recv_sem.at[self.count],
-            device_id=partner(dim, self.s, self.f),
+            device_id=target(dim, self.s, self.f),
             device_id_type=MESH,
         )
         copy.start()
@@ -198,28 +207,24 @@
         self.pending.append(copy)
         return copy
 
-    def begin(self, p):
+    def load(self, p):
         tensor, r0, rows, c0, cols, _, _ = PARTS[p]
-        core = bit_of("C", self.s, self.f)
-        grad = self.grads[tensor]
-        if len(grad.shape) == 2:
-            deep = grad.shape[0] // 4
-            pick = lambda high, low: grad.at[span((2 * high + low) * deep + r0, rows, 16), pl.ds(c0, cols)]
-            self.flights[p] = [
-                self.send(pick(high, 1 - core), self.from_core[p].at[high], "C") for high in range(2)
-            ]
-            self.mine = getattr(self, "mine", {})
-            self.mine[p] = [(span((2 * high + core) * deep + r0, rows, 16)) for high in range(2)]
-        else:
-            block_ = (pl.ds(0, 2), pl.ds(r0, rows), pl.ds(c0, cols))
-            self.flights[p] = [
-                self.send(grad.at[block_[0], 1 - core, block_[1], block_[2]], self.from_core[p], "C")
-            ]
-            self.loads[p] = pltpu.make_async_copy(
-                grad.at[block_[0], core, block_[1], block_[2]], self.acc[p], self.local_sem.at[p]
-            )
-            self.loads[p].start()
-        self.where[p] = Region((0, 2), (0, rows), (0, cols))
+        self.loads[p] = pltpu.make_async_copy(
+            self.grads[tensor].at[:, pl.ds(r0, rows), pl.ds(c0, cols)], self.acc[p], self.local_sem.at[p]
+        )
+        self.loads[p].start()
+
+    def resume(self, p):
+        _, _, rows, _, cols, order, _ = PARTS[p]
+        self.loads[p].wait()
+        self.loads[p] = None
+        dim = order[0]
+        axis = "q" if dim == "X1" else next(self.cuts[p])
+        self.trail[p].append((dim, axis))
+        region = Region((0, 2), (0, rows), (0, cols))
+        self.where[p], theirs = region.halved(axis, bit_of(dim, self.s, self.f))
+        self.flights[p] = [self.send(theirs.of(self.acc[p]), self.inbox[p][0], dim)]
+        self.stage[p] = 1
 
     def advance(self, p):
         part, stage, s, f = PARTS[p], self.stage[p], self.s, self.f
@@ -229,15 +234,8 @@
         for flight in self.flights[p]:
             flight.wait_recv()
         if stage < 5:
-            if stage == 0 and self.loads[p] is None:
-                grad, deep = self.grads[tensor], self.mine[p]
-                for high in range(2):
-                    acc[high] = grad[deep[high], pl.ds(c0, cols)] + self.from_core[p][high]
-            else:
-                if stage == 0:
-                    self.loads[p].wait()
-                source = self.from_core[p] if stage == 0 else self.inbox[p][stage - 1]
-                add_blocks(view(acc, where), view(acc, where), whole_view(source), where.shape)
+            source = self.inbox[p][stage - 1]
+            add_blocks(view(acc, where), view(acc, where), whole_view(source), where.shape)
             if stage == 4:
                 self.flights[p] = [self.send(where.of(acc), extra[0], order[4])]
                 return
@@ -267,11 +265,121 @@
         self.flights[p] = [self.send(region, region, self.trail[p][0][0])]
 
 
+class Late:
+    STAGES = 6
+    FLIPS = ((1, 0), (0, 1), (1, 1))
+
+    def __init__(self, reduce, number, grad, total, scratch):
+        self.reduce, self.grad, self.total = reduce, grad, total
+        self.c0, self.axes = LATE[number]
+        self.acc, self.from_core, *self.inbox = scratch
+        self.where = Region((0, 2), (0, 160), (0, 512))
+        self.cuts, self.trail, self.stage = iter("ccr"), [], 0
+        self.flights = []
+
+    def bit(self, dim):
+        return bit_of(dim, self.reduce.s, self.reduce.f)
+
+    def begin(self):
+        core = self.bit("C")
+        for high in range(2):
+            theirs = self.grad.at[span((2 * high + 1 - core) * 160, 160, 16), pl.ds(self.c0, 512)]
+            self.flights.append(self.reduce.send(theirs, self.from_core.at[high], "C"))
+
+    def scatter(self, axis, inbox):
+        moves = [(dim, "q" if dim == "X1" else next(self.cuts)) for dim in AXES[axis]]
+        self.trail.append(moves)
+        here = self.where
+
+        def cut(flips):
+            region = here
+            for (dim, along), flip in zip(moves, flips):
+                bit = self.bit(dim)
+                region = region.halved(along, 1 - bit if flip else bit)[0]
+            return region
+
+        self.flights = [
+            self.reduce.send(
+                cut(flips).of(self.acc),
+                inbox.at[k],
+                tuple(dim for (dim, _), flip in zip(moves, flips) if flip),
+            )
+            for k, flips in enumerate(self.FLIPS)
+        ]
+        self.where = cut((0, 0))
+
+    def spread(self):
+        moves = [move for move in self.trail.pop() if move[1] != "q"]
+        self.grow = moves
+        region = self.where.flat(self.total, 0, self.c0)
+        choices = self.FLIPS if len(moves) == 2 else ((1,),)
+        self.flights = [
+            self.reduce.send(region, region, tuple(dim for (dim, _), flip in zip(moves, flips) if flip))
+            for flips in choices
+        ]
+
+    def summed(self, inbox):
+        spot = (
+            pl.ds(*self.where.q),
+            span(*self.where.r, 16),
+            span(*self.where.c, 128),
+        )
+        terms = [self.acc[spot]] + [inbox[k] for k in range(3)]
+        first, second, third, fourth = (term.astype(jnp.float32) for term in terms)
+        return spot, ((first + second) + (third + fourth)).astype(jnp.bfloat16)
+
+    def advance(self):
+        for flight in self.flights:
+            flight.wait_recv()
+        stage = self.stage
+        self.stage += 1
+        if stage == 0:
+            core = self.bit("C")
+            for high in range(2):
+                mine = span((2 * high + core) * 160, 160, 16)
+                self.acc[high] = self.grad[mine, pl.ds(self.c0, 512)] + self.from_core[high]
+            self.scatter(self.axes[0], self.inbox[0])
+        elif stage == 1:
+            spot, value = self.summed(self.inbox[0])
+            self.acc[spot] = value
+            self.scatter(self.axes[1], self.inbox[1])
+        elif stage == 2:
+            spot, value = self.summed(self.inbox[1])
+            self.acc[spot] = value
+            self.flights = [
+                self.reduce.send(
+                    self.where.of(self.acc),
+                    self.inbox[2].at[k],
+                    tuple(dim for dim, flip in zip(AXES[self.axes[2]], flips) if flip),
+                )
+                for k, flips in enumerate(self.FLIPS)
+            ]
+        elif stage == 3:
+            _, value = self.summed(self.inbox[2])
+            rows, cols = self.where.r, self.where.c
+            self.total[span(*rows, 16), span(cols[0] + self.c0, cols[1], 128)] = value[0]
+            self.spread()
+        else:
+            for dim, axis in reversed(self.grow):
+                start, size = getattr(self.where, axis)
+                setattr(self.where, axis, (start - self.bit(dim) * size, 2 * size))
+            if self.trail:
+                self.spread()
+
+
+def late_scratch():
+    shapes = []
+    for _, axes in LATE:
+        one = (1, 160, 256) if axes[0] == "X" else (2, 160, 128)
+        shapes += [(2, 160, 512)] * 2 + [(3, *one), (3, 1, 80, 128), (3, 1, 80, 128)]
+    return [pltpu.VMEM(shape, jnp.bfloat16) for shape in shapes]
+
+
 def reduce_scratch():
-    scratch, sends = [], 7
+    scratch, sends = [], 10 + 17 * len(LATE)
     for part in PARTS:
         shapes = part_shapes(part)
-        scratch += [pltpu.VMEM((2, part[2], part[4]), jnp.bfloat16)] * 2
+        scratch += [pltpu.VMEM((2, part[2], part[4]), jnp.bfloat16)]
         scratch += [pltpu.VMEM(shape, jnp.bfloat16) for shape in shapes]
         scratch += [pltpu.VMEM(shapes[-1], jnp.bfloat16)] * 3
         sends += 11
@@ -279,30 +387,29 @@
 
 
 PIECES = (
-    (0, 0, 0, 160, 1024, "X0", "Z0", "c"),
-    (1, 0, 1024, 160, 256, "Z0", "X0", "c"),
-    (2, 0, 1280, 160, 256, "Z0", "X0", "c"),
-    (3, 1, 0, 256, 640, "Y0", "X0", "r"),
+    (0, 0, 0, 160, 1024, "Y0", "Z0", "c"),
+    (1, 0, 1024, 160, 256, None, None, "whole"),
+    (2, 0, 1280, 160, 256, None, None, "whole"),
+    (3, 1, 0, 256, 640, "X0", "Z1", "r"),
     (4, 2, 0, 160, 2048, "Z1", "Y1", "c"),
-    (5, 2, 2048, 160, 2048, "Z0", "Y0", "c"),
-    (6, 3, 0, 512, 640, "Y1", "Z1", "r"),
+    (5, 2, 2048, 160, 2048, "Y0", "Z0", "c"),
+    (6, 3, 0, 512, 640, "X0", "Y1", "r"),
 )
 WHOLES = ((640, 1536), (1024, 640), (640, 4096), (2048, 640))
 
 
 def own_gains(gain_shards, gain_own, f):
-    gain_own[...] = jnp.zeros_like(gain_own)
-    for i, shard in enumerate(gain_shards):
-        share = shard.shape[1]
-        shift = lax.broadcasted_iota(jnp.int32, (share, 4 * share), 1) - lax.broadcasted_iota(
-            jnp.int32, (share, 4 * share), 0
+    def placed(share):
+        shift = lax.broadcasted_iota(jnp.int32, (256, 4 * share), 1) - lax.broadcasted_iota(
+            jnp.int32, (256, 4 * share), 0
         )
         chosen = jnp.where(shift == share * f, 1.0, 0.0).astype(jnp.bfloat16)
-        row = jnp.dot(shard[...], chosen, preferred_element_type=jnp.float32)
-        if i < 4:
-            gain_own[i : i + 1, :] = row
-        else:
-            gain_own[4:5, 256 * (i - 4) : 256 * (i - 3)] = row
+        return jnp.dot(gain_shards[...].astype(jnp.bfloat16), chosen, preferred_element_type=jnp.float32)
+
+    gain_own[...] = jnp.where(lax.broadcasted_iota(jnp.int32, (8, 640), 0) < 4, placed(160), 0.0)
+    heads = placed(64)
+    gain_own[4:5, 0:256] = heads[4:5, :]
+    gain_own[4:5, 256:512] = heads[5:6, :]
 
 
 class Gather:
@@ -320,7 +427,7 @@
             dst_ref=dst,
             send_sem=self.send_sem.at[self.count],
             recv_sem=self.recv_sem.at[self.count],
-            device_id=partner(dim, self.s, self.f),
+            device_id=target(dim, self.s, self.f),
             device_id_type=MESH,
         )
         copy.start()
@@ -328,25 +435,26 @@
         self.copies.append(copy)
         return copy
 
-    def boxes(self, piece, bit_one, bit_two):
+    def quarter(self, piece, bit_one, bit_two):
         _, _, c0, rows, cols, _, _, cut = piece
         half = rows // 2
         if cut == "c":
-            quarter = ((bit_two * half, half), (bit_one * (cols // 2), cols // 2))
-        else:
-            quarter = ((bit_two * half + bit_one * (half // 2), half // 2), (0, cols))
-        return quarter, ((bit_two * half, half), (0, cols))
+            return (bit_two * half, half), (bit_one * (cols // 2), cols // 2)
+        return (bit_two * half + bit_one * (half // 2), half // 2), (0, cols)
 
     def spot(self, piece, share, box):
         (r, nr), (c, nc) = box
         return self.outs[piece[1]].at[span(r + share * piece[3], nr, 16), span(c + piece[2], nc, 128)]
 
+    def first(self, piece):
+        if piece[7] == "whole":
+            return (0, piece[3]), (0, piece[4])
+        return self.quarter(piece, bit_of(piece[5], self.s, self.f), bit_of(piece[6], self.s, self.f))
+
     def begin(self, pieces):
         for i in pieces:
             piece = PIECES[i]
-            (r, nr), (c, nc) = quarter = self.boxes(
-                piece, bit_of(piece[5], self.s, self.f), bit_of(piece[6], self.s, self.f)
-            )[0]
+            (r, nr), (c, nc) = quarter = self.first(piece)
             src = self.shards[i].at[span(r, nr, 16), span(c, nc, 128)]
             self.flights[i] = self.send(src, self.spot(piece, self.f, quarter), "X1")
         for i in pieces:
@@ -356,21 +464,26 @@
             self.loads[i] = pltpu.make_async_copy(self.shards[i], dst, self.local_sem.at[i])
             self.loads[i].start()
 
-    def step(self, i, number):
-        piece, s, f, far = PIECES[i], self.s, self.f, self.far
+    def fan(self, i):
+        piece, s, f = PIECES[i], self.s, self.f
+        self.flights[i].wait_recv()
+        here = self.spot(piece, self.far, self.first(piece))
+        self.sides[i].append(self.send(here, here, "C"))
+        if piece[7] == "whole":
+            return
         one, two = bit_of(piece[5], s, f), bit_of(piece[6], s, f)
-        quarter, half = self.boxes(piece, one, two)
-        self.flights[i].wait_recv()
-        if number == 0:
-            here = self.spot(piece, far, quarter)
-            self.flights[i] = self.send(here, here, piece[5])
-        elif number == 1:
-            here = self.spot(piece, far, half)
-            self.flights[i] = self.send(here, here, piece[6])
-            here = self.spot(piece, far, self.boxes(piece, 1 - one, two)[0])
-        else:
-            here = self.spot(piece, far, self.boxes(piece, one, 1 - two)[1])
-        self.sides[i].append(self.send(here, here, "C"))
+        self.flights[i] = [
+            (self.send(here, here, piece[5]), (1 - one, two)),
+            (self.send(here, here, piece[6]), (one, 1 - two)),
+            (self.send(here, here, (piece[5], piece[6])), (1 - one, 1 - two)),
+        ]
+
+    def relay(self, i):
+        piece = PIECES[i]
+        for flight, bits in self.flights[i]:
+            flight.wait_recv()
+            here = self.spot(piece, self.far, self.quarter(piece, *bits))
+            self.sides[i].append(self.send(here, here, "C"))
 
     def arrive(self, i):
         for copy in self.sides[i]:
@@ -378,7 +491,7 @@
         self.loads[i].wait()
 
 
-SENDS = 7 * len(PIECES) + 2
+SENDS = 9 * len(PIECES) + 7
 
 
 NT = (((1,), (1,)), ((), ()))
@@ -393,6 +506,8 @@
 
 
 def block(i, size):
+    if isinstance(i, int):
+        return pl.ds(i * size, size)
     return pl.ds(pl.multiple_of(i * size, size), size)
 
 
@@ -404,6 +519,11 @@
     lax.fori_loop(0, count, step, 0)
 
 
+def unrolled(count, body):
+    for i in range(count):
+        body(i)
+
+
 def scale_of(y):
     return lax.rsqrt(jnp.mean(y * y, -1, keepdims=True) + epsilon)
 
@@ -429,19 +549,19 @@
 
 
 def forward_kernel(*refs):
-    x_far, cot_far, cosine, sine, doc = refs[:5]
-    shards, gain_shards = refs[5:12], refs[12:18]
-    outs, gains, gain_grads, weight = refs[18:31], refs[31], refs[32], refs[33]
+    x_far, cot_far, doc, frequency, gain_shards = refs[:5]
+    shards = refs[5:12]
+    outs, gains, gain_grads, weight, cosine, sine = refs[12:25], *refs[25:30]
     (
         x, cot, d_hidden, d_att, d_att_scaled, queries, pair, soft, raw, normed,
         grad_down, grad_gate_up, grad_output, w_qkv, w_output, w_gate_up, w_down,
         turned_v, att, att_t, projected, hidden, normed_two, normed_two_t,
         product, slope, level, gate, up, down, d_down, d_proj, layer_out, sums, weight_sums,
-        gain_own, gain_mid, gain_in,
-        send_sem, recv_sem, local_sem, out_sem, in_sem, pair_sem,
-    ) = refs[34:]
+        gain_own, gain_mid, gain_in, normed_spots, *from_core,
+    ) = refs[30:-6]
+    send_sem, recv_sem, local_sem, out_sem, in_sem, pair_sem = refs[-6:]
     s, f = place()
-    greet(s, f)
+    greet(s, f, CORNERS)
     gather = Gather(s, f, shards, (w_qkv, w_output, w_gate_up, w_down), send_sem, recv_sem, local_sem)
     gather.begin((1, 2, 0))
     load_x = pltpu.make_async_copy(x_far, x, in_sem.at[0])
@@ -458,14 +578,25 @@
         copy.start()
         written.append(copy)
 
+    token = lax.broadcasted_iota(jnp.int32, (1, 512), 1) + s * 512
+    position = (token - doc[...]).astype(jnp.float32)
+    position = jnp.broadcast_to(position, (8, 512)).T
+
+    def table(i):
+        rows = block(i, 64)
+        angle = spots[rows, 0:1] * frequency[0:1, :]
+        cosine[rows, :] = jnp.cos(angle)
+        sine[rows, :] = jnp.sin(angle)
+
+    spots = normed_spots
+    spots[...] = position
     flight.wait_recv()
     gain_mid[...] = gain_own[...] + gain_in[0]
     flight = gather.send(gain_mid, gain_in.at[1], "X1")
+    unrolled(8, table)
     for i in (1, 2, 0):
-        gather.step(i, 0)
+        gather.fan(i)
     gather.begin((3, 4, 5, 6))
-    for i in (1, 2, 0):
-        gather.step(i, 1)
     flight.wait_recv()
     gains[...] = gain_mid[...] + gain_in[1]
     load_x.wait()
@@ -475,10 +606,8 @@
         y = x[rows, :].astype(jnp.float32)
         normed[rows, :] = (y * scale_of(y) * lanes(0)).astype(jnp.bfloat16)
 
-    each(8, norm_in)
+    unrolled(8, norm_in)
     write(normed, 7)
-    for i in (1, 2, 0):
-        gather.step(i, 2)
     gather.arrive(1)
     gather.arrive(2)
     pair_raw = dot(normed[...], w_qkv[:, 1024:1536])
@@ -489,9 +618,9 @@
         rows = block(i, 128)
         y = raw[rows, 1024:1280]
         y = turn(y * scale_of(y) * gains[pl.ds(4, 1), 256:512], cosine[rows, :], sine[rows, :])
-        pair[pl.ds(pl.multiple_of(512 + i * 128, 128), 128), 0:256] = y.astype(jnp.bfloat16)
-
-    each(4, shape_key)
+        pair[pl.ds(512 + i * 128, 128), 0:256] = y.astype(jnp.bfloat16)
+
+    unrolled(4, shape_key)
     pass_on = pltpu.make_async_remote_copy(
         src_ref=pair.at[pl.ds(512, 512), :],
         dst_ref=pair.at[pl.ds(0, 512), :],
@@ -501,6 +630,7 @@
         device_id_type=MESH,
     )
     pass_on.start()
+    gather.relay(0)
     gather.arrive(0)
     write(w_qkv, 11)
 
@@ -511,16 +641,16 @@
             rows = block(i, 128)
             y = raw[rows, block(h, 256)]
             y = turn(y * scale_of(y) * gains[pl.ds(4, 1), 0:256], cosine[rows, :], sine[rows, :])
-            at = pl.ds(pl.multiple_of(h * 256 + lax.rem(i, 2) * 128, 128), 128)
-            queries[lax.div(i, 2), at, :] = (y * 0.0625).astype(jnp.bfloat16)
-
-        each(4, rows_of)
+            at = pl.ds(pl.multiple_of(h * 256 + i % 2 * 128, 128), 128)
+            queries[i // 2, at, :] = (y * 0.0625).astype(jnp.bfloat16)
+
+        unrolled(4, rows_of)
 
     each(4, shape_query)
     write(raw, 6)
     write(queries, 3)
-    for i in (3, 4, 5, 6):
-        gather.step(i, 0)
+    gather.fan(3)
+    gather.fan(4)
     row = [lax.broadcasted_iota(jnp.int32, (1, 256), 1) + i * 256 for i in range(2)]
     lowest = [
         jnp.maximum(row[i] + 1, doc[0:1, 256 * i : 256 * (i + 1)] - (s - 1) * 512) for i in range(2)
@@ -545,8 +675,8 @@
             weight_sums[i, h] = weigh(i, h, first, count)
 
         each(4, own_keys)
-    for i in (3, 4, 5, 6):
-        gather.step(i, 1)
+        gather.fan(5 + i)
+    gather.relay(3)
     pass_on.wait_recv()
     write(pair, 4)
     turned_v[...] = pair[:, 256:512].T
@@ -561,9 +691,8 @@
             att[256 * i : 256 * (i + 1), block(h, 256)] = mixed.T.astype(jnp.bfloat16)
 
         each(4, attend)
+        gather.relay(4 + i)
     write(soft, 5)
-    for i in (3, 4, 5, 6):
-        gather.step(i, 2)
     gather.arrive(3)
     projected[...] = dot(att[...], w_output[...])
 
@@ -574,8 +703,9 @@
         hidden[rows, :] = z
         normed_two[rows, :] = (z * scale_of(z) * lanes(2)).astype(jnp.bfloat16)
 
-    each(8, mid)
+    unrolled(8, mid)
     normed_two_t[...] = normed_two[...].T
+    gather.relay(6)
     gather.arrive(4)
     gather.arrive(5)
 
@@ -596,7 +726,7 @@
             slope[rows, cols] = (rise * u).astype(jnp.bfloat16)
             level[rows, cols] = gelu.astype(jnp.bfloat16)
 
-        each(8, bend)
+        unrolled(8, bend)
 
     each(8, feed)
     gather.arrive(6)
@@ -612,13 +742,12 @@
         d_down[rows, :] = norm_back(dz, y, r, lanes(3)).astype(jnp.bfloat16)
         sums[2] += fold(dz * y * r)
 
-    each(8, end)
+    unrolled(8, end)
     write(layer_out, 0)
 
     def feed_back(j):
         cols = block(j, 256)
         gate[...] = dot_nt(d_down[...], w_down[cols, :])
-        grad_down[cols, :] = dot(product[:, cols].T, d_down[...]).astype(jnp.bfloat16)
 
         def bend(i):
             rows = block(i, 128)
@@ -626,15 +755,46 @@
             slope[rows, cols] = (d * slope[rows, cols].astype(jnp.float32)).astype(jnp.bfloat16)
             level[rows, cols] = (d * level[rows, cols].astype(jnp.float32)).astype(jnp.bfloat16)
 
-        each(4, bend)
-        grad_gate_up[:, cols] = dot(normed_two_t[...], slope[:, cols]).astype(jnp.bfloat16)
-        grad_gate_up[:, pl.ds(pl.multiple_of(2048 + j * 256, 256), 256)] = dot(
-            normed_two_t[...], level[:, cols]
+        unrolled(4, bend)
+        for grad, at in ((slope, 0), (level, 2048)):
+            block_ = dot(normed_two_t[...], grad[:, cols]).astype(jnp.bfloat16)
+            for q in range(4):
+                grad_gate_up[q // 2, q % 2, :, pl.ds(pl.multiple_of(at + j * 256, 256), 256)] = block_[
+                    160 * q : 160 * (q + 1), :
+                ]
+
+    def down_back(j):
+        q = lax.div(j, 2)
+        grad_down[lax.div(q, 2), lax.rem(q, 2), block(lax.rem(j, 2), 256), :] = dot(
+            product[:, block(j, 256)].T, d_down[...]
         ).astype(jnp.bfloat16)
 
+    core, exchanged = bit_of("C", s, f), {}
+    tensors = (grad_down, grad_gate_up, grad_output)
+
+    def exchange(p):
+        tensor, r0, rows, c0, cols, _, _ = PARTS[p]
+        theirs = tensors[tensor].at[pl.ds(0, 2), 1 - core, pl.ds(r0, rows), pl.ds(c0, cols)]
+        exchanged[p] = gather.send(theirs, from_core[p], "C")
+
+    def add_exchanged(p):
+        tensor, r0, rows, c0, cols, _, _ = PARTS[p]
+        exchanged[p].wait_recv()
+        step = rows_per_step(rows, cols)
+        for q in range(2):
+
+            def add(i, q=q):
+                at = pl.ds(pl.multiple_of(r0 + i * step, 16), step)
+                tensors[tensor][q, core, at, pl.ds(c0, cols)] += from_core[p][q, block(i, step), :]
+
+            each(rows // step, add)
+
     each(8, feed_back)
-    write(grad_down, 8)
-    write(grad_gate_up, 9)
+    for p in (1, 2, 3):
+        exchange(p)
+    each(8, down_back)
+    for p in (0, 4):
+        exchange(p)
     down[...] = dot_nt(slope[...], w_gate_up[:, 0:2048])
     down[...] += dot_nt(level[...], w_gate_up[:, 2048:4096])
 
@@ -650,9 +810,15 @@
         d_proj[rows, :] = norm_back(total, y, r, lanes(1)).astype(jnp.bfloat16)
         sums[0] += fold(total * y * r)
 
-    each(8, mid_back)
+    unrolled(8, mid_back)
     write(d_hidden, 1)
     columns = weight[...].T
+
+    def output_back(h):
+        grad_output[lax.div(h, 2), lax.rem(h, 2)] = dot(att_t[block(h, 256), :], d_proj[...]).astype(jnp.bfloat16)
+
+    each(4, output_back)
+    exchange(5)
     for h in range(4):
         part = pl.ds(256 * h, 256)
         back = dot_nt(d_proj[...], w_output[part, :])
@@ -663,12 +829,14 @@
             d_att_scaled[i, part, :] = (mine * columns[:, n : n + 1]).astype(jnp.bfloat16)
     write(d_att, 2)
     write(d_att_scaled, 10)
-
-    def output_back(h):
-        grad_output[block(h, 256), :] = dot(att_t[block(h, 256), :], d_proj[...]).astype(jnp.bfloat16)
-
-    each(4, output_back)
-    write(grad_output, 12)
+    for p in (1, 2, 3):
+        add_exchanged(p)
+    write(grad_gate_up.at[:, core], 9)
+    for p in (0, 4):
+        add_exchanged(p)
+    write(grad_down.at[:, core], 8)
+    add_exchanged(5)
+    write(grad_output.at[:, core], 12)
     gain_grads[...] = jnp.zeros_like(gain_grads)
     for i in range(3):
         gain_grads[pl.ds(i + 1, 1), :] = jnp.sum(sums[i], 0, keepdims=True)
@@ -679,38 +847,39 @@
         copy.wait_send()
 
 
-def forward(x, cot, cosine, sine, doc, shards, gain_shards):
+def forward(x, cot, doc, frequency, gain_shards, shards):
     b, f32 = jnp.bfloat16, jnp.float32
     outs = [
         ((512, 640), b), ((512, 640), f32), ((2, 1024, 256), b), ((2, 1024, 256), b), ((1024, 512), b),
         ((2, 768, 1024), b), ((512, 1280), f32), ((512, 640), b),
-        ((2048, 640), b), ((640, 4096), b), ((2, 1024, 256), b), ((640, 1536), b), ((1024, 640), b),
+        ((2, 512, 640), b), ((2, 160, 4096), b), ((2, 1024, 256), b), ((640, 1536), b), ((2, 256, 640), b),
     ]
-    near = [((8, 640), f32), ((8, 640), f32), ((8, 256), f32)]
+    near = [((8, 640), f32), ((8, 640), f32), ((8, 256), f32), ((512, 128), f32), ((512, 128), f32)]
     scratch = [
         ((512, 640), b), ((512, 640), b), ((512, 640), f32), ((2, 1024, 256), b), ((2, 1024, 256), b),
         ((2, 1024, 256), b), ((1024, 512), b), ((2, 768, 1024), b), ((512, 1280), f32), ((512, 640), b),
-        ((2048, 640), b), ((640, 4096), b), ((1024, 640), b),
+        ((2, 2, 512, 640), b), ((2, 2, 160, 4096), b), ((2, 2, 256, 640), b),
         ((640, 1536), b), ((1024, 640), b), ((640, 4096), b), ((2048, 640), b),
         ((256, 1024), b), ((512, 1024), b), ((1024, 512), b), ((512, 640), f32), ((512, 640), f32),
         ((512, 640), b), ((640, 512), b), ((512, 2048), b), ((512, 2048), b), ((512, 2048), b),
         ((512, 256), f32), ((512, 256), f32), ((512, 640), f32), ((512, 640), b), ((512, 640), b),
         ((512, 640), b), ((3, 8, 640), f32), ((2, 4, 8, 256), f32),
-        ((8, 640), f32), ((8, 640), f32), ((2, 8, 640), f32),
+        ((8, 640), f32), ((8, 640), f32), ((2, 8, 640), f32), ((512, 8), f32),
     ]
+    scratch += [((2, part[2], part[4]), b) for part in PARTS]
     sems = (SENDS, SENDS, 7, len(outs), 2, 2)
     far, vmem = pl.BlockSpec(memory_space=pl.ANY), pl.BlockSpec(memory_space=pltpu.VMEM)
     return pl.pallas_call(
         forward_kernel,
         out_shape=[jax.ShapeDtypeStruct(*o) for o in outs + near],
-        in_specs=[far] * 2 + [vmem] * 3 + [far] * 7 + [vmem] * 6,
+        in_specs=[far] * 2 + [vmem] * 3 + [far] * 7,
         out_specs=[far] * len(outs) + [vmem] * len(near),
         scratch_shapes=[pltpu.VMEM(*o) for o in scratch] + [pltpu.SemaphoreType.DMA((n,)) for n in sems],
         compiler_params=pltpu.CompilerParams(
             collective_id=2, has_side_effects=True, vmem_limit_bytes=60 << 20
         ),
         name="forward",
-    )(x, cot, cosine, sine, doc, *shards, *gain_shards)
+    )(x, cot, doc, frequency, gain_shards, *shards)
 
 
 def backward_kernel(*refs):
@@ -727,16 +896,20 @@
     ) = rest
     in_sem, pair_sem, send_sem, recv_sem, local_sem = rest[-5:]
     s, f = place()
-    greet(s, f)
-    reduce = Reduce(s, f, (*grads, grad_qkv), totals, list(rest[:-5]), send_sem, recv_sem, local_sem)
+    boxes = list(rest[:-5])
+    reduce = Reduce(s, f, grads, totals, boxes[15:], send_sem, recv_sem, local_sem)
+    lates = [Late(reduce, n, grad_qkv, totals[3], boxes[5 * n : 5 * n + 5]) for n in range(len(LATE))]
+    for p in EARLY:
+        reduce.load(p)
+    greet(s, f, tuple(AXES.values()))
+    for p in EARLY:
+        reduce.resume(p)
     loads = []
     for i, (src, dst) in enumerate(
         zip(fars, (d_att, pair, soft, d_att_scaled, queries, raw, normed, w_qkv, x, d_hidden))
     ):
         loads.append(pltpu.make_async_copy(src, dst, in_sem.at[i]))
         loads[-1].start()
-    for p in EARLY:
-        reduce.begin(p)
 
     def all_of(parts):
         for p in parts:
@@ -785,7 +958,6 @@
         device_id_type=MESH,
     )
     pass_back.start()
-    all_of(EARLY)
     to_pair(0, 512, 256)
     to_pair(1, 512, 512)
     for load in loads[5:]:
@@ -799,21 +971,22 @@
             d_queries[...] = mixed.T
 
             def rows_of(n):
-                rows = pl.ds(pl.multiple_of(256 * i + n * 128, 128), 128)
+                rows = pl.ds(256 * i + n * 128, 128)
                 dz = turn_back(d_queries[block(n, 128), :], cosine[rows, :], sine[rows, :])
                 y = raw[rows, cols]
                 r = scale_of(y)
                 d_raw[rows, cols] = norm_back(dz, y, r, gains[pl.ds(4, 1), 0:256]).astype(jnp.bfloat16)
                 head_sums[0] += fold(dz * y * r)
 
-            each(2, rows_of)
+            unrolled(2, rows_of)
 
         each(4, query_back)
+    all_of(EARLY)
     pass_back.wait_recv()
 
     def key_back(i):
         rows = block(i, 128)
-        own = pl.ds(pl.multiple_of(512 + i * 128, 128), 128)
+        own = pl.ds(512 + i * 128, 128)
         dz = d_pair[own, 0:256] + other[rows, 0:256].astype(jnp.float32)
         dz = turn_back(dz, cosine[rows, :], sine[rows, :])
         y = raw[rows, 1024:1280]
@@ -823,15 +996,15 @@
         d_value = d_pair[own, 256:512] + other[rows, 256:512].astype(jnp.float32)
         d_raw[rows, 1280:1536] = d_value.astype(jnp.bfloat16)
 
-    each(4, key_back)
+    unrolled(4, key_back)
 
     def weigh_in(j):
         cols = block(j, 256)
         grad_qkv[:, cols] = dot(normed_t[...], d_raw[:, cols]).astype(jnp.bfloat16)
 
     each(6, weigh_in)
-    for p in LATE:
-        reduce.begin(p)
+    for late in lates:
+        late.begin()
     all_of(EARLY)
     d_normed[...] = dot_nt(d_raw[...], w_qkv[...])
     lanes_in = gains[pl.ds(0, 1), :]
@@ -843,23 +1016,30 @@
         input_grad[rows, :] = d_hidden[rows, :] + norm_back(dz, y, r, lanes_in)
         sums[...] += fold(dz * y * r)
 
-    each(8, norm_in_back)
+    unrolled(8, norm_in_back)
     gain_sum[0] = gain_grads[...]
     gain_sum[0, pl.ds(0, 1), :] = jnp.sum(sums[...], 0, keepdims=True)
     gain_sum[0, pl.ds(4, 1), 0:256] = jnp.sum(head_sums[0], 0, keepdims=True)
     gain_sum[0, pl.ds(4, 1), 256:512] = jnp.sum(head_sums[1], 0, keepdims=True)
-    gain_dims = ("C", "X1", "X0", "Y1", "Y0", "Z1", "Z0")
-    flight = reduce.send(gain_sum.at[0], gain_in.at[0], gain_dims[0])
-    for stage in range(Reduce.STAGES):
-        all_of(LATE)
-        if stage < 7:
-            flight.wait_recv()
-            gain_sum[stage + 1] = gain_sum[stage] + gain_in[stage]
-            if stage < 6:
-                flight = reduce.send(gain_sum.at[stage + 1], gain_in.at[stage + 1], gain_dims[stage + 1])
-        if stage < Reduce.STAGES - 2:
-            all_of(EARLY)
-    gain_total[...] = gain_sum[7]
+    flights = [reduce.send(gain_sum.at[0], gain_in.at[0], "C")]
+    for stage in range(7):
+        if stage < Late.STAGES:
+            for late in lates:
+                late.advance()
+        if stage < 4:
+            total = gain_sum[stage]
+            for k, flight in enumerate(flights):
+                flight.wait_recv()
+                total = total + gain_in[max(3 * stage - 2, 0) + k]
+            gain_sum[stage + 1] = total
+        if stage < 3:
+            high, low = AXES["XYZ"[stage]]
+            flights = [
+                reduce.send(gain_sum.at[stage + 1], gain_in.at[3 * stage + 1 + k], dims)
+                for k, dims in enumerate(((high,), (low,), (high, low)))
+            ]
+        all_of(EARLY)
+    gain_total[...] = gain_sum[4]
     pass_back.wait_send()
     for copy in reduce.pending:
         copy.wait_send()
@@ -875,7 +1055,7 @@
     scratch = [
         ((256, 1024), b), ((768, 256), f32), ((2, 768, 1024), b), ((256, 256), f32), ((1024, 512), f32),
         ((512, 512), b), ((512, 512), b), ((512, 1536), b), ((640, 512), b), ((512, 640), f32),
-        ((640, 1536), b), ((8, 640), f32), ((2, 8, 256), f32), ((7, 8, 640), f32), ((8, 8, 640), f32),
+        ((640, 1536), b), ((8, 640), f32), ((2, 8, 256), f32), ((10, 8, 640), f32), ((5, 8, 640), f32),
     ]
     parts, sends = reduce_scratch()
     sems = (len(held), 2, sends, sends, len(PARTS))
@@ -886,6 +1066,7 @@
         in_specs=[far] * 10 + [vmem] * 5 + [far] * 3,
         out_specs=[vmem] * len(outs),
         scratch_shapes=[pltpu.VMEM(*o) for o in held + scratch]
+        + late_scratch()
         + parts
         + [pltpu.SemaphoreType.DMA((n,)) for n in sems],
         compiler_params=pltpu.CompilerParams(
@@ -895,10 +1076,37 @@
     )(*fars, *near, *grads)
 
 
-def rope_tables(positions):
-    frequency = rope_base ** (-(jnp.arange(128, dtype=jnp.float32) * (2.0 / 256)))
-    angles = positions[:, None] * frequency[None, :]
-    return jnp.cos(angles), jnp.sin(angles)
+FREQUENCY = (rope_base ** (-np.arange(128) / 128.0)).astype(np.float32)[None, :]
+
+
+def finish_kernel(layer_out, input_grad, down, gate_up, output, qkv, *outs):
+    outs[0][...] = layer_out[...]
+    outs[1][...] = input_grad[...]
+    cuts = ((qkv, 0), (qkv, 1024), (qkv, 1280), (output, 0), (gate_up, 0), (gate_up, 2048), (down, 0))
+    for out, (src, at) in zip(outs[2:], cuts):
+        rows, cols = out.shape
+
+        def widen(i, out=out, src=src, at=at, cols=cols):
+            part = block(i, 32)
+            out[part, :] = src[part, at : at + cols].astype(jnp.float32)
+
+        each(rows // 32, widen)
+
+
+def finish(layer_out, input_grad, down, gate_up, output, qkv):
+    shapes = ((160, 1024), (160, 256), (160, 256), (256, 640), (160, 2048), (160, 2048), (512, 640))
+    return pl.pallas_call(
+        finish_kernel,
+        out_shape=[
+            jax.ShapeDtypeStruct((512, 640), jnp.bfloat16),
+            jax.ShapeDtypeStruct((512, 640), jnp.float32),
+        ]
+        + [jax.ShapeDtypeStruct(shape, jnp.float32) for shape in shapes],
+        in_specs=[pl.BlockSpec(memory_space=pltpu.VMEM)] * 6,
+        out_specs=[pl.BlockSpec(memory_space=pltpu.VMEM)] * 9,
+        compiler_params=pltpu.CompilerParams(vmem_limit_bytes=40 << 20),
+        name="finish",
+    )(layer_out, input_grad, down, gate_up, output, qkv)
 
 
 def body(
@@ -919,39 +1127,29 @@
     norm_key,
     cotangent,
 ):
-    row_index = lax.axis_index("seq") * 512 + jnp.arange(512, dtype=jnp.int32)
-    cosine, sine = rope_tables((row_index - doc_start[0]).astype(jnp.float32))
+    packed = sum(
+        jnp.pad(g.astype(jnp.float32)[None, :], ((i, 7 - i), (0, 256 - g.shape[0])))
+        for i, g in enumerate((norm_attn_in, norm_attn_out, norm_ffn_in, norm_ffn_out, norm_query, norm_key))
+    )
     (
-        layer_out, d_hidden, d_att, queries, pair, soft, raw, normed,
-        grad_down, grad_gate_up, d_att_scaled, w_qkv, grad_output, gains, gain_grads, weight,
+        layer_out, d_hidden, d_att, queries, pair, soft, raw, normed, grad_down, grad_gate_up,
+        d_att_scaled, w_qkv, grad_output, gains, gain_grads, weight, cosine, sine,
     ) = forward(
-        inputs[0], cotangent[0], cosine, sine, doc_start,
+        inputs[0], cotangent[0], doc_start, jnp.asarray(FREQUENCY), packed,
         (w_query, w_key, w_value, w_output, w_gate, w_up, w_down),
-        [
-            g.reshape(1, -1)
-            for g in (norm_attn_in, norm_attn_out, norm_ffn_in, norm_ffn_out, norm_query, norm_key)
-        ],
     )
     input_grad, down, gate_up_share, output, qkv, gain_grads = backward(
         (d_att, pair, soft, d_att_scaled, queries, raw, normed, w_qkv, inputs[0], d_hidden),
         (cosine, sine, gains, gain_grads, weight),
-        [
-            grad.reshape(2, 2, grad.shape[0] // 4, grad.shape[1])
-            for grad in (grad_down, grad_gate_up, grad_output)
-        ],
+        (grad_down, grad_gate_up, grad_output),
     )
+    layer_out, input_grad, *shares = finish(layer_out, input_grad, down, gate_up_share, output, qkv)
     at = lax.axis_index("fsdp")
     wide = lax.dynamic_slice(gain_grads, (0, at * 160), (4, 160))
     return (
         layer_out[None],
         input_grad[None],
-        qkv[:, :1024].astype(jnp.float32),
-        qkv[:, 1024:1280].astype(jnp.float32),
-        qkv[:, 1280:].astype(jnp.float32),
-        output.astype(jnp.float32),
-        gate_up_share[:, :2048].astype(jnp.float32),
-        gate_up_share[:, 2048:].astype(jnp.float32),
-        down.astype(jnp.float32),
+        *shares,
         wide[0],
         wide[1],
         wide[2],

time: 193 us -> 179 us (0.927)
  other arithmetic: 10.9 us -> 1.28 us
  Pallas kernels: 171 us -> 166 us
    convert_element_type x6 -> x0, other arithmetic: 9.13 us -> none  [the longest x1 1.98 us: body(): qkv[:, :1024].astype(jnp.float32)]
    pallas_call x1, Pallas kernels: 87.4 us -> 80.9 us  [backward(): pl.pallas_call(backward_kernel, out_shape=[jax.ShapeDtypeStruct(*o) for o...]
    reshape x4 -> x0, local copies, waits for them, and re-layouts: 4.88 us -> none  [body(): g.reshape(1, -1)]
    unnamed x10 -> x12, local copies, waits for them, and re-layouts: 1.91 us -> 5.72 us
    pallas_call x0 -> x1, Pallas kernels: none -> 3.77 us  [finish(): pl.pallas_call(finish_kernel, out_shape=[jax.ShapeDtypeStruct((512, 640),...]
    pallas_call x1, Pallas kernels: 84 us -> 81 us  [forward(): pl.pallas_call(forward_kernel, out_shape=[jax.ShapeDtypeStruct(*o) for o...]
    broadcast_in_dim x0 -> x4, local copies, waits for them, and re-layouts: none -> 2.63 us  [body(): g.astype(jnp.float32)[None, :]]
where the time goes in v4:
time: 179 us
  Pallas kernels  166 us (93%)
  local copies, waits for them, and re-layouts  11.2 us (6%)
    pallas_call x1, Pallas kernels, forward(): pl.pallas_call(forward_kernel, out_shape=[jax.ShapeDtypeStruct(*o) for o...  81 us
    pallas_call x1, Pallas kernels, backward(): pl.pallas_call(backward_kernel, out_shape=[jax.ShapeDtypeStruct(*o) for o...  80.9 us
    unnamed x12, local copies, waits for them, and re-layouts  5.72 us
    pallas_call x1, Pallas kernels, finish(): pl.pallas_call(finish_kernel, out_shape=[jax.ShapeDtypeStruct((512, 640),...  3.77 us

profile of v4, /device:TPU:0, one launch (start us, length us, event | category | flops | bytes accessed | tf_op | source)
XLA Modules:
  0.0 178.8 jit_solution(6490968641647212214)
XLA Ops:
  0.6 0.7 broadcast_in_dim.33
  1.3 0.7 broadcast_in_dim.32
  2.0 0.7 broadcast_in_dim.31
  2.6 0.7 broadcast_in_dim.30
  3.3 1.3 convert_add_fusion.refs_4_
  4.6 81.0 %forward.1 = (bf16[512,640]{1,0:T(8,128)(2,1)}, f32[512,640]{1,0:T(8,128)}, bf16[2,1024,256]{2,1,0:T(8,128)(2,1)}, bf16[2,1024,256]{2,1,0:T(8,128)(2,1)}, bf16[1...) custom-call(bf16[512,640]{1,0:T(8,128)(2,1)} %bitcast.14, ...), custom_call_target="tpu_custom_call" | custom-call | tf_op jit(solution)/shard_map/forward/pallas_call | solution.py:872
  85.5 0.0 copy-start.2
  85.5 80.9 %backward.1 = (f32[512,640]{1,0:T(8,128)}, bf16[512,640]{1,0:T(8,128)(2,1)}, bf16[160,4096]{1,0:T(8,128)(2,1)}, bf16[256,640]{1,0:T(8,128)(2,1)}, bf16[160,1536]{1,0:T(8,128)(2,1)}, /*index=5*/f32[8,640]{1,0:T(8,128)}) custom-call(bf16[2,1024,256]{2,1,0:T(8,128)(2,1)} %get-tuple-element.49.refs_0_, bf16[1024,512]{1,0:T(8,128)(2,1)} %get-tuple-element.50.refs_1_, ...), custom_call_target="tpu_custom_call" | custom-call | tf_op jit(solution)/shard_map/backward/pallas_call | solution.py:1063
  166.4 0.0 copy-done.2
  166.5 0.0 copy-start
  166.5 1.3 copy-done
  167.8 0.0 copy-start.1
  167.8 1.3 copy-done.1
  169.1 0.0 copy-start.3
  169.1 1.1 copy-done.3
  170.2 0.0 copy-start.4
  170.2 1.0 copy-done.4
  171.2 0.0 copy-start.5
  171.2 1.0 copy-done.5
  172.2 3.8 %finish.1 = (bf16[512,640]{1,0:T(8,128)(2,1)}, f32[512,640]{1,0:T(8,128)}, f32[160,1024]{1,0:T(8,128)}, f32[160,256]{1,0:T(8,128)}, f32[160,256]{1,0:T(8,128)}, ...) custom-call(bf16[512,640]{1,0:T(8,128)(2,1)S(1)} %copy-done.2, ...), custom_call_target="tpu_custom_call" | custom-call | tf_op jit(solution)/shard_map/finish/pallas_call | solution.py:1098
  176.0 1.5 fusion.3
  177.5 0.7 fusion.2
  178.2 0.6 fusion
Async XLA Ops:
  85.5 80.9 %copy-start.2 = (bf16[512,640]{1,0:T(8,128)(2,1)S(1)}, bf16[512,640]{1,0:T(8,128)(2,1)}, u32[]{:S(2)}) copy-start(bf16[512,640]{1,0:T(8,128)(2,1)} %get-tuple-element.48.layer_out) | copy-start | bytes 1966084
  166.5 1.3 copy-start
  167.8 1.3 copy-start.1
  169.1 1.1 copy-start.3
  170.2 1.0 copy-start.4
  171.2 1.0 copy-start.5

commit v5 on v4

--- a/solution.py
+++ b/solution.py
@@ -156,8 +156,8 @@
 PARTS = (
     (0, 0, 256, 0, 640, ORDERS[3], "rrr"),
     (1, 0, 160, 0, 1536, ORDERS[0], "ccr"),
-    (1, 0, 160, 1536, 1536, ORDERS[1], "ccr"),
-    (1, 0, 160, 3072, 1024, ORDERS[2], "ccc"),
+    (1, 0, 160, 1536, 1536, ORDERS[2], "ccr"),
+    (1, 0, 160, 3072, 1024, ORDERS[1], "ccc"),
     (0, 256, 256, 0, 640, ORDERS[4], "rrr"),
     (2, 0, 256, 0, 640, ORDERS[5], "rrr"),
 )
@@ -710,9 +710,9 @@
     gather.arrive(5)
 
     def feed(j):
-        cols = block(j, 256)
+        cols = block(j, 512)
         gate[...] = dot(normed_two[...], w_gate_up[:, cols])
-        up[...] = dot(normed_two[...], w_gate_up[:, pl.ds(pl.multiple_of(2048 + j * 256, 256), 256)])
+        up[...] = dot(normed_two[...], w_gate_up[:, pl.ds(pl.multiple_of(2048 + j * 512, 512), 512)])
 
         def bend(i):
             rows = block(i, 64)
@@ -728,7 +728,7 @@
 
         unrolled(8, bend)
 
-    each(8, feed)
+    each(4, feed)
     gather.arrive(6)
     down[...] = dot(product[...], w_down[...])
     sums[...] = jnp.zeros_like(sums)
@@ -746,7 +746,7 @@
     write(layer_out, 0)
 
     def feed_back(j):
-        cols = block(j, 256)
+        cols = block(j, 512)
         gate[...] = dot_nt(d_down[...], w_down[cols, :])
 
         def bend(i):
@@ -759,15 +759,14 @@
         for grad, at in ((slope, 0), (level, 2048)):
             block_ = dot(normed_two_t[...], grad[:, cols]).astype(jnp.bfloat16)
             for q in range(4):
-                grad_gate_up[q // 2, q % 2, :, pl.ds(pl.multiple_of(at + j * 256, 256), 256)] = block_[
+                grad_gate_up[q // 2, q % 2, :, pl.ds(pl.multiple_of(at + j * 512, 512), 512)] = block_[
                     160 * q : 160 * (q + 1), :
                 ]
 
-    def down_back(j):
-        q = lax.div(j, 2)
-        grad_down[lax.div(q, 2), lax.rem(q, 2), block(lax.rem(j, 2), 256), :] = dot(
-            product[:, block(j, 256)].T, d_down[...]
-        ).astype(jnp.bfloat16)
+    def down_back(q):
+        grad_down[lax.div(q, 2), lax.rem(q, 2)] = dot(product[:, block(q, 512)].T, d_down[...]).astype(
+            jnp.bfloat16
+        )
 
     core, exchanged = bit_of("C", s, f), {}
     tensors = (grad_down, grad_gate_up, grad_output)
@@ -789,10 +788,10 @@
 
             each(rows // step, add)
 
-    each(8, feed_back)
+    each(4, feed_back)
     for p in (1, 2, 3):
         exchange(p)
-    each(8, down_back)
+    each(4, down_back)
     for p in (0, 4):
         exchange(p)
     down[...] = dot_nt(slope[...], w_gate_up[:, 0:2048])
@@ -862,7 +861,7 @@
         ((640, 1536), b), ((1024, 640), b), ((640, 4096), b), ((2048, 640), b),
         ((256, 1024), b), ((512, 1024), b), ((1024, 512), b), ((512, 640), f32), ((512, 640), f32),
         ((512, 640), b), ((640, 512), b), ((512, 2048), b), ((512, 2048), b), ((512, 2048), b),
-        ((512, 256), f32), ((512, 256), f32), ((512, 640), f32), ((512, 640), b), ((512, 640), b),
+        ((512, 512), f32), ((512, 512), f32), ((512, 640), f32), ((512, 640), b), ((512, 640), b),
         ((512, 640), b), ((3, 8, 640), f32), ((2, 4, 8, 256), f32),
         ((8, 640), f32), ((8, 640), f32), ((2, 8, 640), f32), ((512, 8), f32),
     ]
@@ -999,13 +998,12 @@
     unrolled(4, key_back)
 
     def weigh_in(j):
-        cols = block(j, 256)
+        cols = block(j, 512)
         grad_qkv[:, cols] = dot(normed_t[...], d_raw[:, cols]).astype(jnp.bfloat16)
 
-    each(6, weigh_in)
+    each(3, weigh_in)
     for late in lates:
         late.begin()
-    all_of(EARLY)
     d_normed[...] = dot_nt(d_raw[...], w_qkv[...])
     lanes_in = gains[pl.ds(0, 1), :]
 
@@ -1022,7 +1020,7 @@
     gain_sum[0, pl.ds(4, 1), 0:256] = jnp.sum(head_sums[0], 0, keepdims=True)
     gain_sum[0, pl.ds(4, 1), 256:512] = jnp.sum(head_sums[1], 0, keepdims=True)
     flights = [reduce.send(gain_sum.at[0], gain_in.at[0], "C")]
-    for stage in range(7):
+    for stage in range(8):
         if stage < Late.STAGES:
             for late in lates:
                 late.advance()
@@ -1079,18 +1077,38 @@
 FREQUENCY = (rope_base ** (-np.arange(128) / 128.0)).astype(np.float32)[None, :]
 
 
-def finish_kernel(layer_out, input_grad, down, gate_up, output, qkv, *outs):
-    outs[0][...] = layer_out[...]
-    outs[1][...] = input_grad[...]
-    cuts = ((qkv, 0), (qkv, 1024), (qkv, 1280), (output, 0), (gate_up, 0), (gate_up, 2048), (down, 0))
-    for out, (src, at) in zip(outs[2:], cuts):
+def finish_kernel(*refs):
+    fars, outs, near, sem = refs[:6], refs[6:15], refs[15:21], refs[21]
+    loads = []
+    for i, (src, dst) in enumerate(zip(fars, near)):
+        loads.append(pltpu.make_async_copy(src, dst, sem.at[i]))
+        loads[-1].start()
+    layer_out, input_grad, down, gate_up, output, qkv = near
+    cuts = (
+        (2, down, 8, 0),
+        (3, gate_up, 6, 0),
+        (3, gate_up, 7, 2048),
+        (4, output, 5, 0),
+        (5, qkv, 2, 0),
+        (5, qkv, 3, 1024),
+        (5, qkv, 4, 1280),
+    )
+    waited = set()
+    for number, src, at, first in cuts:
+        if number not in waited:
+            loads[number].wait()
+            waited.add(number)
+        out = outs[at]
         rows, cols = out.shape
 
-        def widen(i, out=out, src=src, at=at, cols=cols):
+        def widen(i, out=out, src=src, first=first, cols=cols):
             part = block(i, 32)
-            out[part, :] = src[part, at : at + cols].astype(jnp.float32)
+            out[part, :] = src[part, first : first + cols].astype(jnp.float32)
 
         each(rows // 32, widen)
+    for number in range(2):
+        loads[number].wait()
+        outs[number][...] = near[number][...]
 
 
 def finish(layer_out, input_grad, down, gate_up, output, qkv):
@@ -1102,9 +1120,15 @@
             jax.ShapeDtypeStruct((512, 640), jnp.float32),
         ]
         + [jax.ShapeDtypeStruct(shape, jnp.float32) for shape in shapes],
-        in_specs=[pl.BlockSpec(memory_space=pltpu.VMEM)] * 6,
+        in_specs=[pl.BlockSpec(memory_space=pl.ANY)] * 6,
         out_specs=[pl.BlockSpec(memory_space=pltpu.VMEM)] * 9,
-        compiler_params=pltpu.CompilerParams(vmem_limit_bytes=40 << 20),
+        scratch_shapes=[
+            pltpu.VMEM((512, 640), jnp.bfloat16),
+            pltpu.VMEM((512, 640), jnp.float32),
+        ]
+        + [pltpu.VMEM(shape, jnp.bfloat16) for shape in SHARES]
+        + [pltpu.SemaphoreType.DMA((6,))],
+        compiler_params=pltpu.CompilerParams(vmem_limit_bytes=60 << 20),
         name="finish",
     )(layer_out, input_grad, down, gate_up, output, qkv)
 

time: 179 us -> 167 us (0.933)
  Pallas kernels: 166 us -> 159 us
  local copies, waits for them, and re-layouts: 11.2 us -> 5.45 us
    pallas_call x1, Pallas kernels: 81 us -> 74.3 us  [forward(): pl.pallas_call(forward_kernel, out_shape=[jax.ShapeDtypeStruct(*o) for o...]
    unnamed x12 -> x0, local copies, waits for them, and re-layouts: 5.72 us -> none
    pallas_call x1, Pallas kernels: 80.9 us -> 78.8 us  [backward(): pl.pallas_call(backward_kernel, out_shape=[jax.ShapeDtypeStruct(*o) for o...]
    pallas_call x1, Pallas kernels: 3.77 us -> 5.66 us  [finish(): pl.pallas_call(finish_kernel, out_shape=[jax.ShapeDtypeStruct((512, 640),...]
where the time goes in v5:
time: 167 us; the launch traced here: 166 us
  Pallas kernels  159 us (95%)
  local copies, waits for them, and re-layouts  5.45 us (3%)
    pallas_call x1, Pallas kernels, backward(): pl.pallas_call(backward_kernel, out_shape=[jax.ShapeDtypeStruct(*o) for o...  78.8 us
    pallas_call x1, Pallas kernels, forward(): pl.pallas_call(forward_kernel, out_shape=[jax.ShapeDtypeStruct(*o) for o...  74.3 us
    pallas_call x1, Pallas kernels, finish(): pl.pallas_call(finish_kernel, out_shape=[jax.ShapeDtypeStruct((512, 640),...  5.66 us

profile of v5, /device:TPU:0, one launch (start us, length us, event | category | flops | bytes accessed | tf_op | source)
XLA Modules:
  0.0 166.1 jit_solution(17327615496116521248)
XLA Ops:
  0.6 0.7 broadcast_in_dim.33
  1.3 0.7 broadcast_in_dim.32
  2.0 0.7 broadcast_in_dim.31
  2.6 0.7 broadcast_in_dim.30
  3.3 1.3 convert_add_fusion.refs_4_
  4.6 74.3 %forward.1 = (bf16[512,640]{1,0:T(8,128)(2,1)}, f32[512,640]{1,0:T(8,128)}, bf16[2,1024,256]{2,1,0:T(8,128)(2,1)}, bf16[2,1024,256]{2,1,0:T(8,128)(2,1)}, bf16[1...) custom-call(bf16[512,640]{1,0:T(8,128)(2,1)} %bitcast.14, ...), custom_call_target="tpu_custom_call" | custom-call | tf_op jit(solution)/shard_map/forward/pallas_call | solution.py:871
  78.8 78.8 %backward.1 = (f32[512,640]{1,0:T(8,128)}, bf16[512,640]{1,0:T(8,128)(2,1)}, bf16[160,4096]{1,0:T(8,128)(2,1)}, bf16[256,640]{1,0:T(8,128)(2,1)}, bf16[160,1536]{1,0:T(8,128)(2,1)}, /*index=5*/f32[8,640]{1,0:T(8,128)}) custom-call(bf16[2,1024,256]{2,1,0:T(8,128)(2,1)} %get-tuple-element.49.refs_0_, bf16[1024,512]{1,0:T(8,128)(2,1)} %get-tuple-element.50.refs_1_, ...), custom_call_target="tpu_custom_call" | custom-call | tf_op jit(solution)/shard_map/backward/pallas_call | solution.py:1061
  157.7 5.7 %finish.1 = (bf16[512,640]{1,0:T(8,128)(2,1)}, f32[512,640]{1,0:T(8,128)}, f32[160,1024]{1,0:T(8,128)}, f32[160,256]{1,0:T(8,128)}, f32[160,256]{1,0:T(8,128)}, ...) custom-call(bf16[512,640]{1,0:T(8,128)(2,1)} %get-tuple-element.48.refs_0_, ...), custom_call_target="tpu_custom_call" | custom-call | tf_op jit(solution)/shard_map/finish/pallas_call | solution.py:1116
  163.3 1.5 fusion.3
  164.8 0.7 fusion.2
  165.6 0.6 fusion

commit v6 on v5

--- a/solution.py
+++ b/solution.py
@@ -646,7 +646,7 @@
 
         unrolled(4, rows_of)
 
-    each(4, shape_query)
+    unrolled(4, shape_query)
     write(raw, 6)
     write(queries, 3)
     gather.fan(3)
@@ -674,7 +674,7 @@
         def own_keys(h, i=i, first=first, count=count):
             weight_sums[i, h] = weigh(i, h, first, count)
 
-        each(4, own_keys)
+        unrolled(4, own_keys)
         gather.fan(5 + i)
     gather.relay(3)
     pass_on.wait_recv()
@@ -690,7 +690,7 @@
             att_t[block(h, 256), 256 * i : 256 * (i + 1)] = mixed.astype(jnp.bfloat16)
             att[256 * i : 256 * (i + 1), block(h, 256)] = mixed.T.astype(jnp.bfloat16)
 
-        each(4, attend)
+        unrolled(4, attend)
         gather.relay(4 + i)
     write(soft, 5)
     gather.arrive(3)
@@ -938,7 +938,7 @@
                 p = soft[i, rows, cols].astype(jnp.float32)
                 d_scores[i, rows, cols] = (p * ((d_soft[rows, :] - inner) * inverse)).astype(jnp.bfloat16)
 
-        each(4, one_head)
+        unrolled(4, one_head)
 
     def to_pair(i, low, count):
         at, here = pl.ds(low, count), pl.ds(low - 256 * i, count)
@@ -979,7 +979,7 @@
 
             unrolled(2, rows_of)
 
-        each(4, query_back)
+        unrolled(4, query_back)
     all_of(EARLY)
     pass_back.wait_recv()
 

time: 167 us -> 165 us (0.988)
  no operation moved by 1% of the time
where the time goes in v6:
time: 165 us
  Pallas kernels  158 us (96%)
  local copies, waits for them, and re-layouts  5.45 us (3%)
    pallas_call x1, Pallas kernels, backward(): pl.pallas_call(backward_kernel, out_shape=[jax.ShapeDtypeStruct(*o) for o...  77.8 us
    pallas_call x1, Pallas kernels, forward(): pl.pallas_call(forward_kernel, out_shape=[jax.ShapeDtypeStruct(*o) for o...  74.1 us
    pallas_call x1, Pallas kernels, finish(): pl.pallas_call(finish_kernel, out_shape=[jax.ShapeDtypeStruct((512, 640),...  5.66 us

profile of v6, /device:TPU:0, one launch (start us, length us, event | category | flops | bytes accessed | tf_op | source)
XLA Modules:
  0.0 164.9 jit_solution(7235600014898902529)
XLA Ops:
  0.6 0.7 broadcast_in_dim.33
  1.3 0.7 broadcast_in_dim.32
  2.0 0.7 broadcast_in_dim.31
  2.6 0.7 broadcast_in_dim.30
  3.3 1.3 convert_add_fusion.refs_4_
  4.6 74.1 %forward.1 = (bf16[512,640]{1,0:T(8,128)(2,1)}, f32[512,640]{1,0:T(8,128)}, bf16[2,1024,256]{2,1,0:T(8,128)(2,1)}, bf16[2,1024,256]{2,1,0:T(8,128)(2,1)}, bf16[1...) custom-call(bf16[512,640]{1,0:T(8,128)(2,1)} %bitcast.14, ...), custom_call_target="tpu_custom_call" | custom-call | tf_op jit(solution)/shard_map/forward/pallas_call | solution.py:871
  78.7 77.8 %backward.1 = (f32[512,640]{1,0:T(8,128)}, bf16[512,640]{1,0:T(8,128)(2,1)}, bf16[160,4096]{1,0:T(8,128)(2,1)}, bf16[256,640]{1,0:T(8,128)(2,1)}, bf16[160,1536]{1,0:T(8,128)(2,1)}, /*index=5*/f32[8,640]{1,0:T(8,128)}) custom-call(bf16[2,1024,256]{2,1,0:T(8,128)(2,1)} %get-tuple-element.49.refs_0_, bf16[1024,512]{1,0:T(8,128)(2,1)} %get-tuple-element.50.refs_1_, ...), custom_call_target="tpu_custom_call" | custom-call | tf_op jit(solution)/shard_map/backward/pallas_call | solution.py:1061
  156.5 5.7 %finish.1 = (bf16[512,640]{1,0:T(8,128)(2,1)}, f32[512,640]{1,0:T(8,128)}, f32[160,1024]{1,0:T(8,128)}, f32[160,256]{1,0:T(8,128)}, f32[160,256]{1,0:T(8,128)}, ...) custom-call(bf16[512,640]{1,0:T(8,128)(2,1)} %get-tuple-element.48.refs_0_, ...), custom_call_target="tpu_custom_call" | custom-call | tf_op jit(solution)/shard_map/finish/pallas_call | solution.py:1116
  162.1 1.5 fusion.3
  163.6 0.7 fusion.2
  164.4 0.6 fusion
